TPU v7x, 32 devices: a whole 2x2x4 slice. The times are simulated.
32 devices in a mesh: sec: 8 (over y, x, core), mode: 4 (over z).
Axes of the slice: x: 2, y: 2, z: 4, core: 2. Of those that a mesh axis runs over, the one named last changes fastest.
Arguments:
- coupling: float32 [8, 512, 512], P('sec'), may hold values from -1.25 to 0.25
- stiffness: float32 [8, 512, 512], P('sec'), may hold values from -0.5 to 3.5, as said below
- loads: float32 [8, 16, 512], P('sec'), may hold values from -60 to 60
- modes: bfloat16 [8, 512, 1024], P('sec', None, 'mode'), may hold values from -0.09375 to 0.09375
- joint_section: int32 [8192], P('sec'), may hold values from 0 to 7
- regime: int32 [128], P('sec'), may hold values from 0 to 3
- participation: bfloat16 [8192, 1024], P('sec', 'mode'), may hold values from -0.0625 to 0.0625
Outputs:
- displacement: float32 [8, 16, 512], P('sec', None, 'mode')
- motion: float32 [8, 16, 512], P('sec', None, 'mode')
Inputs may be any that keep to these rules, and one draw needn't show every extreme that they name: Each section's block is symmetric, and the whole block-tridiagonal operator built from stiffness and coupling is symmetric positive definite.
All inputs are finite; a program needn't handle non-finite values.
Results may differ from a plain program's by a relative error of at most 0.00047.
Values sent between devices are 32-bit elements; how exact they have to be, the bound alone decides.
No kernel may reach another device: no remote copies, remote signals or barrier semaphores. Data moves between devices by JAX's collectives and lax.ppermute only.
A program may use at most 64 MiB of HBM per device.

v0:
```python
import functools

import jax
import jax.numpy as jnp
from jax import lax
from jax.experimental import pallas as pl
from jax.experimental.pallas import tpu as pltpu
from jax.sharding import PartitionSpec as P

LEVELS = 3
BUCKET = 64
RATES = (0.2, 0.5, 1.0, 2.0)
AXES = ("sec", "mode")
TILE = 128
f32, bf16 = jnp.float32, jnp.bfloat16


def split(value):
    high = value.astype(bf16)
    return high, (value - high.astype(f32)).astype(bf16)


def dot(left, right):
    return jnp.dot(left, right, preferred_element_type=f32)


def dot_t(left, right):
    return lax.dot_general(left, right, (((1,), (1,)), ((), ())), preferred_element_type=f32)


def times(left, right, product=dot):
    return product(left[0], right[0]) + product(left[0], right[1]) + product(left[1], right[0])


def upper(size):
    count = size // TILE
    return [(a, b) for a in range(count) for b in range(a, count)]


def band(index):
    return slice(TILE * index, TILE * index + TILE)


def unpack(packed, block, thin):
    size = block.shape[0]
    cells = upper(size)
    for index, (a, b) in enumerate(cells):
        cell = packed[band(index), :]
        block[band(a), band(b)] = cell
        if a != b:
            block[band(b), band(a)] = cell.T
    rows = thin.shape[0]
    for c in range(size // TILE):
        start = TILE * len(cells) + rows * c
        thin[:, band(c)] = packed[start : start + rows, :]


def pack(packed, block, thin):
    size = block.shape[1]
    cells = upper(size)
    for index, (a, b) in enumerate(cells):
        packed[band(index), :] = block[band(a), band(b)]
    rows = thin.shape[0]
    for c in range(size // TILE):
        start = TILE * len(cells) + rows * c
        packed[start : start + rows, :] = thin[:, band(c)]


def scaled(block):
    size = block.shape[0]
    eye = lax.broadcasted_iota(jnp.int32, (size, size), 0) == lax.broadcasted_iota(
        jnp.int32, (size, size), 1
    )
    only = jnp.where(eye, block, 0.0)
    down = jnp.sum(only, axis=1, keepdims=True)
    along = jnp.sum(only, axis=0, keepdims=True)
    down = jnp.where(down == 0.0, 0.0, 1.0 / down)
    along = jnp.where(along == 0.0, 0.0, 1.0 / along)
    unit = jnp.where(eye, 1.0, 0.0)
    return unit, down, along, unit - down * block


def inverse_of(block):
    unit, down, along, first = scaled(block)
    one = split(first)
    second = times(one, one)
    two = split(second)
    third = times(one, two)
    fourth = dot(two[0], two[0]).astype(bf16)
    series = unit + first + second + third
    series = series + dot(series.astype(bf16), fourth)
    return series * along


def schur(rows_and_thin, inverse, right, product):
    through = times(split(rows_and_thin), split(inverse))
    return through, times(split(through), split(right), product)


def pack_kernel(block, thin, packed):
    pack(packed, block, thin)


def own_kernel(block, thin, lower, packed, stack, out):
    size = block.shape[0]
    inverse = inverse_of(block[...])
    stack[0:size, :] = lower[...].T
    stack[size:, :] = thin[...]
    _, out[...] = schur(stack[...], inverse, lower[...], dot)
    pack(packed, out, out.at[size:, :])


def above_kernel(inverse, thin, lower, packed, stack, out):
    size = inverse.shape[0]
    stack[0:size, :] = lower[...].T
    stack[size:, :] = thin[...]
    _, out[...] = schur(stack[...], inverse[...], lower[...], dot)
    pack(packed, out, out.at[size:, :])


def receive_kernel(packed, lower, block, thin, above, through, out, stack, whole):
    size = block.shape[0]
    unpack(packed, whole, stack.at[size:, :])
    inverse = inverse_of(whole[...])
    stack[0:size, :] = lower[...]
    half, full = schur(stack[...], inverse, lower[...], dot_t)
    through[...] = half[0:size, :]
    stack[...] = full
    cells = upper(size)
    for index, (a, b) in enumerate(cells):
        out[band(index), :] = block[band(a), band(b)] - stack[band(a), band(b)] - above[band(index), :]
    rows = thin.shape[0]
    for c in range(size // TILE):
        start = TILE * len(cells) + rows * c
        out[start : start + rows, :] = (
            thin[:, band(c)] - stack[size:, band(c)] - above[start : start + rows, :]
        )


def invert_kernel(packed, inverse, block, thin):
    unpack(packed, block, thin)
    inverse[...] = inverse_of(block[...])


def lower_kernel(through, passed, lower):
    lower[...] = -times(split(through[...]), split(passed[...]))


def last_lower_kernel(through, passed, inverse, thin, lower, packed, stack, out):
    size = inverse.shape[0]
    value = -times(split(through[...]), split(passed[...]))
    lower[...] = value
    stack[0:size, :] = value.T
    stack[size:, :] = thin[...]
    _, out[...] = schur(stack[...], inverse[...], value, dot)
    pack(packed, out, out.at[size:, :])


def last_receive_kernel(inverse, thin_passed, lower, block, thin, block_out, thin_out, stack):
    size = block.shape[0]
    stack[0:size, :] = lower[...]
    stack[size:, :] = thin_passed[...]
    _, full = schur(stack[...], inverse[...], lower[...], dot_t)
    block_out[...] = block[...] - full[0:size, :]
    thin_out[...] = thin[...] - full[size:, :]


def solve_kernel(block, thin, above, solution, whole, own):
    unpack(above, whole, own)
    value = block[...] - whole[...]
    _, down, along, first = scaled(value)
    one = split(first)
    now = (thin[...] - own[...]) * along
    for power in (1, 2, 4):
        moved = now
        for _ in range(power):
            moved = times(split(moved), one, dot_t)
        now = now + moved
    solution[...] = now


def modal_kernel(a, b, c, d, modes, shares, whole, payload):
    value = a[...] + b[...] + c[...] + d[...]
    whole[...] = value
    amplitude = jnp.sqrt(jnp.sum(value * value, keepdims=True) / value.size + 1e-06)
    rows = value.shape[0]
    payload[...] = jnp.zeros_like(payload)
    payload[0:rows, :] = dot(value.astype(bf16), modes[...])
    payload[rows : rows + 1, :] = shares[...] * (amplitude / (1.0 + amplitude))


def back_kernel(place, mine, other, modes, *outs):
    total = mine[...] + other[...]
    scratch = outs[-1]
    pieces = outs[:-1]
    rows = scratch.shape[0]
    damping = total[rows : rows + 1, :]
    removed = (total[0:rows, :] * (damping / (1.0 + damping))).astype(bf16)
    scratch[...] = dot_t(removed, modes[...])
    width = pieces[0].shape[1]
    for k, piece in enumerate(pieces):
        start = lax.rem(place[0] + k, len(pieces)) * width
        piece[...] = scratch[:, pl.ds(pl.multiple_of(start, width), width)]


def call(kernel, outs, scratch, args, flops, smem=0):
    vmem, scalar = pl.BlockSpec(memory_space=pltpu.VMEM), pl.BlockSpec(memory_space=pltpu.SMEM)
    moved = sum(a.size * a.dtype.itemsize for a in args) + sum(4 * o[0] * o[1] for o in outs)
    single = len(outs) == 1
    shapes = [jax.ShapeDtypeStruct(o, f32) for o in outs]
    return pl.pallas_call(
        kernel,
        out_shape=shapes[0] if single else tuple(shapes),
        in_specs=[scalar] * smem + [vmem] * (len(args) - smem),
        out_specs=vmem if single else tuple([vmem] * len(outs)),
        scratch_shapes=[pltpu.VMEM(s, f32) for s in scratch],
        compiler_params=pltpu.CompilerParams(vmem_limit_bytes=40 << 20),
        cost_estimate=pl.CostEstimate(flops=flops, transcendentals=0, bytes_accessed=moved),
    )(*args)


def per_device(coupling, stiffness, loads, modes, joint_section, regime, participation):
    position, plane = lax.axis_index("sec"), lax.axis_index("mode")
    sections, groups = lax.axis_size("sec"), lax.axis_size("mode")
    size, columns = stiffness.shape[1], loads.shape[1]
    width = size // groups
    cells = len(upper(size))
    packed = (TILE * cells + columns * (size // TILE), TILE)
    square, stacked, thin_shape = (size, size), (size + columns, size), (columns, size)
    product = 6 * size**3

    def moved(value, step, level):
        stride = min(2 ** (level + 1), groups)
        pairs = []
        for target in range(sections):
            source = target - step
            if 0 <= source < sections:
                pairs += [
                    (source * groups + m, target * groups + m)
                    for m in range(groups)
                    if (target - m) % stride == 0
                ]
        return lax.ppermute(value, AXES, pairs)

    def exchanged(value, to, wanted=lambda s, m: True):
        pairs = []
        for s in range(sections):
            for m in range(groups):
                if wanted(s, m):
                    s_to, m_to = to(s, m)
                    pairs.append((s * groups + m, s_to * groups + m_to))
        return lax.ppermute(value, AXES, pairs)

    lower = coupling[0] * (position >= 1).astype(f32)
    block, thin = stiffness[0], loads[0]

    matches = (jnp.arange(sections, dtype=jnp.int32)[:, None] == joint_section[None, :]).astype(f32)
    joint_regime = jnp.broadcast_to(regime[:, None], (regime.shape[0], BUCKET)).reshape(-1)
    joint_rate = jnp.zeros(joint_regime.shape, f32)
    for value_index, rate_value in enumerate(RATES):
        joint_rate = joint_rate + (joint_regime == value_index).astype(f32) * rate_value
    weights = participation.astype(f32)
    shares = jnp.dot(
        matches * joint_rate[None, :], weights * weights, precision=lax.Precision.HIGHEST
    )

    sent = call(pack_kernel, [packed], [], (block, thin), 0)
    block_down = moved(sent, 1, 0)
    lower_down = moved(lower, 1, 0)
    up = call(own_kernel, [packed], [stacked, stacked], (block, thin, lower), 6 * product)
    up = moved(up, -1, 0)
    through, sent = call(
        receive_kernel, [square, packed], [stacked, square], (block_down, lower, block, thin, up), 6 * product
    )

    def unpacked(value):
        def kernel(packed_ref, block_ref, thin_ref):
            unpack(packed_ref, block_ref, thin_ref)

        return call(kernel, [square, thin_shape], [], (value,), 0)

    block_down = moved(sent, 2, 1)
    block, thin = unpacked(sent)
    inverse = call(invert_kernel, [square], [square, thin_shape], (sent,), 4 * product)
    lower = call(lower_kernel, [square], [], (through, lower_down), product)
    lower_down = moved(lower, 2, 1)
    up = call(above_kernel, [packed], [stacked, stacked], (inverse, thin, lower), 2 * product)
    up = moved(up, -2, 1)
    through, sent = call(
        receive_kernel, [square, packed], [stacked, square], (block_down, lower, block, thin, up), 6 * product
    )

    block_down = moved(sent, 4, 2)
    block, thin = unpacked(sent)
    inverse = call(invert_kernel, [square], [square, thin_shape], (sent,), 4 * product)
    lower, up = call(
        last_lower_kernel, [square, packed], [stacked, stacked], (through, lower_down, inverse, thin), 3 * product
    )
    up = moved(up, -4, 2)
    thin_down = unpacked(block_down)[1]
    inverse = call(invert_kernel, [square], [square, thin_shape], (block_down,), 4 * product)
    block, thin = call(
        last_receive_kernel, [square, thin_shape], [stacked], (inverse, thin_down, lower, block, thin), 2 * product
    )
    solved = call(solve_kernel, [thin_shape], [square, thin_shape], (block, thin, up), product)

    home = lambda s, m: m == s % groups
    parts = [
        exchanged(solved, lambda s, m, k=k: (s, (m + k) % groups), home) for k in range(1, groups)
    ]
    solved = jnp.where(lax.rem(position, groups) == plane, solved, 0.0)
    for bit in range(sections.bit_length() - 1):
        shares = shares + exchanged(shares, lambda s, m, bit=bit: (s ^ (1 << bit), m))
    shares = lax.dynamic_slice_in_dim(shares, position, 1, 0)
    padded = (columns + 8, modes.shape[2])
    whole, payload = call(
        modal_kernel, [thin_shape, padded], [], (solved, *parts, modes[0], shares), product // 32
    )
    for bit in range(sections.bit_length() - 1):
        other = exchanged(payload, lambda s, m, bit=bit: (s ^ (1 << bit), m))
        if bit < sections.bit_length() - 2:
            payload = payload + other
    pieces = call(
        back_kernel,
        [(columns, width)] * groups,
        [thin_shape],
        (plane.reshape(1), payload, other, modes[0]),
        product // 32,
        smem=1,
    )
    summed = pieces[0]
    for k in range(1, groups):
        summed = summed + exchanged(pieces[k], lambda s, m, k=k: (s, (m + k) % groups))
    own_columns = lax.dynamic_slice_in_dim(whole, plane * width, width, 1)
    return (own_columns[None], (own_columns - summed)[None])


def solution(mesh):
    in_specs = (
        P("sec", None, None),
        P("sec", None, None),
        P("sec", None, None),
        P("sec", None, "mode"),
        P("sec"),
        P("sec"),
        P("sec", "mode"),
    )
    out_specs = (P("sec", None, "mode"), P("sec", None, "mode"))
    return jax.shard_map(
        per_device, mesh=mesh, in_specs=in_specs, out_specs=out_specs, check_vma=False
    )
```

profile of v0, /device:TPU:0, one launch (start us, length us, event | category | flops | bytes accessed | tf_op | source)
XLA Modules:
  0.0 115.6 jit_solution(4123908598103929318)
XLA Ops:
  0.7 1.4 %multiply_bitcast_fusion.lower = f32[512,512]{1,0:T(8,128)S(1)} fusion(f32[1,512,512]{2,1,0:T(8,128)} %param.7, f32[]{:T(128)S(6)} %convert_element_type.19), kind=kLoop, calls=%fused_computation.3 | loop fusion | flops 262144 | bytes 2097156 | tf_op jit(solution)/shard_map/mul | solution.py:254
  2.1 0.1 copy-done
  2.2 4.5 %shard_map.87 = f32[1344,128]{1,0:T(8,128)S(1)} custom-call(f32[512,512]{1,0:T(8,128)S(1)} %bitcast.10, f32[16,512]{1,0:T(8,128)S(1)} %bitcast.15, f32[512,512]{1,0:T(8,128)S(1)} %multiply_bitcast_fusion.lower), custom_call_target="tpu_custom_call" | custom-call | flops 4831838208 | bytes 2818048 | tf_op jit(solution)/shard_map/pallas_call | solution.py:211
  6.7 1.3 %collective-permute-start.1 = (f32[1344,128]{1,0:T(8,128)S(1)}, f32[1344,128]{1,0:T(8,128)S(1)}, u32[]{:S(2)}, u32[]{:S(2)}) collective-permute-start(f32[1344,128]{1,0:T(8,128)S(1)} %shard_map.87), channel_id=1, source_target_pairs={{4,0},{6,2},{9,5},{11,7},{12,8},{14,10},{17,13},{19,15},{20,16},{2... | collective-permute-start | bytes 2064392 | tf_op jit(solution)/shard_map/ppermute | solution.py:243
  8.0 0.1 shard_map.86
  8.0 0.7 collective-permute-start
  8.7 0.7 collective-permute-start.3
  9.5 1.2 %collective-permute-done.1.above = f32[1344,128]{1,0:T(8,128)S(1)} collective-permute-done((f32[1344,128]{1,0:T(8,128)S(1)}, f32[1344,128]{1,0:T(8,128)S(1)}, u32[]{:S(2)}, u32[]{:S(2)}) %collective-permute-start.1) | collective-permute-done | bytes 688160 | tf_op jit(solution)/shard_map/ppermute | solution.py:243
  10.7 4.4 %shard_map.88 = (f32[512,512]{1,0:T(8,128)S(1)}, f32[1344,128]{1,0:T(8,128)S(1)}) custom-call(f32[1344,128]{1,0:T(8,128)S(1)} %collective-permute-done.packed, f32[512,512]{1,0:T(8,128)S(1)} %multiply_bitcast_fusion.lower, f32[512,512]{1,0:T(8,128)S(1)} %bitcast.12, f32[16,512]{1,0:T(8,128)S(1)} %bitcast.17, f32[1344,128]{1,0:T(8,128)S(1)} %collective-permute-done.1.above), custom_call_target="tpu_custom_call" | custom-call | flops 4831838208 | bytes 5242880 | tf_op jit(solution)/shard_map/pallas_call | solution.py:211
  15.1 0.2 shard_map.90
  15.3 0.9 collective-permute-start.2
  16.2 2.7 %shard_map.91.inverse = f32[512,512]{1,0:T(8,128)S(1)} custom-call(f32[1344,128]{1,0:T(8,128)S(1)} %get-tuple-element.21.packed_ref.packed), custom_call_target="tpu_custom_call" | custom-call | flops 3221225472 | bytes 1736704 | tf_op jit(solution)/shard_map/pallas_call | solution.py:211
  18.9 0.0 collective-permute-done.3.passed
  18.9 1.0 shard_map.89.lower
  19.9 0.0 copy-start.9
  19.9 2.8 %shard_map.92 = f32[1344,128]{1,0:T(8,128)} custom-call(f32[512,512]{1,0:T(8,128)S(1)} %shard_map.91.inverse, f32[16,512]{1,0:T(8,128)S(1)} %get-tuple-element.24.thin, f32[512,512]{1,0:T(8,128)S(1)} %shard_map.89.lower), custom_call_target="tpu_custom_call" | custom-call | flops 1610612736 | bytes 2818048 | tf_op jit(solution)/shard_map/pallas_call | solution.py:211
  22.7 1.3 %collective-permute-start.4 = (f32[1344,128]{1,0:T(8,128)}, f32[1344,128]{1,0:T(8,128)}, u32[]{:S(2)}, u32[]{:S(2)}) collective-permute-start(f32[1344,128]{1,0:T(8,128)} %shard_map.92), channel_id=1, source_target_pairs={{8,0},{13,5},{18,10},{23,15},{24,16},{29,21}} | collective-permute-start | bytes 2064392 | tf_op jit(solution)/shard_map/ppermute | solution.py:243
  24.0 1.6 %collective-permute-start.6 = (f32[512,512]{1,0:T(8,128)S(1)}, f32[512,512]{1,0:T(8,128)}, u32[]{:S(2)}, u32[]{:S(2)}) collective-permute-start(f32[512,512]{1,0:T(8,128)S(1)} %shard_map.89.lower), channel_id=1, source_target_pairs={{2,10},{7,15},{8,16},{13,21},{18,26},{23,31}} | collective-permute-start | bytes 3145736 | tf_op jit(solution)/shard_map/ppermute | solution.py:243
  25.6 0.1 broadcast.93
  25.7 0.1 reshape.57
  25.8 0.8 copy-done.3
  26.6 22.7 %collective-permute-done.4.above = f32[1344,128]{1,0:T(8,128)} collective-permute-done((f32[1344,128]{1,0:T(8,128)}, f32[1344,128]{1,0:T(8,128)}, u32[]{:S(2)}, u32[]{:S(2)}) %collective-permute-start.4) | collective-permute-done | bytes 688160 | tf_op jit(solution)/shard_map/ppermute | solution.py:243
  49.3 1.1 copy-done.4
  50.4 5.5 %shard_map.93 = (f32[512,512]{1,0:T(8,128)S(1)}, f32[1344,128]{1,0:T(8,128)S(1)}) custom-call(f32[1344,128]{1,0:T(8,128)S(1)} %copy-done.4, f32[512,512]{1,0:T(8,128)S(1)} %shard_map.89.lower, f32[512,512]{1,0:T(8,128)S(1)} %get-tuple-element.23.block, f32[16,512]{1,0:T(8,128)S(1)} %get-tuple-element.24.thin, f32[1344,128]{1,0:T(8,128)} %collective-permute-done.4.above), custom_call_target="tpu_custom_call" | custom-call | flops 4831838208 | bytes 5242880 | tf_op jit(solution)/shard_map/pallas_call | solution.py:211
  56.0 5.3 %collective-permute-start.5 = (f32[1344,128]{1,0:T(8,128)S(1)}, f32[1344,128]{1,0:T(8,128)S(1)}, u32[]{:S(2)}, u32[]{:S(2)}) collective-permute-start(f32[1344,128]{1,0:T(8,128)S(1)} %get-tuple-element.25.packed.packed_ref), channel_id=1, source_target_pairs={{0,16},{5,21},{10,26},{15,31}} | collective-permute-start | bytes 2064392 | tf_op jit(solution)/shard_map/ppermute | solution.py:243
  61.3 2.7 %shard_map.96.inverse = f32[512,512]{1,0:T(8,128)S(1)} custom-call(f32[1344,128]{1,0:T(8,128)S(1)} %get-tuple-element.25.packed.packed_ref), custom_call_target="tpu_custom_call" | custom-call | flops 3221225472 | bytes 1736704 | tf_op jit(solution)/shard_map/pallas_call | solution.py:211
  64.0 0.2 shard_map.97
  64.1 0.0 collective-permute-done.6.passed
  64.2 0.0 copy-start.7
  64.2 0.0 copy-start.8
  64.2 4.2 %shard_map.98 = (f32[512,512]{1,0:T(8,128)S(1)}, f32[1344,128]{1,0:T(8,128)S(1)}) custom-call(f32[512,512]{1,0:T(8,128)S(1)} %get-tuple-element.27.through, f32[512,512]{1,0:T(8,128)} %collective-permute-done.6.passed, f32[512,512]{1,0:T(8,128)S(1)} %shard_map.96.inverse, f32[16,512]{1,0:T(8,128)S(1)} %get-tuple-element.28.thin), custom_call_target="tpu_custom_call" | custom-call | flops 2415919104 | bytes 4915200 | tf_op jit(solution)/shard_map/pallas_call | solution.py:211
  68.4 1.0 copy-done.5
  69.3 1.3 %collective-permute-start.7 = (f32[1344,128]{1,0:T(8,128)S(1)}, f32[1344,128]{1,0:T(8,128)}, u32[]{:S(2)}, u32[]{:S(2)}) collective-permute-start(f32[1344,128]{1,0:T(8,128)S(1)} %get-tuple-element.33), channel_id=1, source_target_pairs={{16,0},{21,5},{26,10},{31,15}} | collective-permute-start | bytes 2064392 | tf_op jit(solution)/shard_map/ppermute | solution.py:243
  70.6 0.6 fusion
  71.2 0.0 collective-permute-start.11
  71.2 1.2 %collective-permute-done.11 = f32[8,256]{1,0:T(8,128)S(1)} collective-permute-done((f32[8,256]{1,0:T(8,128)S(1)}, f32[8,256]{1,0:T(8,128)S(1)}, u32[]{:S(2)}, u32[]{:S(2)}) %collective-permute-start.11) | collective-permute-done | bytes 8224 | tf_op jit(solution)/shard_map/ppermute | solution.py:252
  72.4 3.6 %collective-permute-done.12 = f32[8,256]{1,0:T(8,128)S(1)} collective-permute-done((f32[8,256]{1,0:T(8,128)S(1)}, f32[8,256]{1,0:T(8,128)S(1)}, u32[]{:S(2)}, u32[]{:S(2)}) %collective-permute-start.12) | collective-permute-done | bytes 8224 | tf_op jit(solution)/shard_map/ppermute | solution.py:252
  76.1 3.5 %collective-permute-start.13 = (f32[8,256]{1,0:T(8,128)S(1)}, f32[8,256]{1,0:T(8,128)S(1)}, u32[]{:S(2)}, u32[]{:S(2)}) collective-permute-start(f32[8,256]{1,0:T(8,128)S(1)} %add.62), channel_id=1, source_target_pairs={{0,16},{1,17},{2,18},{3,19},{4,20},{5,21},{6,22},{7,23},{8,24},{9,... | collective-permute-start | bytes 24584 | tf_op jit(solution)/shard_map/ppermute | solution.py:252
  79.5 2.8 %collective-permute-done.13 = f32[8,256]{1,0:T(8,128)S(1)} collective-permute-done((f32[8,256]{1,0:T(8,128)S(1)}, f32[8,256]{1,0:T(8,128)S(1)}, u32[]{:S(2)}, u32[]{:S(2)}) %collective-permute-start.13) | collective-permute-done | bytes 8224 | tf_op jit(solution)/shard_map/ppermute | solution.py:252
  82.4 1.2 %shard_map.95 = (f32[512,512]{1,0:T(8,128)}, f32[16,512]{1,0:T(8,128)S(1)}) custom-call(f32[1344,128]{1,0:T(8,128)S(1)} %collective-permute-done.5.packed.packed_ref), custom_call_target="tpu_custom_call" | custom-call | bytes 1769472 | tf_op jit(solution)/shard_map/pallas_call | solution.py:211
  83.5 2.7 %shard_map.94.inverse = f32[512,512]{1,0:T(8,128)S(1)} custom-call(f32[1344,128]{1,0:T(8,128)S(1)} %collective-permute-done.5.packed.packed_ref), custom_call_target="tpu_custom_call" | custom-call | flops 3221225472 | bytes 1736704 | tf_op jit(solution)/shard_map/pallas_call | solution.py:211
  86.2 1.9 %shard_map.99 = (f32[512,512]{1,0:T(8,128)S(1)}, f32[16,512]{1,0:T(8,128)S(1)}) custom-call(f32[512,512]{1,0:T(8,128)S(1)} %shard_map.94.inverse, f32[16,512]{1,0:T(8,128)S(1)} %get-tuple-element.26.thin_passed, f32[512,512]{1,0:T(8,128)S(1)} %copy-done.6, f32[512,512]{1,0:T(8,128)S(1)} %get-tuple-element.30.block, f32[16,512]{1,0:T(8,128)S(1)} %get-tuple-element.28.thin), custom_call_target="tpu_custom_call" | custom-call | flops 1610612736 | bytes 4292608 | tf_op jit(solution)/shard_map/pallas_call | solution.py:211
  88.1 0.0 collective-permute-done.7.above
  88.1 0.0 copy-start.1
  88.1 4.6 %shard_map.100 = f32[16,512]{1,0:T(8,128)S(1)} custom-call(f32[512,512]{1,0:T(8,128)S(1)} %get-tuple-element.31.block, f32[16,512]{1,0:T(8,128)S(1)} %get-tuple-element.32.thin, f32[1344,128]{1,0:T(8,128)} %collective-permute-done.7.above), custom_call_target="tpu_custom_call" | custom-call | flops 805306368 | bytes 1802240 | tf_op jit(solution)/shard_map/pallas_call | solution.py:211
  92.7 1.3 %collective-permute-start.10 = (f32[16,512]{1,0:T(8,128)S(1)}, f32[16,512]{1,0:T(8,128)S(1)}, u32[]{:S(2)}, u32[]{:S(2)}) collective-permute-start(f32[16,512]{1,0:T(8,128)S(1)} %shard_map.100), channel_id=1, source_target_pairs={{0,3},{5,4},{10,9},{15,14},{16,19},{21,20},{26,25},{31,30}} | collective-permute-start | bytes 98312 | tf_op jit(solution)/shard_map/ppermute | solution.py:252
  94.0 1.3 %collective-permute-start.8 = (f32[16,512]{1,0:T(8,128)S(1)}, f32[16,512]{1,0:T(8,128)S(1)}, u32[]{:S(2)}, u32[]{:S(2)}) collective-permute-start(f32[16,512]{1,0:T(8,128)S(1)} %shard_map.100), channel_id=1, source_target_pairs={{0,1},{5,6},{10,11},{15,12},{16,17},{21,22},{26,27},{31,28}} | collective-permute-start | bytes 98312 | tf_op jit(solution)/shard_map/ppermute | solution.py:252
  95.3 1.3 %collective-permute-start.9 = (f32[16,512]{1,0:T(8,128)S(1)}, f32[16,512]{1,0:T(8,128)S(1)}, u32[]{:S(2)}, u32[]{:S(2)}) collective-permute-start(f32[16,512]{1,0:T(8,128)S(1)} %shard_map.100), channel_id=1, source_target_pairs={{0,2},{5,7},{10,8},{15,13},{16,18},{21,23},{26,24},{31,29}} | collective-permute-start | bytes 98312 | tf_op jit(solution)/shard_map/ppermute | solution.py:252
  96.6 0.2 collective-permute-done.8.b
  96.9 1.3 %collective-permute-done.9.c = f32[16,512]{1,0:T(8,128)S(1)} collective-permute-done((f32[16,512]{1,0:T(8,128)S(1)}, f32[16,512]{1,0:T(8,128)S(1)}, u32[]{:S(2)}, u32[]{:S(2)}) %collective-permute-start.9) | collective-permute-done | bytes 32800 | tf_op jit(solution)/shard_map/ppermute | solution.py:252
  98.2 0.1 shard_map.101
  98.3 0.1 collective-permute-start.14
  98.4 1.2 %collective-permute-done.14 = f32[24,256]{1,0:T(8,128)S(1)} collective-permute-done((f32[24,256]{1,0:T(8,128)S(1)}, f32[24,256]{1,0:T(8,128)S(1)}, u32[]{:S(2)}, u32[]{:S(2)}) %collective-permute-start.14) | collective-permute-done | bytes 24608 | tf_op jit(solution)/shard_map/ppermute | solution.py:252
  99.6 3.2 %collective-permute-start.15 = (f32[24,256]{1,0:T(8,128)S(1)}, f32[24,256]{1,0:T(8,128)S(1)}, u32[]{:S(2)}, u32[]{:S(2)}) collective-permute-start(f32[24,256]{1,0:T(8,128)S(1)} %add.66), channel_id=1, source_target_pairs={{0,8},{1,9},{2,10},{3,11},{4,12},{5,13},{6,14},{7,15},{8,0},{9,1},... | collective-permute-start | bytes 73736 | tf_op jit(solution)/shard_map/ppermute | solution.py:252
  102.7 1.8 %collective-permute-done.15 = f32[24,256]{1,0:T(8,128)S(1)} collective-permute-done((f32[24,256]{1,0:T(8,128)S(1)}, f32[24,256]{1,0:T(8,128)S(1)}, u32[]{:S(2)}, u32[]{:S(2)}) %collective-permute-start.15) | collective-permute-done | bytes 24608 | tf_op jit(solution)/shard_map/ppermute | solution.py:252
  104.5 0.8 collective-permute-start.16
  105.4 3.0 %collective-permute-done.16.other = f32[24,256]{1,0:T(8,128)S(1)} collective-permute-done((f32[24,256]{1,0:T(8,128)S(1)}, f32[24,256]{1,0:T(8,128)S(1)}, u32[]{:S(2)}, u32[]{:S(2)}) %collective-permute-start.16) | collective-permute-done | bytes 24608 | tf_op jit(solution)/shard_map/ppermute | solution.py:252
  108.4 0.2 shard_map.102
  108.5 0.0 collective-permute-start.17
  108.6 2.1 %collective-permute-start.18 = (f32[16,128]{1,0:T(8,128)S(1)}, f32[16,128]{1,0:T(8,128)S(1)}, u32[]{:S(2)}, u32[]{:S(2)}) collective-permute-start(f32[16,128]{1,0:T(8,128)S(1)} %get-tuple-element.38), channel_id=1, source_target_pairs={{0,2},{1,3},{2,0},{3,1},{4,6},{5,7},{6,4},{7,5},{8,10},{9,11},{10,... | collective-permute-start | bytes 24584 | tf_op jit(solution)/shard_map/ppermute | solution.py:252
  110.7 2.9 %collective-permute-start.19 = (f32[16,128]{1,0:T(8,128)S(1)}, f32[16,128]{1,0:T(8,128)S(1)}, u32[]{:S(2)}, u32[]{:S(2)}) collective-permute-start(f32[16,128]{1,0:T(8,128)S(1)} %get-tuple-element.39), channel_id=1, source_target_pairs={{0,3},{1,0},{2,1},{3,2},{4,7},{5,4},{6,5},{7,6},{8,11},{9,8},{10,9... | collective-permute-start | bytes 24584 | tf_op jit(solution)/shard_map/ppermute | solution.py:252
  113.6 0.4 collective-permute-done.17
  114.0 0.9 collective-permute-done.19
  114.9 0.6 subtract_bitcast_fusion
  (25 shorter events, 0.1 us)
Async XLA Ops:
  0.6 1.5 %copy-start = (f32[1,512,512]{2,1,0:T(8,128)S(1)}, f32[1,512,512]{2,1,0:T(8,128)}, u32[]{:S(2)}) copy-start(f32[1,512,512]{2,1,0:T(8,128)} %param.8) | copy-start | bytes 3145732
  0.6 1.5 %copy-start.2 = (f32[1,16,512]{2,1,0:T(8,128)S(1)}, f32[1,16,512]{2,1,0:T(8,128)}, u32[]{:S(2)}) copy-start(f32[1,16,512]{2,1,0:T(8,128)} %param.9) | copy-start | bytes 98308
  6.7 4.0 %collective-permute-start.1 = (f32[1344,128]{1,0:T(8,128)S(1)}, f32[1344,128]{1,0:T(8,128)S(1)}, u32[]{:S(2)}, u32[]{:S(2)}) collective-permute-start(f32[1344,128]{1,0:T(8,128)S(1)} %shard_map.87), channel_id=1, source_target_pairs={{4,0},{6,2},{9,5},{11,7},{12,8},{14,10},{17,13},{19,15},{20,16},{2... | collective-permute-start | bytes 2064392 | tf_op jit(solution)/shard_map/ppermute | solution.py:243
  8.0 2.7 %collective-permute-start = (f32[1344,128]{1,0:T(8,128)S(1)}, f32[1344,128]{1,0:T(8,128)S(1)}, u32[]{:S(2)}, u32[]{:S(2)}) collective-permute-start(f32[1344,128]{1,0:T(8,128)S(1)} %shard_map.86), channel_id=1, source_target_pairs={{1,5},{3,7},{4,8},{6,10},{9,13},{11,15},{12,16},{14,18},{17,21},{1... | collective-permute-start | bytes 2064392 | tf_op jit(solution)/shard_map/ppermute | solution.py:243
  8.7 10.2 %collective-permute-start.3 = (f32[512,512]{1,0:T(8,128)S(1)}, f32[512,512]{1,0:T(8,128)S(1)}, u32[]{:S(2)}, u32[]{:S(2)}) collective-permute-start(f32[512,512]{1,0:T(8,128)S(1)} %multiply_bitcast_fusion.lower), channel_id=1, source_target_pairs={{1,5},{3,7},{4,8},{6,10},{9,13},{11,15},{12,16},{14,18},{17,21},{1... | collective-permute-start | bytes 3145736 | tf_op jit(solution)/shard_map/ppermute | solution.py:243
  15.3 10.4 %collective-permute-start.2 = (f32[1344,128]{1,0:T(8,128)S(1)}, f32[1344,128]{1,0:T(8,128)S(1)}, u32[]{:S(2)}, u32[]{:S(2)}) collective-permute-start(f32[1344,128]{1,0:T(8,128)S(1)} %get-tuple-element.21.packed_ref.packed), channel_id=1, source_target_pairs={{2,10},{7,15},{8,16},{13,21},{18,26},{23,31}} | collective-permute-start | bytes 2064392 | tf_op jit(solution)/shard_map/ppermute | solution.py:243
  19.9 5.7 %copy-start.9 = (s32[16]{0:T(128)S(1)}, s32[16]{0:T(128)}, u32[]{:S(2)}) copy-start(s32[16]{0:T(128)} %param.12) | copy-start | bytes 196
  22.7 26.6 %collective-permute-start.4 = (f32[1344,128]{1,0:T(8,128)}, f32[1344,128]{1,0:T(8,128)}, u32[]{:S(2)}, u32[]{:S(2)}) collective-permute-start(f32[1344,128]{1,0:T(8,128)} %shard_map.92), channel_id=1, source_target_pairs={{8,0},{13,5},{18,10},{23,15},{24,16},{29,21}} | collective-permute-start | bytes 2064392 | tf_op jit(solution)/shard_map/ppermute | solution.py:243
  24.0 40.2 %collective-permute-start.6 = (f32[512,512]{1,0:T(8,128)S(1)}, f32[512,512]{1,0:T(8,128)}, u32[]{:S(2)}, u32[]{:S(2)}) collective-permute-start(f32[512,512]{1,0:T(8,128)S(1)} %shard_map.89.lower), channel_id=1, source_target_pairs={{2,10},{7,15},{8,16},{13,21},{18,26},{23,31}} | collective-permute-start | bytes 3145736 | tf_op jit(solution)/shard_map/ppermute | solution.py:243
  25.8 0.8 copy-start.3
  49.3 1.1 copy-start.4
  56.0 26.4 %collective-permute-start.5 = (f32[1344,128]{1,0:T(8,128)S(1)}, f32[1344,128]{1,0:T(8,128)S(1)}, u32[]{:S(2)}, u32[]{:S(2)}) collective-permute-start(f32[1344,128]{1,0:T(8,128)S(1)} %get-tuple-element.25.packed.packed_ref), channel_id=1, source_target_pairs={{0,16},{5,21},{10,26},{15,31}} | collective-permute-start | bytes 2064392 | tf_op jit(solution)/shard_map/ppermute | solution.py:243
  64.2 6.5 %copy-start.7 = (bf16[1024,256]{1,0:T(8,128)(2,1)S(1)}, bf16[1024,256]{1,0:T(8,128)(2,1)}, u32[]{:S(2)}) copy-start(bf16[1024,256]{1,0:T(8,128)(2,1)} %param.13) | copy-start | bytes 1572868
  64.2 6.5 %copy-start.8 = (s32[1024]{0:T(1024)S(1)}, s32[1024]{0:T(1024)}, u32[]{:S(2)}) copy-start(s32[1024]{0:T(1024)} %param.11) | copy-start | bytes 12292
  68.4 1.0 copy-start.5
  69.3 18.7 %collective-permute-start.7 = (f32[1344,128]{1,0:T(8,128)S(1)}, f32[1344,128]{1,0:T(8,128)}, u32[]{:S(2)}, u32[]{:S(2)}) collective-permute-start(f32[1344,128]{1,0:T(8,128)S(1)} %get-tuple-element.33), channel_id=1, source_target_pairs={{16,0},{21,5},{26,10},{31,15}} | collective-permute-start | bytes 2064392 | tf_op jit(solution)/shard_map/ppermute | solution.py:243
  71.2 1.2 %collective-permute-start.11 = (f32[8,256]{1,0:T(8,128)S(1)}, f32[8,256]{1,0:T(8,128)S(1)}, u32[]{:S(2)}, u32[]{:S(2)}) collective-permute-start(f32[8,256]{1,0:T(8,128)S(1)} %fusion), channel_id=1, source_target_pairs={{0,4},{1,5},{2,6},{3,7},{4,0},{5,1},{6,2},{7,3},{8,12},{9,13},{10,... | collective-permute-start | bytes 24584 | tf_op jit(solution)/shard_map/ppermute | solution.py:252
  72.4 3.7 %collective-permute-start.12 = (f32[8,256]{1,0:T(8,128)S(1)}, f32[8,256]{1,0:T(8,128)S(1)}, u32[]{:S(2)}, u32[]{:S(2)}) collective-permute-start(f32[8,256]{1,0:T(8,128)S(1)} %add.61), channel_id=1, source_target_pairs={{0,8},{1,9},{2,10},{3,11},{4,12},{5,13},{6,14},{7,15},{8,0},{9,1},... | collective-permute-start | bytes 24584 | tf_op jit(solution)/shard_map/ppermute | solution.py:252
  76.1 6.3 %collective-permute-start.13 = (f32[8,256]{1,0:T(8,128)S(1)}, f32[8,256]{1,0:T(8,128)S(1)}, u32[]{:S(2)}, u32[]{:S(2)}) collective-permute-start(f32[8,256]{1,0:T(8,128)S(1)} %add.62), channel_id=1, source_target_pairs={{0,16},{1,17},{2,18},{3,19},{4,20},{5,21},{6,22},{7,23},{8,24},{9,... | collective-permute-start | bytes 24584 | tf_op jit(solution)/shard_map/ppermute | solution.py:252
  83.5 2.7 %copy-start.6 = (f32[512,512]{1,0:T(8,128)S(1)}, f32[512,512]{1,0:T(8,128)}, u32[]{:S(2)}) copy-start(f32[512,512]{1,0:T(8,128)} %copy-done.5) | copy-start | bytes 3145732
  88.1 10.1 %copy-start.1 = (bf16[1,512,256]{2,1,0:T(8,128)(2,1)S(1)}, bf16[1,512,256]{2,1,0:T(8,128)(2,1)}, u32[]{:S(2)}) copy-start(bf16[1,512,256]{2,1,0:T(8,128)(2,1)} %param.10) | copy-start | bytes 786436
  92.7 3.9 %collective-permute-start.10 = (f32[16,512]{1,0:T(8,128)S(1)}, f32[16,512]{1,0:T(8,128)S(1)}, u32[]{:S(2)}, u32[]{:S(2)}) collective-permute-start(f32[16,512]{1,0:T(8,128)S(1)} %shard_map.100), channel_id=1, source_target_pairs={{0,3},{5,4},{10,9},{15,14},{16,19},{21,20},{26,25},{31,30}} | collective-permute-start | bytes 98312 | tf_op jit(solution)/shard_map/ppermute | solution.py:252
  94.0 2.9 %collective-permute-start.8 = (f32[16,512]{1,0:T(8,128)S(1)}, f32[16,512]{1,0:T(8,128)S(1)}, u32[]{:S(2)}, u32[]{:S(2)}) collective-permute-start(f32[16,512]{1,0:T(8,128)S(1)} %shard_map.100), channel_id=1, source_target_pairs={{0,1},{5,6},{10,11},{15,12},{16,17},{21,22},{26,27},{31,28}} | collective-permute-start | bytes 98312 | tf_op jit(solution)/shard_map/ppermute | solution.py:252
  95.3 2.9 %collective-permute-start.9 = (f32[16,512]{1,0:T(8,128)S(1)}, f32[16,512]{1,0:T(8,128)S(1)}, u32[]{:S(2)}, u32[]{:S(2)}) collective-permute-start(f32[16,512]{1,0:T(8,128)S(1)} %shard_map.100), channel_id=1, source_target_pairs={{0,2},{5,7},{10,8},{15,13},{16,18},{21,23},{26,24},{31,29}} | collective-permute-start | bytes 98312 | tf_op jit(solution)/shard_map/ppermute | solution.py:252
  98.3 1.3 %collective-permute-start.14 = (f32[24,256]{1,0:T(8,128)S(1)}, f32[24,256]{1,0:T(8,128)S(1)}, u32[]{:S(2)}, u32[]{:S(2)}) collective-permute-start(f32[24,256]{1,0:T(8,128)S(1)} %get-tuple-element.35), channel_id=1, source_target_pairs={{0,4},{1,5},{2,6},{3,7},{4,0},{5,1},{6,2},{7,3},{8,12},{9,13},{10,... | collective-permute-start | bytes 73736 | tf_op jit(solution)/shard_map/ppermute | solution.py:252
  99.6 5.0 %collective-permute-start.15 = (f32[24,256]{1,0:T(8,128)S(1)}, f32[24,256]{1,0:T(8,128)S(1)}, u32[]{:S(2)}, u32[]{:S(2)}) collective-permute-start(f32[24,256]{1,0:T(8,128)S(1)} %add.66), channel_id=1, source_target_pairs={{0,8},{1,9},{2,10},{3,11},{4,12},{5,13},{6,14},{7,15},{8,0},{9,1},... | collective-permute-start | bytes 73736 | tf_op jit(solution)/shard_map/ppermute | solution.py:252
  104.5 3.8 %collective-permute-start.16 = (f32[24,256]{1,0:T(8,128)S(1)}, f32[24,256]{1,0:T(8,128)S(1)}, u32[]{:S(2)}, u32[]{:S(2)}) collective-permute-start(f32[24,256]{1,0:T(8,128)S(1)} %add.67.mine), channel_id=1, source_target_pairs={{0,16},{1,17},{2,18},{3,19},{4,20},{5,21},{6,22},{7,23},{8,24},{9,... | collective-permute-start | bytes 73736 | tf_op jit(solution)/shard_map/ppermute | solution.py:252
  108.5 5.5 %collective-permute-start.17 = (f32[16,128]{1,0:T(8,128)S(1)}, f32[16,128]{1,0:T(8,128)S(1)}, u32[]{:S(2)}, u32[]{:S(2)}) collective-permute-start(f32[16,128]{1,0:T(8,128)S(1)} %get-tuple-element.37), channel_id=1, source_target_pairs={{0,1},{1,2},{2,3},{3,0},{4,5},{5,6},{6,7},{7,4},{8,9},{9,10},{10,1... | collective-permute-start | bytes 24584 | tf_op jit(solution)/shard_map/ppermute | solution.py:252
  108.6 5.4 %collective-permute-start.18 = (f32[16,128]{1,0:T(8,128)S(1)}, f32[16,128]{1,0:T(8,128)S(1)}, u32[]{:S(2)}, u32[]{:S(2)}) collective-permute-start(f32[16,128]{1,0:T(8,128)S(1)} %get-tuple-element.38), channel_id=1, source_target_pairs={{0,2},{1,3},{2,0},{3,1},{4,6},{5,7},{6,4},{7,5},{8,10},{9,11},{10,... | collective-permute-start | bytes 24584 | tf_op jit(solution)/shard_map/ppermute | solution.py:252
  110.7 4.2 %collective-permute-start.19 = (f32[16,128]{1,0:T(8,128)S(1)}, f32[16,128]{1,0:T(8,128)S(1)}, u32[]{:S(2)}, u32[]{:S(2)}) collective-permute-start(f32[16,128]{1,0:T(8,128)S(1)} %get-tuple-element.39), channel_id=1, source_target_pairs={{0,3},{1,0},{2,1},{3,2},{4,7},{5,4},{6,5},{7,6},{8,11},{9,8},{10,9... | collective-permute-start | bytes 24584 | tf_op jit(solution)/shard_map/ppermute | solution.py:252
where the time goes:
time: 116 us
  waiting for transfers between devices  40.5 us (35%)
  Pallas kernels  38.7 us (33%)
  starting transfers between devices  29.6 us (26%)
  local copies, waits for them, and re-layouts  3.22 us (3%)
  other arithmetic  2.05 us (2%)
    pallas_call x17, Pallas kernels, call(): pl.pallas_call(kernel, out_shape=shapes[0] if single else tuple(shapes),...  38.7 us
    ppermute x8, waiting for transfers between devices, moved(): return lax.ppermute(value, AXES, pairs)  23.9 us
    ppermute x12, waiting for transfers between devices, exchanged(): return lax.ppermute(value, AXES, pairs)  16.5 us
    ppermute x12, starting transfers between devices, exchanged(): return lax.ppermute(value, AXES, pairs)  16.4 us
    ppermute x8, starting transfers between devices, moved(): return lax.ppermute(value, AXES, pairs)  13.1 us
    unnamed x20, local copies, waits for them, and re-layouts  3.07 us
  transfers between devices with their start and end apart: 20, of which 12 were waited for; matrix products, arithmetic and copies ran while one was open for 1% of the time, Pallas kernels for 25%

commit v1 on v0

--- a/solution.py
+++ b/solution.py
@@ -101,6 +101,25 @@
     pack(packed, block, thin)
 
 
+def folded(packed, block, thin, *others):
+    size = block.shape[0]
+    cells = upper(size)
+    for index, (a, b) in enumerate(cells):
+        value = block[band(a), band(b)]
+        for other in others:
+            same = other.shape == packed.shape
+            value = value - (other[band(index), :] if same else other[band(a), band(b)])
+        packed[band(index), :] = value
+    rows = thin.shape[0]
+    for c in range(size // TILE):
+        start = TILE * len(cells) + rows * c
+        value = thin[:, band(c)]
+        for other in others:
+            same = other.shape == packed.shape
+            value = value - (other[start : start + rows, :] if same else other[size:, band(c)])
+        packed[start : start + rows, :] = value
+
+
 def own_kernel(block, thin, lower, packed, stack, out):
     size = block.shape[0]
     inverse = inverse_of(block[...])
@@ -110,34 +129,36 @@
     pack(packed, out, out.at[size:, :])
 
 
-def above_kernel(inverse, thin, lower, packed, stack, out):
-    size = inverse.shape[0]
-    stack[0:size, :] = lower[...].T
-    stack[size:, :] = thin[...]
-    _, out[...] = schur(stack[...], inverse[...], lower[...], dot)
-    pack(packed, out, out.at[size:, :])
-
-
-def receive_kernel(packed, lower, block, thin, above, through, out, stack, whole):
-    size = block.shape[0]
+def receive_kernel(packed, lower, through, full, stack, whole):
+    size = lower.shape[0]
     unpack(packed, whole, stack.at[size:, :])
     inverse = inverse_of(whole[...])
     stack[0:size, :] = lower[...]
-    half, full = schur(stack[...], inverse, lower[...], dot_t)
+    half, full[...] = schur(stack[...], inverse, lower[...], dot_t)
     through[...] = half[0:size, :]
-    stack[...] = full
-    cells = upper(size)
-    for index, (a, b) in enumerate(cells):
-        out[band(index), :] = block[band(a), band(b)] - stack[band(a), band(b)] - above[band(index), :]
-    rows = thin.shape[0]
-    for c in range(size // TILE):
-        start = TILE * len(cells) + rows * c
-        out[start : start + rows, :] = (
-            thin[:, band(c)] - stack[size:, band(c)] - above[start : start + rows, :]
-        )
-
-
-def invert_kernel(packed, inverse, block, thin):
+
+
+def fold_kernel(block, thin, full, above, packed, block_out, thin_out):
+    folded(packed, block, thin, full, above)
+    unpack(packed, block_out, thin_out)
+
+
+def fold_above_kernel(packed_above, passed, block, thin, full, packed, block_out, thin_out, stack, out, whole):
+    size = block.shape[0]
+    unpack(packed_above, whole, stack.at[size:, :])
+    right = split(passed[...])
+    stack[0:size, :] = times(split(passed[...].T), split(whole[...]))
+    stack[size:, :] = -stack[size:, :]
+    out[...] = times(split(stack[...]), right)
+    folded(packed, block, thin, full, out)
+    unpack(packed, block_out, thin_out)
+
+
+def whole_inverse_kernel(block, inverse):
+    inverse[...] = inverse_of(block[...])
+
+
+def invert_kernel(packed, inverse, thin, block):
     unpack(packed, block, thin)
     inverse[...] = inverse_of(block[...])
 
@@ -168,13 +189,16 @@
 def solve_kernel(block, thin, above, solution, whole, own):
     unpack(above, whole, own)
     value = block[...] - whole[...]
-    _, down, along, first = scaled(value)
-    one = split(first)
+    unit, _, along, _ = scaled(value)
+    high, low = split(unit - value * along)
+    rows = thin.shape[0]
     now = (thin[...] - own[...]) * along
     for power in (1, 2, 4):
         moved = now
         for _ in range(power):
-            moved = times(split(moved), one, dot_t)
+            top, rest = split(moved)
+            both = dot(jnp.concatenate([top, rest], axis=0), high)
+            moved = both[0:rows, :] + both[rows:, :] + dot(top, low)
         now = now + moved
     solution[...] = now
 
@@ -189,10 +213,11 @@
     payload[rows : rows + 1, :] = shares[...] * (amplitude / (1.0 + amplitude))
 
 
-def back_kernel(place, mine, other, modes, *outs):
-    total = mine[...] + other[...]
-    scratch = outs[-1]
-    pieces = outs[:-1]
+def back_kernel_of(count, place, *refs):
+    parts, modes, pieces, scratch = refs[:count], refs[count], refs[count + 1 : -1], refs[-1]
+    total = parts[0][...]
+    for part in parts[1:]:
+        total = total + part[...]
     rows = scratch.shape[0]
     damping = total[rows : rows + 1, :]
     removed = (total[0:rows, :] * (damping / (1.0 + damping))).astype(bf16)
@@ -214,7 +239,7 @@
         in_specs=[scalar] * smem + [vmem] * (len(args) - smem),
         out_specs=vmem if single else tuple([vmem] * len(outs)),
         scratch_shapes=[pltpu.VMEM(s, f32) for s in scratch],
-        compiler_params=pltpu.CompilerParams(vmem_limit_bytes=40 << 20),
+        compiler_params=pltpu.CompilerParams(vmem_limit_bytes=24 << 20),
         cost_estimate=pl.CostEstimate(flops=flops, transcendentals=0, bytes_accessed=moved),
     )(*args)
 
@@ -229,30 +254,22 @@
     square, stacked, thin_shape = (size, size), (size + columns, size), (columns, size)
     product = 6 * size**3
 
-    def moved(value, step, level):
-        stride = min(2 ** (level + 1), groups)
-        pairs = []
-        for target in range(sections):
-            source = target - step
-            if 0 <= source < sections:
-                pairs += [
-                    (source * groups + m, target * groups + m)
-                    for m in range(groups)
-                    if (target - m) % stride == 0
-                ]
-        return lax.ppermute(value, AXES, pairs)
-
-    def exchanged(value, to, wanted=lambda s, m: True):
+    def sent_to(value, where):
         pairs = []
         for s in range(sections):
             for m in range(groups):
-                if wanted(s, m):
-                    s_to, m_to = to(s, m)
-                    pairs.append((s * groups + m, s_to * groups + m_to))
+                to = where(s, m)
+                if to is not None and 0 <= to[0] < sections:
+                    pairs.append((s * groups + m, to[0] * groups + to[1]))
         return lax.ppermute(value, AXES, pairs)
 
-    lower = coupling[0] * (position >= 1).astype(f32)
-    block, thin = stiffness[0], loads[0]
+    def home(s):
+        return s % 2 + 2 * ((s // 2 + s // 4) % 2) if groups == 4 else s % groups
+
+    def parity(s, m):
+        return (s - m) % min(2, groups) == 0
+
+    block, thin, lower = stiffness[0], loads[0], coupling[0]
 
     matches = (jnp.arange(sections, dtype=jnp.int32)[:, None] == joint_section[None, :]).astype(f32)
     joint_regime = jnp.broadcast_to(regime[:, None], (regime.shape[0], BUCKET)).reshape(-1)
@@ -263,74 +280,85 @@
     shares = jnp.dot(
         matches * joint_rate[None, :], weights * weights, precision=lax.Precision.HIGHEST
     )
-
-    sent = call(pack_kernel, [packed], [], (block, thin), 0)
-    block_down = moved(sent, 1, 0)
-    lower_down = moved(lower, 1, 0)
+    bits = sections.bit_length() - 1
+    rounds = [[1]] + [[1 << b, 2 << b, 3 << b] if b + 1 < bits else [1 << b] for b in range(1, bits, 2)]
+
+    def summed_over_sections(value):
+        parts = [value]
+        for steps in rounds:
+            value = parts[0]
+            for part in parts[1:]:
+                value = value + part
+            parts = [value] + [sent_to(value, lambda s, m, k=k: (s ^ k, m)) for k in steps]
+        return parts
+
+    shares = sum(summed_over_sections(shares))
+    shares = lax.dynamic_slice_in_dim(shares, position, 1, 0)
+
+    packed_down = call(pack_kernel, [packed], [], (block, thin), 0)
+    packed_down = sent_to(packed_down, lambda s, m: (s + 1, m) if parity(s + 1, m) else None)
+
+    def needs_lower(s, m):
+        return m == home(s) or (s + 2 < sections and m == home(s + 2))
+
+    lower_down = sent_to(lower, lambda s, m: (s + 1, m) if s >= 1 and needs_lower(s + 1, m) else None)
+    lower_up = sent_to(lower, lambda s, m: (s - 1, m) if s >= 1 and m == home(s - 1) else None)
     up = call(own_kernel, [packed], [stacked, stacked], (block, thin, lower), 6 * product)
-    up = moved(up, -1, 0)
-    through, sent = call(
-        receive_kernel, [square, packed], [stacked, square], (block_down, lower, block, thin, up), 6 * product
-    )
-
-    def unpacked(value):
-        def kernel(packed_ref, block_ref, thin_ref):
-            unpack(packed_ref, block_ref, thin_ref)
-
-        return call(kernel, [square, thin_shape], [], (value,), 0)
-
-    block_down = moved(sent, 2, 1)
-    block, thin = unpacked(sent)
-    inverse = call(invert_kernel, [square], [square, thin_shape], (sent,), 4 * product)
+    up = sent_to(up, lambda s, m: (s - 1, m) if parity(s - 1, m) else None)
+    through, full = call(receive_kernel, [square, stacked], [stacked, square], (packed_down, lower), 6 * product)
+    sent, block, thin = call(fold_kernel, [packed, square, thin_shape], [], (block, thin, full, up), 0)
+
+    packed_down = sent_to(sent, lambda s, m: (s + 2, m) if m == home(s + 2) else None)
+    up = call(own_kernel, [packed], [stacked, stacked], (block, thin, through), 6 * product)
+    up = sent_to(up, lambda s, m: (s - 2, m) if m == home(s - 2) else None)
+    lower_down, shares = lax.optimization_barrier((lower_down, shares))
     lower = call(lower_kernel, [square], [], (through, lower_down), product)
-    lower_down = moved(lower, 2, 1)
-    up = call(above_kernel, [packed], [stacked, stacked], (inverse, thin, lower), 2 * product)
-    up = moved(up, -2, 1)
-    through, sent = call(
-        receive_kernel, [square, packed], [stacked, square], (block_down, lower, block, thin, up), 6 * product
-    )
-
-    block_down = moved(sent, 4, 2)
-    block, thin = unpacked(sent)
-    inverse = call(invert_kernel, [square], [square, thin_shape], (sent,), 4 * product)
+    lower_down = sent_to(lower, lambda s, m: (s + 2, m) if s >= 2 and m == home(s + 2) else None)
+    through, full = call(receive_kernel, [square, stacked], [stacked, square], (packed_down, lower), 6 * product)
+    sent, block, thin = call(
+        fold_above_kernel,
+        [packed, square, thin_shape],
+        [stacked, stacked, square],
+        (up, lower_up, block, thin, full),
+        2 * product,
+    )
+
+    packed_down = sent_to(sent, lambda s, m: (s + 4, home(s + 4)) if m == home(s) else None)
+    inverse = call(whole_inverse_kernel, [square], [], (block,), 4 * product)
     lower, up = call(
         last_lower_kernel, [square, packed], [stacked, stacked], (through, lower_down, inverse, thin), 3 * product
     )
-    up = moved(up, -4, 2)
-    thin_down = unpacked(block_down)[1]
-    inverse = call(invert_kernel, [square], [square, thin_shape], (block_down,), 4 * product)
+    up = sent_to(up, lambda s, m: (s - 4, home(s - 4)) if m == home(s) else None)
+    inverse, thin_down = call(
+        invert_kernel, [square, thin_shape], [square], (packed_down,), 4 * product
+    )
     block, thin = call(
         last_receive_kernel, [square, thin_shape], [stacked], (inverse, thin_down, lower, block, thin), 2 * product
     )
     solved = call(solve_kernel, [thin_shape], [square, thin_shape], (block, thin, up), product)
 
-    home = lambda s, m: m == s % groups
     parts = [
-        exchanged(solved, lambda s, m, k=k: (s, (m + k) % groups), home) for k in range(1, groups)
+        sent_to(solved, lambda s, m, k=k: (s, (m + k) % groups) if m == home(s) else None)
+        for k in range(1, groups)
     ]
-    solved = jnp.where(lax.rem(position, groups) == plane, solved, 0.0)
-    for bit in range(sections.bit_length() - 1):
-        shares = shares + exchanged(shares, lambda s, m, bit=bit: (s ^ (1 << bit), m))
-    shares = lax.dynamic_slice_in_dim(shares, position, 1, 0)
+    homes = jnp.asarray([home(s) for s in range(sections)], jnp.int32)
+    solved = jnp.where(homes[position] == plane, solved, 0.0)
     padded = (columns + 8, modes.shape[2])
     whole, payload = call(
         modal_kernel, [thin_shape, padded], [], (solved, *parts, modes[0], shares), product // 32
     )
-    for bit in range(sections.bit_length() - 1):
-        other = exchanged(payload, lambda s, m, bit=bit: (s ^ (1 << bit), m))
-        if bit < sections.bit_length() - 2:
-            payload = payload + other
+    parts = summed_over_sections(payload)
     pieces = call(
-        back_kernel,
+        functools.partial(back_kernel_of, len(parts)),
         [(columns, width)] * groups,
         [thin_shape],
-        (plane.reshape(1), payload, other, modes[0]),
+        (plane.reshape(1), *parts, modes[0]),
         product // 32,
         smem=1,
     )
     summed = pieces[0]
     for k in range(1, groups):
-        summed = summed + exchanged(pieces[k], lambda s, m, k=k: (s, (m + k) % groups))
+        summed = summed + sent_to(pieces[k], lambda s, m, k=k: (s, (m + k) % groups))
     own_columns = lax.dynamic_slice_in_dim(whole, plane * width, width, 1)
     return (own_columns[None], (own_columns - summed)[None])
 

time: 116 us -> 108 us (0.931)
  waiting for transfers between devices: 40.5 us -> 21.5 us
  starting transfers between devices: 29.6 us -> 41.4 us
  Pallas kernels: 38.7 us -> 36.6 us
  other arithmetic: 2.05 us -> 0.65 us
    ppermute x20 -> x23, waiting for transfers between devices: 40.5 us -> 21.5 us  [sent_to(): return lax.ppermute(value, AXES, pairs)]
    ppermute x20 -> x23, starting transfers between devices: 29.6 us -> 41.4 us  [sent_to(): return lax.ppermute(value, AXES, pairs)]
    pallas_call x17 -> x15, Pallas kernels: 38.7 us -> 36.6 us  [call(): pl.pallas_call(kernel, out_shape=shapes[0] if single else tuple(shapes),...]
    mul x1 -> x0, other arithmetic: 1.4 us -> none  [per_device(): lower = coupling[0] * (position >= 1).astype(f32)]
    unnamed x20 -> x26, local copies, waits for them, and re-layouts: 3.07 us -> 3.02 us
  transfers between devices with their start and end apart: 20 -> 23, of which waited for: 12 -> 11; matrix products, arithmetic and copies ran while one was open for 1% -> 2% of each run, Pallas kernels for 25% -> 32%
where the time goes in v1:
time: 108 us; the launch traced here: 107 us
  starting transfers between devices  41.4 us (38%)
  Pallas kernels  36.6 us (34%)
  waiting for transfers between devices  21.5 us (20%)
  local copies, waits for them, and re-layouts  3.75 us (3%)
  between operations  1.71 us (2%)
  matrix products  1.62 us (2%)
    ppermute x23, starting transfers between devices, sent_to(): return lax.ppermute(value, AXES, pairs)  41.4 us
    pallas_call x15, Pallas kernels, call(): pl.pallas_call(kernel, out_shape=shapes[0] if single else tuple(shapes),...  36.6 us
    ppermute x23, waiting for transfers between devices, sent_to(): return lax.ppermute(value, AXES, pairs)  21.5 us
    unnamed x26, local copies, waits for them, and re-layouts  3.02 us
  transfers between devices with their start and end apart: 23, of which 11 were waited for; matrix products, arithmetic and copies ran while one was open for 2% of the time, Pallas kernels for 32%

profile of v1, /device:TPU:0, one launch (start us, length us, event | category | flops | bytes accessed | tf_op | source)
XLA Modules:
  0.0 107.3 jit_solution(1819021830945533711)
XLA Ops:
  0.6 0.7 collective-permute-start.5
  1.4 0.0 copy-start
  1.4 1.2 %copy-done = f32[1,512,512]{2,1,0:T(8,128)S(1)} copy-done((f32[1,512,512]{2,1,0:T(8,128)S(1)}, f32[1,512,512]{2,1,0:T(8,128)}, u32[]{:S(2)}) %copy-start) | copy-done | bytes 1048600
  2.6 0.8 copy-done.3
  3.4 0.1 shard_map.95
  3.4 0.0 copy-start.11
  3.4 0.0 copy-start.10
  3.4 1.7 %collective-permute-start = (f32[1344,128]{1,0:T(8,128)S(1)}, f32[1344,128]{1,0:T(8,128)}, u32[]{:S(2)}, u32[]{:S(2)}) collective-permute-start(f32[1344,128]{1,0:T(8,128)S(1)} %shard_map.95), channel_id=1, source_target_pairs={{1,5},{3,7},{4,8},{6,10},{9,13},{11,15},{12,16},{14,18},{17,21},{1... | collective-permute-start | bytes 2064392 | tf_op jit(solution)/shard_map/ppermute | solution.py:264
  5.1 5.3 %shard_map.97 = f32[1344,128]{1,0:T(8,128)} custom-call(f32[512,512]{1,0:T(8,128)S(1)} %bitcast.11, f32[16,512]{1,0:T(8,128)S(1)} %bitcast.16, f32[512,512]{1,0:T(8,128)S(1)} %bitcast.19), custom_call_target="tpu_custom_call" | custom-call | flops 4831838208 | bytes 2818048 | tf_op jit(solution)/shard_map/pallas_call | solution.py:236
  10.4 1.3 %collective-permute-start.1 = (f32[1344,128]{1,0:T(8,128)}, f32[1344,128]{1,0:T(8,128)S(1)}, u32[]{:S(2)}, u32[]{:S(2)}) collective-permute-start(f32[1344,128]{1,0:T(8,128)} %shard_map.97), channel_id=1, source_target_pairs={{4,0},{6,2},{9,5},{11,7},{12,8},{14,10},{17,13},{19,15},{20,16},{2... | collective-permute-start | bytes 2064392 | tf_op jit(solution)/shard_map/ppermute | solution.py:264
  11.7 0.1 broadcast.90
  11.8 0.1 reshape.55
  11.9 1.6 %fusion = f32[8,256]{1,0:T(8,128)S(1)} fusion(bf16[1024,256]{1,0:T(8,128)(2,1)} %param.14, f32[1024]{0:T(1024)S(1)} %reshape.55, s32[1024]{0:T(1024)S(1)} %copy-done.10), kind=kOutput, calls=%fused_computation | convolution fusion | flops 25706496 | bytes 540672 | tf_op jit(solution)/shard_map/dot_general | solution.py:280
  13.5 4.3 %collective-permute-start.6 = (f32[8,256]{1,0:T(8,128)S(1)}, f32[8,256]{1,0:T(8,128)S(1)}, u32[]{:S(2)}, u32[]{:S(2)}) collective-permute-start(f32[8,256]{1,0:T(8,128)S(1)} %fusion), channel_id=1, source_target_pairs={{0,4},{1,5},{2,6},{3,7},{4,0},{5,1},{6,2},{7,3},{8,12},{9,13},{10,... | collective-permute-start | bytes 24584 | tf_op jit(solution)/shard_map/ppermute | solution.py:264
  17.8 1.3 %collective-permute-start.3 = (f32[512,512]{1,0:T(8,128)S(1)}, f32[512,512]{1,0:T(8,128)}, u32[]{:S(2)}, u32[]{:S(2)}) collective-permute-start(f32[512,512]{1,0:T(8,128)S(1)} %bitcast.20), channel_id=1, source_target_pairs={{4,0},{9,5},{14,10},{19,15},{22,18},{27,23},{28,24}} | collective-permute-start | bytes 3145736 | tf_op jit(solution)/shard_map/ppermute | solution.py:264
  19.2 0.0 copy-start.1
  19.2 0.0 copy-start.4
  19.2 2.5 %collective-permute-start.7 = (f32[8,256]{1,0:T(8,128)S(1)}, f32[8,256]{1,0:T(8,128)S(1)}, u32[]{:S(2)}, u32[]{:S(2)}) collective-permute-start(f32[8,256]{1,0:T(8,128)S(1)} %add.63), channel_id=1, source_target_pairs={{0,8},{1,9},{2,10},{3,11},{4,12},{5,13},{6,14},{7,15},{8,0},{9,1},... | collective-permute-start | bytes 24584 | tf_op jit(solution)/shard_map/ppermute | solution.py:264
  21.7 0.0 collective-permute-done.packed
  21.7 6.7 %collective-permute-start.8 = (f32[8,256]{1,0:T(8,128)S(1)}, f32[8,256]{1,0:T(8,128)S(1)}, u32[]{:S(2)}, u32[]{:S(2)}) collective-permute-start(f32[8,256]{1,0:T(8,128)S(1)} %add.63), channel_id=1, source_target_pairs={{0,16},{1,17},{2,18},{3,19},{4,20},{5,21},{6,22},{7,23},{8,24},{9,... | collective-permute-start | bytes 24584 | tf_op jit(solution)/shard_map/ppermute | solution.py:264
  28.4 5.5 %shard_map.96 = (f32[512,512]{1,0:T(8,128)S(1)}, f32[528,512]{1,0:T(8,128)S(1)}) custom-call(f32[1344,128]{1,0:T(8,128)} %collective-permute-done.packed, f32[512,512]{1,0:T(8,128)S(1)} %bitcast.21), custom_call_target="tpu_custom_call" | custom-call | flops 4831838208 | bytes 3866624 | tf_op jit(solution)/shard_map/pallas_call | solution.py:236
  33.9 0.0 collective-permute-done.1.above
  33.9 0.1 collective-permute-start.9
  34.0 0.2 shard_map.98
  34.3 0.9 collective-permute-start.4
  35.2 4.5 %shard_map.99 = f32[1344,128]{1,0:T(8,128)S(1)} custom-call(f32[512,512]{1,0:T(8,128)S(1)} %get-tuple-element.27.block, f32[16,512]{1,0:T(8,128)S(1)} %get-tuple-element.28.thin, f32[512,512]{1,0:T(8,128)S(1)} %get-tuple-element.29.lower.through), custom_call_target="tpu_custom_call" | custom-call | flops 4831838208 | bytes 2818048 | tf_op jit(solution)/shard_map/pallas_call | solution.py:236
  39.6 1.3 %collective-permute-start.2 = (f32[1344,128]{1,0:T(8,128)S(1)}, f32[1344,128]{1,0:T(8,128)S(1)}, u32[]{:S(2)}, u32[]{:S(2)}) collective-permute-start(f32[1344,128]{1,0:T(8,128)S(1)} %shard_map.99), channel_id=1, source_target_pairs={{8,0},{13,5},{18,10},{23,15},{26,18},{31,23}} | collective-permute-start | bytes 2064392 | tf_op jit(solution)/shard_map/ppermute | solution.py:264
  41.0 1.0 shard_map.100.lower
  42.0 0.7 collective-permute-start.11
  42.7 4.4 %shard_map.101 = (f32[512,512]{1,0:T(8,128)S(1)}, f32[528,512]{1,0:T(8,128)S(1)}) custom-call(f32[1344,128]{1,0:T(8,128)S(1)} %collective-permute-done.4.packed, f32[512,512]{1,0:T(8,128)S(1)} %shard_map.100.lower), custom_call_target="tpu_custom_call" | custom-call | flops 4831838208 | bytes 3866624 | tf_op jit(solution)/shard_map/pallas_call | solution.py:236
  47.2 5.3 %collective-permute-done.2.packed_above = f32[1344,128]{1,0:T(8,128)S(1)} collective-permute-done((f32[1344,128]{1,0:T(8,128)S(1)}, f32[1344,128]{1,0:T(8,128)S(1)}, u32[]{:S(2)}, u32[]{:S(2)}) %collective-permute-start.2) | collective-permute-done | bytes 688160 | tf_op jit(solution)/shard_map/ppermute | solution.py:264
  52.5 3.3 %shard_map.102 = (f32[1344,128]{1,0:T(8,128)S(1)}, f32[512,512]{1,0:T(8,128)S(1)}, f32[16,512]{1,0:T(8,128)S(1)}) custom-call(f32[1344,128]{1,0:T(8,128)S(1)} %collective-permute-done.2.packed_above, f32[512,512]{1,0:T(8,128)} %collective-permute-done.3.passed, f32[512,512]{1,0:T(8,128)S(1)} %get-tuple-element.27.block, ...), custom_call_target="tpu_custom_call" | custom-call | flops 1610612736 | bytes 5668864 | tf_op jit(solution)/shard_map/pallas_call | solution.py:236
  55.8 6.3 %collective-permute-start.10 = (f32[1344,128]{1,0:T(8,128)S(1)}, f32[1344,128]{1,0:T(8,128)S(1)}, u32[]{:S(2)}, u32[]{:S(2)}) collective-permute-start(f32[1344,128]{1,0:T(8,128)S(1)} %get-tuple-element.33), channel_id=1, source_target_pairs={{0,18},{5,23},{10,24},{15,29}} | collective-permute-start | bytes 2064392 | tf_op jit(solution)/shard_map/ppermute | solution.py:264
  62.2 2.7 %shard_map.104.inverse = f32[512,512]{1,0:T(8,128)S(1)} custom-call(f32[512,512]{1,0:T(8,128)S(1)} %get-tuple-element.37.block), custom_call_target="tpu_custom_call" | custom-call | flops 3221225472 | bytes 2097152 | tf_op jit(solution)/shard_map/pallas_call | solution.py:236
  64.8 0.0 copy-start.12
  64.9 2.9 %shard_map.105 = (f32[512,512]{1,0:T(8,128)S(1)}, f32[1344,128]{1,0:T(8,128)S(1)}) custom-call(f32[512,512]{1,0:T(8,128)S(1)} %get-tuple-element.36.through, f32[512,512]{1,0:T(8,128)S(1)} %collective-permute-done.11.passed, f32[512,512]{1,0:T(8,128)S(1)} %shard_map.104.inverse, f32[16,512]{1,0:T(8,128)S(1)} %get-tuple-element.38.thin), custom_call_target="tpu_custom_call" | custom-call | flops 2415919104 | bytes 4915200 | tf_op jit(solution)/shard_map/pallas_call | solution.py:236
  67.8 1.0 copy-done.8
  68.7 1.3 %collective-permute-start.12 = (f32[1344,128]{1,0:T(8,128)S(1)}, f32[1344,128]{1,0:T(8,128)S(1)}, u32[]{:S(2)}, u32[]{:S(2)}) collective-permute-start(f32[1344,128]{1,0:T(8,128)S(1)} %get-tuple-element.42), channel_id=1, source_target_pairs={{18,0},{23,5},{24,10},{29,15}} | collective-permute-start | bytes 2064392 | tf_op jit(solution)/shard_map/ppermute | solution.py:264
  70.0 0.6 dynamic_slice.9
  71.3 2.7 %shard_map.103 = (f32[512,512]{1,0:T(8,128)S(1)}, f32[16,512]{1,0:T(8,128)S(1)}) custom-call(f32[1344,128]{1,0:T(8,128)S(1)} %collective-permute-done.10.packed), custom_call_target="tpu_custom_call" | custom-call | flops 3221225472 | bytes 1769472 | tf_op jit(solution)/shard_map/pallas_call | solution.py:236
  74.0 1.9 %shard_map.106 = (f32[512,512]{1,0:T(8,128)S(1)}, f32[16,512]{1,0:T(8,128)S(1)}) custom-call(f32[512,512]{1,0:T(8,128)S(1)} %get-tuple-element.34.inverse, f32[16,512]{1,0:T(8,128)S(1)} %get-tuple-element.35.thin_passed, f32[512,512]{1,0:T(8,128)S(1)} %copy-done.9, f32[512,512]{1,0:T(8,128)S(1)} %copy-done.7, f32[16,512]{1,0:T(8,128)S(1)} %get-tuple-element.38.thin), custom_call_target="tpu_custom_call" | custom-call | flops 1610612736 | bytes 4292608 | tf_op jit(solution)/shard_map/pallas_call | solution.py:236
  75.9 8.2 %collective-permute-done.12.above = f32[1344,128]{1,0:T(8,128)S(1)} collective-permute-done((f32[1344,128]{1,0:T(8,128)S(1)}, f32[1344,128]{1,0:T(8,128)S(1)}, u32[]{:S(2)}, u32[]{:S(2)}) %collective-permute-start.12) | collective-permute-done | bytes 688160 | tf_op jit(solution)/shard_map/ppermute | solution.py:264
  84.1 1.9 %shard_map.107 = f32[16,512]{1,0:T(8,128)S(1)} custom-call(f32[512,512]{1,0:T(8,128)S(1)} %get-tuple-element.40.block, f32[16,512]{1,0:T(8,128)S(1)} %get-tuple-element.41.thin, f32[1344,128]{1,0:T(8,128)S(1)} %collective-permute-done.12.above), custom_call_target="tpu_custom_call" | custom-call | flops 805306368 | bytes 1802240 | tf_op jit(solution)/shard_map/pallas_call | solution.py:236
  86.0 1.3 %collective-permute-start.13 = (f32[16,512]{1,0:T(8,128)S(1)}, f32[16,512]{1,0:T(8,128)S(1)}, u32[]{:S(2)}, u32[]{:S(2)}) collective-permute-start(f32[16,512]{1,0:T(8,128)S(1)} %shard_map.107), channel_id=1, source_target_pairs={{0,1},{5,6},{10,11},{15,12},{18,19},{23,20},{24,25},{29,30}} | collective-permute-start | bytes 98312 | tf_op jit(solution)/shard_map/ppermute | solution.py:264
  87.2 1.3 %collective-permute-start.14 = (f32[16,512]{1,0:T(8,128)S(1)}, f32[16,512]{1,0:T(8,128)S(1)}, u32[]{:S(2)}, u32[]{:S(2)}) collective-permute-start(f32[16,512]{1,0:T(8,128)S(1)} %shard_map.107), channel_id=1, source_target_pairs={{0,2},{5,7},{10,8},{15,13},{18,16},{23,21},{24,26},{29,31}} | collective-permute-start | bytes 98312 | tf_op jit(solution)/shard_map/ppermute | solution.py:264
  88.5 1.3 %collective-permute-start.15 = (f32[16,512]{1,0:T(8,128)S(1)}, f32[16,512]{1,0:T(8,128)S(1)}, u32[]{:S(2)}, u32[]{:S(2)}) collective-permute-start(f32[16,512]{1,0:T(8,128)S(1)} %shard_map.107), channel_id=1, source_target_pairs={{0,3},{5,4},{10,9},{15,14},{18,17},{23,22},{24,27},{29,28}} | collective-permute-start | bytes 98312 | tf_op jit(solution)/shard_map/ppermute | solution.py:264
  89.9 0.3 collective-permute-done.14.c
  90.1 1.3 %collective-permute-done.15.d = f32[16,512]{1,0:T(8,128)S(1)} collective-permute-done((f32[16,512]{1,0:T(8,128)S(1)}, f32[16,512]{1,0:T(8,128)S(1)}, u32[]{:S(2)}, u32[]{:S(2)}) %collective-permute-start.15) | collective-permute-done | bytes 32800 | tf_op jit(solution)/shard_map/ppermute | solution.py:264
  91.4 0.1 shard_map.108
  91.6 0.1 collective-permute-start.16
  91.7 1.2 %collective-permute-done.16 = f32[24,256]{1,0:T(8,128)S(1)} collective-permute-done((f32[24,256]{1,0:T(8,128)S(1)}, f32[24,256]{1,0:T(8,128)S(1)}, u32[]{:S(2)}, u32[]{:S(2)}) %collective-permute-start.16) | collective-permute-done | bytes 24608 | tf_op jit(solution)/shard_map/ppermute | solution.py:264
  92.8 0.3 collective-permute-start.17
  93.1 3.2 %collective-permute-start.19 = (f32[24,256]{1,0:T(8,128)S(1)}, f32[24,256]{1,0:T(8,128)S(1)}, u32[]{:S(2)}, u32[]{:S(2)}) collective-permute-start(f32[24,256]{1,0:T(8,128)S(1)} %add.68.refs_0_), channel_id=1, source_target_pairs={{0,24},{1,25},{2,26},{3,27},{4,28},{5,29},{6,30},{7,31},{8,16},{9,... | collective-permute-start | bytes 73736 | tf_op jit(solution)/shard_map/ppermute | solution.py:264
  96.3 0.3 collective-permute-done.17.refs_1_
  96.7 0.5 collective-permute-done.18.refs_2_
  97.2 0.9 collective-permute-done.19.refs_3_
  98.1 0.2 shard_map.109
  98.3 1.6 %collective-permute-start.20 = (f32[16,128]{1,0:T(8,128)S(1)}, f32[16,128]{1,0:T(8,128)S(1)}, u32[]{:S(2)}, u32[]{:S(2)}) collective-permute-start(f32[16,128]{1,0:T(8,128)S(1)} %get-tuple-element.47), channel_id=1, source_target_pairs={{0,1},{1,2},{2,3},{3,0},{4,5},{5,6},{6,7},{7,4},{8,9},{9,10},{10,1... | collective-permute-start | bytes 24584 | tf_op jit(solution)/shard_map/ppermute | solution.py:264
  99.9 3.1 %collective-permute-start.21 = (f32[16,128]{1,0:T(8,128)S(1)}, f32[16,128]{1,0:T(8,128)S(1)}, u32[]{:S(2)}, u32[]{:S(2)}) collective-permute-start(f32[16,128]{1,0:T(8,128)S(1)} %get-tuple-element.48), channel_id=1, source_target_pairs={{0,2},{1,3},{2,0},{3,1},{4,6},{5,7},{6,4},{7,5},{8,10},{9,11},{10,... | collective-permute-start | bytes 24584 | tf_op jit(solution)/shard_map/ppermute | solution.py:264
  103.0 0.2 collective-permute-start.22
  103.2 0.9 collective-permute-done.20
  104.1 0.6 collective-permute-done.21
  104.6 2.0 %collective-permute-done.22 = f32[16,128]{1,0:T(8,128)S(1)} collective-permute-done((f32[16,128]{1,0:T(8,128)S(1)}, f32[16,128]{1,0:T(8,128)S(1)}, u32[]{:S(2)}, u32[]{:S(2)}) %collective-permute-start.22) | collective-permute-done | bytes 8224 | tf_op jit(solution)/shard_map/ppermute | solution.py:264
  106.7 0.6 subtract_bitcast_fusion
  (33 shorter events, 0.1 us)
Async XLA Ops:
  0.6 40.3 %collective-permute-start.5 = (f32[512,512]{1,0:T(8,128)}, f32[512,512]{1,0:T(8,128)S(1)}, u32[]{:S(2)}, u32[]{:S(2)}) collective-permute-start(f32[512,512]{1,0:T(8,128)} %bitcast.18), channel_id=1, source_target_pairs={{6,10},{11,15},{12,16},{14,18},{17,21},{19,23},{20,24},{25,29}} | collective-permute-start | bytes 3145736 | tf_op jit(solution)/shard_map/ppermute | solution.py:264
  1.4 1.2 %copy-start = (f32[1,512,512]{2,1,0:T(8,128)S(1)}, f32[1,512,512]{2,1,0:T(8,128)}, u32[]{:S(2)}) copy-start(f32[1,512,512]{2,1,0:T(8,128)} %param.9) | copy-start | bytes 3145732
  2.6 0.8 copy-start.3
  3.4 1.7 %copy-start.5 = (f32[1,512,512]{2,1,0:T(8,128)S(1)}, f32[1,512,512]{2,1,0:T(8,128)}, u32[]{:S(2)}) copy-start(f32[1,512,512]{2,1,0:T(8,128)} %param.8) | copy-start | bytes 3145732
  3.4 8.3 %copy-start.11 = (s32[16]{0:T(128)S(1)}, s32[16]{0:T(128)}, u32[]{:S(2)}) copy-start(s32[16]{0:T(128)} %param.13) | copy-start | bytes 196
  3.4 8.5 %copy-start.10 = (s32[1024]{0:T(1024)S(1)}, s32[1024]{0:T(1024)}, u32[]{:S(2)}) copy-start(s32[1024]{0:T(1024)} %param.12) | copy-start | bytes 12292
  3.4 18.3 %collective-permute-start = (f32[1344,128]{1,0:T(8,128)S(1)}, f32[1344,128]{1,0:T(8,128)}, u32[]{:S(2)}, u32[]{:S(2)}) collective-permute-start(f32[1344,128]{1,0:T(8,128)S(1)} %shard_map.95), channel_id=1, source_target_pairs={{1,5},{3,7},{4,8},{6,10},{9,13},{11,15},{12,16},{14,18},{17,21},{1... | collective-permute-start | bytes 2064392 | tf_op jit(solution)/shard_map/ppermute | solution.py:264
  10.4 23.5 %collective-permute-start.1 = (f32[1344,128]{1,0:T(8,128)}, f32[1344,128]{1,0:T(8,128)S(1)}, u32[]{:S(2)}, u32[]{:S(2)}) collective-permute-start(f32[1344,128]{1,0:T(8,128)} %shard_map.97), channel_id=1, source_target_pairs={{4,0},{6,2},{9,5},{11,7},{12,8},{14,10},{17,13},{19,15},{20,16},{2... | collective-permute-start | bytes 2064392 | tf_op jit(solution)/shard_map/ppermute | solution.py:264
  13.5 5.6 %collective-permute-start.6 = (f32[8,256]{1,0:T(8,128)S(1)}, f32[8,256]{1,0:T(8,128)S(1)}, u32[]{:S(2)}, u32[]{:S(2)}) collective-permute-start(f32[8,256]{1,0:T(8,128)S(1)} %fusion), channel_id=1, source_target_pairs={{0,4},{1,5},{2,6},{3,7},{4,0},{5,1},{6,2},{7,3},{8,12},{9,13},{10,... | collective-permute-start | bytes 24584 | tf_op jit(solution)/shard_map/ppermute | solution.py:264
  17.8 29.3 %collective-permute-start.3 = (f32[512,512]{1,0:T(8,128)S(1)}, f32[512,512]{1,0:T(8,128)}, u32[]{:S(2)}, u32[]{:S(2)}) collective-permute-start(f32[512,512]{1,0:T(8,128)S(1)} %bitcast.20), channel_id=1, source_target_pairs={{4,0},{9,5},{14,10},{19,15},{22,18},{27,23},{28,24}} | collective-permute-start | bytes 3145736 | tf_op jit(solution)/shard_map/ppermute | solution.py:264
  19.2 14.9 %copy-start.1 = (f32[1,512,512]{2,1,0:T(8,128)S(1)}, f32[1,512,512]{2,1,0:T(8,128)}, u32[]{:S(2)}) copy-start(f32[1,512,512]{2,1,0:T(8,128)} %param.9) | copy-start | bytes 3145732
  19.2 14.9 %copy-start.4 = (f32[1,16,512]{2,1,0:T(8,128)S(1)}, f32[1,16,512]{2,1,0:T(8,128)}, u32[]{:S(2)}) copy-start(f32[1,16,512]{2,1,0:T(8,128)} %param.10) | copy-start | bytes 98308
  19.2 15.1 %collective-permute-start.7 = (f32[8,256]{1,0:T(8,128)S(1)}, f32[8,256]{1,0:T(8,128)S(1)}, u32[]{:S(2)}, u32[]{:S(2)}) collective-permute-start(f32[8,256]{1,0:T(8,128)S(1)} %add.63), channel_id=1, source_target_pairs={{0,8},{1,9},{2,10},{3,11},{4,12},{5,13},{6,14},{7,15},{8,0},{9,1},... | collective-permute-start | bytes 24584 | tf_op jit(solution)/shard_map/ppermute | solution.py:264
  21.7 17.9 %collective-permute-start.8 = (f32[8,256]{1,0:T(8,128)S(1)}, f32[8,256]{1,0:T(8,128)S(1)}, u32[]{:S(2)}, u32[]{:S(2)}) collective-permute-start(f32[8,256]{1,0:T(8,128)S(1)} %add.63), channel_id=1, source_target_pairs={{0,16},{1,17},{2,18},{3,19},{4,20},{5,21},{6,22},{7,23},{8,24},{9,... | collective-permute-start | bytes 24584 | tf_op jit(solution)/shard_map/ppermute | solution.py:264
  33.9 7.0 %collective-permute-start.9 = (f32[8,256]{1,0:T(8,128)S(1)}, f32[8,256]{1,0:T(8,128)S(1)}, u32[]{:S(2)}, u32[]{:S(2)}) collective-permute-start(f32[8,256]{1,0:T(8,128)S(1)} %add.63), channel_id=1, source_target_pairs={{0,24},{1,25},{2,26},{3,27},{4,28},{5,29},{6,30},{7,31},{8,16},{9,... | collective-permute-start | bytes 24584 | tf_op jit(solution)/shard_map/ppermute | solution.py:264
  34.3 8.5 %collective-permute-start.4 = (f32[1344,128]{1,0:T(8,128)S(1)}, f32[1344,128]{1,0:T(8,128)S(1)}, u32[]{:S(2)}, u32[]{:S(2)}) collective-permute-start(f32[1344,128]{1,0:T(8,128)S(1)} %get-tuple-element.30), channel_id=1, source_target_pairs={{2,10},{7,15},{10,18},{15,23},{16,24},{21,29}} | collective-permute-start | bytes 2064392 | tf_op jit(solution)/shard_map/ppermute | solution.py:264
  39.6 12.8 %collective-permute-start.2 = (f32[1344,128]{1,0:T(8,128)S(1)}, f32[1344,128]{1,0:T(8,128)S(1)}, u32[]{:S(2)}, u32[]{:S(2)}) collective-permute-start(f32[1344,128]{1,0:T(8,128)S(1)} %shard_map.99), channel_id=1, source_target_pairs={{8,0},{13,5},{18,10},{23,15},{26,18},{31,23}} | collective-permute-start | bytes 2064392 | tf_op jit(solution)/shard_map/ppermute | solution.py:264
  42.0 22.8 %collective-permute-start.11 = (f32[512,512]{1,0:T(8,128)S(1)}, f32[512,512]{1,0:T(8,128)S(1)}, u32[]{:S(2)}, u32[]{:S(2)}) collective-permute-start(f32[512,512]{1,0:T(8,128)S(1)} %shard_map.100.lower), channel_id=1, source_target_pairs={{10,18},{15,23},{16,24},{21,29}} | collective-permute-start | bytes 3145736 | tf_op jit(solution)/shard_map/ppermute | solution.py:264
  55.8 9.0 %copy-start.6 = (f32[512,512]{1,0:T(8,128)}, f32[512,512]{1,0:T(8,128)S(1)}, u32[]{:S(2)}) copy-start(f32[512,512]{1,0:T(8,128)S(1)} %get-tuple-element.37.block) | copy-start | bytes 3145732
  55.8 15.5 %collective-permute-start.10 = (f32[1344,128]{1,0:T(8,128)S(1)}, f32[1344,128]{1,0:T(8,128)S(1)}, u32[]{:S(2)}, u32[]{:S(2)}) collective-permute-start(f32[1344,128]{1,0:T(8,128)S(1)} %get-tuple-element.33), channel_id=1, source_target_pairs={{0,18},{5,23},{10,24},{15,29}} | collective-permute-start | bytes 2064392 | tf_op jit(solution)/shard_map/ppermute | solution.py:264
  64.8 5.2 %copy-start.12 = (s32[8]{0:T(128)S(1)}, s32[8]{0:T(128)}, u32[]{:S(2)}) copy-start(s32[8]{0:T(128)} %constant.38.clone) | copy-start | bytes 100
  67.7 1.0 copy-start.8
  68.7 15.3 %collective-permute-start.12 = (f32[1344,128]{1,0:T(8,128)S(1)}, f32[1344,128]{1,0:T(8,128)S(1)}, u32[]{:S(2)}, u32[]{:S(2)}) collective-permute-start(f32[1344,128]{1,0:T(8,128)S(1)} %get-tuple-element.42), channel_id=1, source_target_pairs={{18,0},{23,5},{24,10},{29,15}} | collective-permute-start | bytes 2064392 | tf_op jit(solution)/shard_map/ppermute | solution.py:264
  71.3 2.7 %copy-start.7 = (f32[512,512]{1,0:T(8,128)S(1)}, f32[512,512]{1,0:T(8,128)}, u32[]{:S(2)}) copy-start(f32[512,512]{1,0:T(8,128)} %copy-done.6) | copy-start | bytes 3145732
  71.3 2.7 %copy-start.9 = (f32[512,512]{1,0:T(8,128)S(1)}, f32[512,512]{1,0:T(8,128)}, u32[]{:S(2)}) copy-start(f32[512,512]{1,0:T(8,128)} %copy-done.8) | copy-start | bytes 3145732
  84.1 7.4 %copy-start.2 = (bf16[1,512,256]{2,1,0:T(8,128)(2,1)S(1)}, bf16[1,512,256]{2,1,0:T(8,128)(2,1)}, u32[]{:S(2)}) copy-start(bf16[1,512,256]{2,1,0:T(8,128)(2,1)} %param.11) | copy-start | bytes 786436
  86.0 3.9 %collective-permute-start.13 = (f32[16,512]{1,0:T(8,128)S(1)}, f32[16,512]{1,0:T(8,128)S(1)}, u32[]{:S(2)}, u32[]{:S(2)}) collective-permute-start(f32[16,512]{1,0:T(8,128)S(1)} %shard_map.107), channel_id=1, source_target_pairs={{0,1},{5,6},{10,11},{15,12},{18,19},{23,20},{24,25},{29,30}} | collective-permute-start | bytes 98312 | tf_op jit(solution)/shard_map/ppermute | solution.py:264
  87.2 2.9 %collective-permute-start.14 = (f32[16,512]{1,0:T(8,128)S(1)}, f32[16,512]{1,0:T(8,128)S(1)}, u32[]{:S(2)}, u32[]{:S(2)}) collective-permute-start(f32[16,512]{1,0:T(8,128)S(1)} %shard_map.107), channel_id=1, source_target_pairs={{0,2},{5,7},{10,8},{15,13},{18,16},{23,21},{24,26},{29,31}} | collective-permute-start | bytes 98312 | tf_op jit(solution)/shard_map/ppermute | solution.py:264
  88.5 2.9 %collective-permute-start.15 = (f32[16,512]{1,0:T(8,128)S(1)}, f32[16,512]{1,0:T(8,128)S(1)}, u32[]{:S(2)}, u32[]{:S(2)}) collective-permute-start(f32[16,512]{1,0:T(8,128)S(1)} %shard_map.107), channel_id=1, source_target_pairs={{0,3},{5,4},{10,9},{15,14},{18,17},{23,22},{24,27},{29,28}} | collective-permute-start | bytes 98312 | tf_op jit(solution)/shard_map/ppermute | solution.py:264
  91.6 1.3 %collective-permute-start.16 = (f32[24,256]{1,0:T(8,128)S(1)}, f32[24,256]{1,0:T(8,128)S(1)}, u32[]{:S(2)}, u32[]{:S(2)}) collective-permute-start(f32[24,256]{1,0:T(8,128)S(1)} %get-tuple-element.45), channel_id=1, source_target_pairs={{0,4},{1,5},{2,6},{3,7},{4,0},{5,1},{6,2},{7,3},{8,12},{9,13},{10,... | collective-permute-start | bytes 73736 | tf_op jit(solution)/shard_map/ppermute | solution.py:264
  92.8 3.8 %collective-permute-start.17 = (f32[24,256]{1,0:T(8,128)S(1)}, f32[24,256]{1,0:T(8,128)S(1)}, u32[]{:S(2)}, u32[]{:S(2)}) collective-permute-start(f32[24,256]{1,0:T(8,128)S(1)} %add.68.refs_0_), channel_id=1, source_target_pairs={{0,8},{1,9},{2,10},{3,11},{4,12},{5,13},{6,14},{7,15},{8,0},{9,1},... | collective-permute-start | bytes 73736 | tf_op jit(solution)/shard_map/ppermute | solution.py:264
  93.1 4.1 %collective-permute-start.18 = (f32[24,256]{1,0:T(8,128)S(1)}, f32[24,256]{1,0:T(8,128)S(1)}, u32[]{:S(2)}, u32[]{:S(2)}) collective-permute-start(f32[24,256]{1,0:T(8,128)S(1)} %add.68.refs_0_), channel_id=1, source_target_pairs={{0,16},{1,17},{2,18},{3,19},{4,20},{5,21},{6,22},{7,23},{8,24},{9,... | collective-permute-start | bytes 73736 | tf_op jit(solution)/shard_map/ppermute | solution.py:264
  93.1 5.0 %collective-permute-start.19 = (f32[24,256]{1,0:T(8,128)S(1)}, f32[24,256]{1,0:T(8,128)S(1)}, u32[]{:S(2)}, u32[]{:S(2)}) collective-permute-start(f32[24,256]{1,0:T(8,128)S(1)} %add.68.refs_0_), channel_id=1, source_target_pairs={{0,24},{1,25},{2,26},{3,27},{4,28},{5,29},{6,30},{7,31},{8,16},{9,... | collective-permute-start | bytes 73736 | tf_op jit(solution)/shard_map/ppermute | solution.py:264
  98.3 5.8 %collective-permute-start.20 = (f32[16,128]{1,0:T(8,128)S(1)}, f32[16,128]{1,0:T(8,128)S(1)}, u32[]{:S(2)}, u32[]{:S(2)}) collective-permute-start(f32[16,128]{1,0:T(8,128)S(1)} %get-tuple-element.47), channel_id=1, source_target_pairs={{0,1},{1,2},{2,3},{3,0},{4,5},{5,6},{6,7},{7,4},{8,9},{9,10},{10,1... | collective-permute-start | bytes 24584 | tf_op jit(solution)/shard_map/ppermute | solution.py:264
  99.9 4.7 %collective-permute-start.21 = (f32[16,128]{1,0:T(8,128)S(1)}, f32[16,128]{1,0:T(8,128)S(1)}, u32[]{:S(2)}, u32[]{:S(2)}) collective-permute-start(f32[16,128]{1,0:T(8,128)S(1)} %get-tuple-element.48), channel_id=1, source_target_pairs={{0,2},{1,3},{2,0},{3,1},{4,6},{5,7},{6,4},{7,5},{8,10},{9,11},{10,... | collective-permute-start | bytes 24584 | tf_op jit(solution)/shard_map/ppermute | solution.py:264
  103.0 3.7 %collective-permute-start.22 = (f32[16,128]{1,0:T(8,128)S(1)}, f32[16,128]{1,0:T(8,128)S(1)}, u32[]{:S(2)}, u32[]{:S(2)}) collective-permute-start(f32[16,128]{1,0:T(8,128)S(1)} %get-tuple-element.49), channel_id=1, source_target_pairs={{0,3},{1,0},{2,1},{3,2},{4,7},{5,4},{6,5},{7,6},{8,11},{9,8},{10,9... | collective-permute-start | bytes 24584 | tf_op jit(solution)/shard_map/ppermute | solution.py:264

commit v2 on v1

--- a/solution.py
+++ b/solution.py
@@ -85,7 +85,7 @@
     one = split(first)
     second = times(one, one)
     two = split(second)
-    third = times(one, two)
+    third = dot(one[0], two[0])
     fourth = dot(two[0], two[0]).astype(bf16)
     series = unit + first + second + third
     series = series + dot(series.astype(bf16), fourth)
@@ -97,8 +97,21 @@
     return through, times(split(through), split(right), product)
 
 
-def pack_kernel(block, thin, packed):
-    pack(packed, block, thin)
+def pack_kernel(block, thin, packed, sems):
+    size = block.shape[0]
+    cells = upper(size)
+    rows = thin.shape[0]
+    pairs = [
+        (block.at[band(a), band(b)], packed.at[band(index), :]) for index, (a, b) in enumerate(cells)
+    ]
+    for c in range(size // TILE):
+        start = TILE * len(cells) + rows * c
+        pairs.append((thin.at[:, band(c)], packed.at[start : start + rows, :]))
+    copies = [pltpu.make_async_copy(src, dst, sems.at[k]) for k, (src, dst) in enumerate(pairs)]
+    for copy in copies:
+        copy.start()
+    for copy in copies:
+        copy.wait()
 
 
 def folded(packed, block, thin, *others):
@@ -163,7 +176,7 @@
     inverse[...] = inverse_of(block[...])
 
 
-def lower_kernel(through, passed, lower):
+def lower_kernel(through, passed, after, lower):
     lower[...] = -times(split(through[...]), split(passed[...]))
 
 
@@ -228,31 +241,45 @@
         piece[...] = scratch[:, pl.ds(pl.multiple_of(start, width), width)]
 
 
-def call(kernel, outs, scratch, args, flops, smem=0):
+def packed_from_hbm(block, thin, packed):
+    cells = len(upper(block.shape[0])) + block.shape[0] // TILE
+    return pl.pallas_call(
+        pack_kernel,
+        out_shape=jax.ShapeDtypeStruct(packed, f32),
+        in_specs=[pl.BlockSpec(memory_space=pl.ANY)] * 2,
+        out_specs=pl.BlockSpec(memory_space=pltpu.VMEM),
+        scratch_shapes=[pltpu.SemaphoreType.DMA((cells,))],
+    )(block, thin)
+
+
+def call(kernel, outs, scratch, args, flops, smem=0, after=0):
     vmem, scalar = pl.BlockSpec(memory_space=pltpu.VMEM), pl.BlockSpec(memory_space=pltpu.SMEM)
-    moved = sum(a.size * a.dtype.itemsize for a in args) + sum(4 * o[0] * o[1] for o in outs)
     single = len(outs) == 1
     shapes = [jax.ShapeDtypeStruct(o, f32) for o in outs]
     return pl.pallas_call(
         kernel,
         out_shape=shapes[0] if single else tuple(shapes),
-        in_specs=[scalar] * smem + [vmem] * (len(args) - smem),
+        in_specs=[scalar] * smem
+        + [vmem] * (len(args) - smem - after)
+        + [pl.BlockSpec(memory_space=pl.ANY)] * after,
         out_specs=vmem if single else tuple([vmem] * len(outs)),
         scratch_shapes=[pltpu.VMEM(s, f32) for s in scratch],
-        compiler_params=pltpu.CompilerParams(vmem_limit_bytes=24 << 20),
-        cost_estimate=pl.CostEstimate(flops=flops, transcendentals=0, bytes_accessed=moved),
+        compiler_params=pltpu.CompilerParams(vmem_limit_bytes=20 << 20),
+        cost_estimate=pl.CostEstimate(flops=int(flops), transcendentals=0, bytes_accessed=1024),
     )(*args)
 
 
 def per_device(coupling, stiffness, loads, modes, joint_section, regime, participation):
     position, plane = lax.axis_index("sec"), lax.axis_index("mode")
     sections, groups = lax.axis_size("sec"), lax.axis_size("mode")
+    assert groups == 4 and LEVELS == 3
     size, columns = stiffness.shape[1], loads.shape[1]
     width = size // groups
     cells = len(upper(size))
     packed = (TILE * cells + columns * (size // TILE), TILE)
     square, stacked, thin_shape = (size, size), (size + columns, size), (columns, size)
-    product = 6 * size**3
+    product = 0.05 * 6 * size**3
+    long = 1.0 * 6 * size**3
 
     def sent_to(value, where):
         pairs = []
@@ -264,10 +291,10 @@
         return lax.ppermute(value, AXES, pairs)
 
     def home(s):
-        return s % 2 + 2 * ((s // 2 + s // 4) % 2) if groups == 4 else s % groups
+        return 2 * (s % 2) + (s // 2 + s // 4) % 2
 
     def parity(s, m):
-        return (s - m) % min(2, groups) == 0
+        return m // 2 == s % 2
 
     block, thin, lower = stiffness[0], loads[0], coupling[0]
 
@@ -295,36 +322,37 @@
     shares = sum(summed_over_sections(shares))
     shares = lax.dynamic_slice_in_dim(shares, position, 1, 0)
 
-    packed_down = call(pack_kernel, [packed], [], (block, thin), 0)
+    packed_down = packed_from_hbm(block, thin, packed)
+    lower_sent, packed_down = lax.optimization_barrier((lower, packed_down))
     packed_down = sent_to(packed_down, lambda s, m: (s + 1, m) if parity(s + 1, m) else None)
 
     def needs_lower(s, m):
         return m == home(s) or (s + 2 < sections and m == home(s + 2))
 
-    lower_down = sent_to(lower, lambda s, m: (s + 1, m) if s >= 1 and needs_lower(s + 1, m) else None)
-    lower_up = sent_to(lower, lambda s, m: (s - 1, m) if s >= 1 and m == home(s - 1) else None)
+    lower_down = sent_to(lower_sent, lambda s, m: (s + 1, m) if s >= 1 and needs_lower(s + 1, m) else None)
+    lower_up = sent_to(lower_sent, lambda s, m: (s - 1, m) if s >= 1 and m == home(s - 1) else None)
     up = call(own_kernel, [packed], [stacked, stacked], (block, thin, lower), 6 * product)
     up = sent_to(up, lambda s, m: (s - 1, m) if parity(s - 1, m) else None)
-    through, full = call(receive_kernel, [square, stacked], [stacked, square], (packed_down, lower), 6 * product)
+    through, full = call(receive_kernel, [square, stacked], [stacked, square], (packed_down, lower), 6 * long)
     sent, block, thin = call(fold_kernel, [packed, square, thin_shape], [], (block, thin, full, up), 0)
 
     packed_down = sent_to(sent, lambda s, m: (s + 2, m) if m == home(s + 2) else None)
-    up = call(own_kernel, [packed], [stacked, stacked], (block, thin, through), 6 * product)
-    up = sent_to(up, lambda s, m: (s - 2, m) if m == home(s - 2) else None)
-    lower_down, shares = lax.optimization_barrier((lower_down, shares))
-    lower = call(lower_kernel, [square], [], (through, lower_down), product)
+    bracket = call(own_kernel, [packed], [stacked, stacked], (block, thin, through), 6 * product)
+    up = sent_to(bracket, lambda s, m: (s - 2, m) if m == home(s - 2) else None)
+    lower = call(lower_kernel, [square], [], (through, lower_down, bracket), product, after=1)
     lower_down = sent_to(lower, lambda s, m: (s + 2, m) if s >= 2 and m == home(s + 2) else None)
-    through, full = call(receive_kernel, [square, stacked], [stacked, square], (packed_down, lower), 6 * product)
+    packed_down, shares = lax.optimization_barrier((packed_down, shares))
+    through, full = call(receive_kernel, [square, stacked], [stacked, square], (packed_down, lower), 6 * long)
     sent, block, thin = call(
         fold_above_kernel,
         [packed, square, thin_shape],
         [stacked, stacked, square],
         (up, lower_up, block, thin, full),
-        2 * product,
+        2 * long,
     )
 
     packed_down = sent_to(sent, lambda s, m: (s + 4, home(s + 4)) if m == home(s) else None)
-    inverse = call(whole_inverse_kernel, [square], [], (block,), 4 * product)
+    inverse = call(whole_inverse_kernel, [square], [], (block,), 4 * long)
     lower, up = call(
         last_lower_kernel, [square, packed], [stacked, stacked], (through, lower_down, inverse, thin), 3 * product
     )

time: 108 us -> 123 us (1.14)
  starting transfers between devices: 41.4 us -> 53.9 us
  Pallas kernels: 36.6 us -> 42.4 us
    ppermute x23, starting transfers between devices: 41.4 us -> 53.9 us  [sent_to(): return lax.ppermute(value, AXES, pairs)]
    pallas_call x15 -> x14, Pallas kernels: 36.6 us -> 40.2 us  [call(): pl.pallas_call(kernel, out_shape=shapes[0] if single else tuple(shapes),...]
    pallas_call x0 -> x1, Pallas kernels: none -> 2.18 us  [packed_from_hbm(): pl.pallas_call(pack_kernel, out_shape=jax.ShapeDtypeStruct(packed, f32),...]
    unnamed x26 -> x22, local copies, waits for them, and re-layouts: 3.02 us -> 2.25 us
  transfers between devices with their start and end apart: 23 -> 23, of which waited for: 11 -> 13; matrix products, arithmetic and copies ran while one was open for 2% -> 1% of each run, Pallas kernels for 32% -> 31%
where the time goes in v2:
time: 123 us
  starting transfers between devices  53.9 us (44%)
  Pallas kernels  42.4 us (34%)
  waiting for transfers between devices  20.7 us (17%)
  local copies, waits for them, and re-layouts  2.98 us (2%)
  between operations  1.66 us (1%)
    ppermute x23, starting transfers between devices, sent_to(): return lax.ppermute(value, AXES, pairs)  53.9 us
    pallas_call x14, Pallas kernels, call(): pl.pallas_call(kernel, out_shape=shapes[0] if single else tuple(shapes),...  40.2 us
    ppermute x23, waiting for transfers between devices, sent_to(): return lax.ppermute(value, AXES, pairs)  20.7 us
  transfers between devices with their start and end apart: 23, of which 13 were waited for; matrix products, arithmetic and copies ran while one was open for 1% of the time, Pallas kernels for 31%

profile of v2, /device:TPU:0, one launch (start us, length us, event | category | flops | bytes accessed | tf_op | source)
XLA Modules:
  0.0 122.9 jit_solution(15368218413738991335)
XLA Ops:
  0.6 2.2 %shard_map.95 = f32[1344,128]{1,0:T(8,128)} custom-call(f32[512,512]{1,0:T(8,128)} %bitcast.10, f32[16,512]{1,0:T(8,128)} %bitcast.15), custom_call_target="tpu_custom_call" | custom-call | tf_op jit(solution)/shard_map/pallas_call | solution.py:246
  2.8 0.7 collective-permute-start
  3.6 5.1 %shard_map.97 = f32[1344,128]{1,0:T(8,128)S(1)} custom-call(f32[512,512]{1,0:T(8,128)S(1)} %bitcast.11, f32[16,512]{1,0:T(8,128)S(1)} %bitcast.16, f32[512,512]{1,0:T(8,128)} %bitcast.3.lower), custom_call_target="tpu_custom_call" | custom-call | flops 241591904 | bytes 1024 | tf_op jit(solution)/shard_map/pallas_call | solution.py:259
  8.7 1.3 %collective-permute-start.1 = (f32[1344,128]{1,0:T(8,128)S(1)}, f32[1344,128]{1,0:T(8,128)S(1)}, u32[]{:S(2)}, u32[]{:S(2)}) collective-permute-start(f32[1344,128]{1,0:T(8,128)S(1)} %shard_map.97), channel_id=1, source_target_pairs={{4,0},{5,1},{10,6},{11,7},{12,8},{13,9},{18,14},{19,15},{20,16},{2... | collective-permute-start | bytes 2064392 | tf_op jit(solution)/shard_map/ppermute | solution.py:291
  10.0 1.7 %collective-permute-start.9 = (f32[512,512]{1,0:T(8,128)}, f32[512,512]{1,0:T(8,128)}, u32[]{:S(2)}, u32[]{:S(2)}) collective-permute-start(f32[512,512]{1,0:T(8,128)} %bitcast.3.lower), channel_id=1, source_target_pairs={{5,9},{11,15},{12,16},{13,17},{18,22},{19,23},{20,24},{26,30}} | collective-permute-start | bytes 3145736 | tf_op jit(solution)/shard_map/ppermute | solution.py:291
  11.7 0.0 collective-permute-done.packed
  11.7 5.1 %shard_map.96 = (f32[512,512]{1,0:T(8,128)S(1)}, f32[528,512]{1,0:T(8,128)S(1)}) custom-call(f32[1344,128]{1,0:T(8,128)S(1)} %collective-permute-done.packed, f32[512,512]{1,0:T(8,128)} %bitcast.3.lower), custom_call_target="tpu_custom_call" | custom-call | flops 4831838208 | bytes 1024 | tf_op jit(solution)/shard_map/pallas_call | solution.py:259
  16.8 0.0 copy-start.9
  16.8 1.1 shard_map.98
  17.9 1.5 %collective-permute-start.4 = (f32[1344,128]{1,0:T(8,128)}, f32[1344,128]{1,0:T(8,128)}, u32[]{:S(2)}, u32[]{:S(2)}) collective-permute-start(f32[1344,128]{1,0:T(8,128)} %get-tuple-element.34), channel_id=1, source_target_pairs={{1,9},{7,15},{9,17},{15,23},{16,24},{22,30}} | collective-permute-start | bytes 2064392 | tf_op jit(solution)/shard_map/ppermute | solution.py:291
  19.4 1.3 %collective-permute-start.3 = (f32[512,512]{1,0:T(8,128)}, f32[512,512]{1,0:T(8,128)}, u32[]{:S(2)}, u32[]{:S(2)}) collective-permute-start(f32[512,512]{1,0:T(8,128)} %bitcast.3.lower), channel_id=1, source_target_pairs={{4,0},{10,6},{13,9},{19,15},{21,17},{27,23},{28,24}} | collective-permute-start | bytes 3145736 | tf_op jit(solution)/shard_map/ppermute | solution.py:291
  20.7 0.1 broadcast.90
  20.8 0.1 reshape.55
  20.9 3.9 %shard_map.99.after = f32[1344,128]{1,0:T(8,128)S(1)} custom-call(f32[512,512]{1,0:T(8,128)S(1)} %get-tuple-element.30.block, f32[16,512]{1,0:T(8,128)S(1)} %get-tuple-element.31.thin, f32[512,512]{1,0:T(8,128)S(1)} %get-tuple-element.32.lower.through), custom_call_target="tpu_custom_call" | custom-call | flops 241591904 | bytes 1024 | tf_op jit(solution)/shard_map/pallas_call | solution.py:259
  24.8 1.3 %collective-permute-start.2 = (f32[1344,128]{1,0:T(8,128)S(1)}, f32[1344,128]{1,0:T(8,128)}, u32[]{:S(2)}, u32[]{:S(2)}) collective-permute-start(f32[1344,128]{1,0:T(8,128)S(1)} %shard_map.99.after), channel_id=1, source_target_pairs={{8,0},{14,6},{17,9},{23,15},{25,17},{31,23}} | collective-permute-start | bytes 2064392 | tf_op jit(solution)/shard_map/ppermute | solution.py:291
  26.1 0.6 fusion
  26.7 5.5 %collective-permute-start.5 = (f32[8,256]{1,0:T(8,128)S(1)}, f32[8,256]{1,0:T(8,128)S(1)}, u32[]{:S(2)}, u32[]{:S(2)}) collective-permute-start(f32[8,256]{1,0:T(8,128)S(1)} %fusion), channel_id=1, source_target_pairs={{0,4},{1,5},{2,6},{3,7},{4,0},{5,1},{6,2},{7,3},{8,12},{9,13},{10,... | collective-permute-start | bytes 24584 | tf_op jit(solution)/shard_map/ppermute | solution.py:291
  32.2 0.0 collective-permute-done.9.passed
  32.2 3.2 %shard_map.100.lower = f32[512,512]{1,0:T(8,128)} custom-call(f32[512,512]{1,0:T(8,128)S(1)} %get-tuple-element.32.lower.through, f32[512,512]{1,0:T(8,128)} %collective-permute-done.9.passed, f32[1344,128]{1,0:T(8,128)S(1)} %shard_map.99.after), custom_call_target="tpu_custom_call" | custom-call | flops 40265320 | bytes 1024 | tf_op jit(solution)/shard_map/pallas_call | solution.py:259
  35.4 0.9 collective-permute-start.11
  36.4 0.0 collective-permute-done.5
  36.4 2.3 %collective-permute-start.6 = (f32[8,256]{1,0:T(8,128)S(1)}, f32[8,256]{1,0:T(8,128)S(1)}, u32[]{:S(2)}, u32[]{:S(2)}) collective-permute-start(f32[8,256]{1,0:T(8,128)S(1)} %add.63), channel_id=1, source_target_pairs={{0,8},{1,9},{2,10},{3,11},{4,12},{5,13},{6,14},{7,15},{8,0},{9,1},... | collective-permute-start | bytes 24584 | tf_op jit(solution)/shard_map/ppermute | solution.py:291
  38.7 3.4 %collective-permute-done.6 = f32[8,256]{1,0:T(8,128)S(1)} collective-permute-done((f32[8,256]{1,0:T(8,128)S(1)}, f32[8,256]{1,0:T(8,128)S(1)}, u32[]{:S(2)}, u32[]{:S(2)}) %collective-permute-start.6) | collective-permute-done | bytes 8224 | tf_op jit(solution)/shard_map/ppermute | solution.py:291
  42.1 12.6 %collective-permute-start.7 = (f32[8,256]{1,0:T(8,128)S(1)}, f32[8,256]{1,0:T(8,128)S(1)}, u32[]{:S(2)}, u32[]{:S(2)}) collective-permute-start(f32[8,256]{1,0:T(8,128)S(1)} %add.63), channel_id=1, source_target_pairs={{0,16},{1,17},{2,18},{3,19},{4,20},{5,21},{6,22},{7,23},{8,24},{9,... | collective-permute-start | bytes 24584 | tf_op jit(solution)/shard_map/ppermute | solution.py:291
  54.7 1.6 %collective-permute-done.7 = f32[8,256]{1,0:T(8,128)S(1)} collective-permute-done((f32[8,256]{1,0:T(8,128)S(1)}, f32[8,256]{1,0:T(8,128)S(1)}, u32[]{:S(2)}, u32[]{:S(2)}) %collective-permute-start.7) | collective-permute-done | bytes 8224 | tf_op jit(solution)/shard_map/ppermute | solution.py:291
  56.3 3.9 %collective-permute-start.8 = (f32[8,256]{1,0:T(8,128)S(1)}, f32[8,256]{1,0:T(8,128)S(1)}, u32[]{:S(2)}, u32[]{:S(2)}) collective-permute-start(f32[8,256]{1,0:T(8,128)S(1)} %add.63), channel_id=1, source_target_pairs={{0,24},{1,25},{2,26},{3,27},{4,28},{5,29},{6,30},{7,31},{8,16},{9,... | collective-permute-start | bytes 24584 | tf_op jit(solution)/shard_map/ppermute | solution.py:291
  60.2 1.6 %collective-permute-done.8 = f32[8,256]{1,0:T(8,128)S(1)} collective-permute-done((f32[8,256]{1,0:T(8,128)S(1)}, f32[8,256]{1,0:T(8,128)S(1)}, u32[]{:S(2)}, u32[]{:S(2)}) %collective-permute-start.8) | collective-permute-done | bytes 8224 | tf_op jit(solution)/shard_map/ppermute | solution.py:291
  61.9 5.4 %shard_map.101 = (f32[512,512]{1,0:T(8,128)S(1)}, f32[528,512]{1,0:T(8,128)S(1)}) custom-call(f32[1344,128]{1,0:T(8,128)} %collective-permute-done.4.packed, f32[512,512]{1,0:T(8,128)} %shard_map.100.lower), custom_call_target="tpu_custom_call" | custom-call | flops 4831838208 | bytes 1024 | tf_op jit(solution)/shard_map/pallas_call | solution.py:259
  67.3 4.4 %shard_map.102 = (f32[1344,128]{1,0:T(8,128)}, f32[512,512]{1,0:T(8,128)S(1)}, f32[16,512]{1,0:T(8,128)S(1)}) custom-call(f32[1344,128]{1,0:T(8,128)} %collective-permute-done.2.packed_above, f32[512,512]{1,0:T(8,128)} %collective-permute-done.3.passed, f32[512,512]{1,0:T(8,128)S(1)} %copy-done.5, f32[16,512]{1,0:T(8,128)S(1)} %get-tuple-element.31.thin, ...), custom_call_target="tpu_custom_call" | custom-call | flops 1610612736 | bytes 1024 | tf_op jit(solution)/shard_map/pallas_call | solution.py:259
  71.7 7.2 %collective-permute-start.10 = (f32[1344,128]{1,0:T(8,128)}, f32[1344,128]{1,0:T(8,128)S(1)}, u32[]{:S(2)}, u32[]{:S(2)}) collective-permute-start(f32[1344,128]{1,0:T(8,128)} %get-tuple-element.37), channel_id=1, source_target_pairs={{0,17},{6,23},{9,24},{15,30}} | collective-permute-start | bytes 2064392 | tf_op jit(solution)/shard_map/ppermute | solution.py:291
  78.9 2.1 %shard_map.104.inverse = f32[512,512]{1,0:T(8,128)S(1)} custom-call(f32[512,512]{1,0:T(8,128)S(1)} %get-tuple-element.41.block), custom_call_target="tpu_custom_call" | custom-call | flops 3221225472 | bytes 1024 | tf_op jit(solution)/shard_map/pallas_call | solution.py:259
  81.0 0.0 copy-start.10
  81.0 3.7 %shard_map.105 = (f32[512,512]{1,0:T(8,128)S(1)}, f32[1344,128]{1,0:T(8,128)}) custom-call(f32[512,512]{1,0:T(8,128)S(1)} %get-tuple-element.40.through, f32[512,512]{1,0:T(8,128)S(1)} %collective-permute-done.11.passed, f32[512,512]{1,0:T(8,128)S(1)} %shard_map.104.inverse, f32[16,512]{1,0:T(8,128)S(1)} %get-tuple-element.42.thin), custom_call_target="tpu_custom_call" | custom-call | flops 120795952 | bytes 1024 | tf_op jit(solution)/shard_map/pallas_call | solution.py:259
  84.8 1.0 copy-done.1
  85.8 1.5 %collective-permute-start.12 = (f32[1344,128]{1,0:T(8,128)}, f32[1344,128]{1,0:T(8,128)S(1)}, u32[]{:S(2)}, u32[]{:S(2)}) collective-permute-start(f32[1344,128]{1,0:T(8,128)} %get-tuple-element.46), channel_id=1, source_target_pairs={{17,0},{23,6},{24,9},{30,15}} | collective-permute-start | bytes 2064392 | tf_op jit(solution)/shard_map/ppermute | solution.py:291
  87.3 0.6 dynamic_slice.9
  88.5 2.1 %shard_map.103 = (f32[512,512]{1,0:T(8,128)S(1)}, f32[16,512]{1,0:T(8,128)S(1)}) custom-call(f32[1344,128]{1,0:T(8,128)S(1)} %collective-permute-done.10.packed), custom_call_target="tpu_custom_call" | custom-call | flops 161061280 | bytes 1024 | tf_op jit(solution)/shard_map/pallas_call | solution.py:259
  90.7 1.2 copy-done.2
  91.9 1.9 %shard_map.106 = (f32[512,512]{1,0:T(8,128)S(1)}, f32[16,512]{1,0:T(8,128)S(1)}) custom-call(f32[512,512]{1,0:T(8,128)S(1)} %get-tuple-element.38.inverse, f32[16,512]{1,0:T(8,128)S(1)} %get-tuple-element.39.thin_passed, f32[512,512]{1,0:T(8,128)S(1)} %copy-done.2, f32[512,512]{1,0:T(8,128)S(1)} %get-tuple-element.41.block, f32[16,512]{1,0:T(8,128)S(1)} %get-tuple-element.42.thin), custom_call_target="tpu_custom_call" | custom-call | flops 80530640 | bytes 1024 | tf_op jit(solution)/shard_map/pallas_call | solution.py:259
  93.8 0.0 copy-start.3
  93.8 5.9 %collective-permute-done.12.above = f32[1344,128]{1,0:T(8,128)S(1)} collective-permute-done((f32[1344,128]{1,0:T(8,128)}, f32[1344,128]{1,0:T(8,128)S(1)}, u32[]{:S(2)}, u32[]{:S(2)}) %collective-permute-start.12) | collective-permute-done | bytes 688160 | tf_op jit(solution)/shard_map/ppermute | solution.py:291
  99.7 1.9 %shard_map.107 = f32[16,512]{1,0:T(8,128)S(1)} custom-call(f32[512,512]{1,0:T(8,128)S(1)} %get-tuple-element.44.block, f32[16,512]{1,0:T(8,128)S(1)} %get-tuple-element.45.thin, f32[1344,128]{1,0:T(8,128)S(1)} %collective-permute-done.12.above), custom_call_target="tpu_custom_call" | custom-call | flops 40265320 | bytes 1024 | tf_op jit(solution)/shard_map/pallas_call | solution.py:259
  101.6 1.3 %collective-permute-start.13 = (f32[16,512]{1,0:T(8,128)S(1)}, f32[16,512]{1,0:T(8,128)S(1)}, u32[]{:S(2)}, u32[]{:S(2)}) collective-permute-start(f32[16,512]{1,0:T(8,128)S(1)} %shard_map.107), channel_id=1, source_target_pairs={{0,1},{6,7},{9,10},{15,12},{17,18},{23,20},{24,25},{30,31}} | collective-permute-start | bytes 98312 | tf_op jit(solution)/shard_map/ppermute | solution.py:291
  102.9 1.3 %collective-permute-start.14 = (f32[16,512]{1,0:T(8,128)S(1)}, f32[16,512]{1,0:T(8,128)S(1)}, u32[]{:S(2)}, u32[]{:S(2)}) collective-permute-start(f32[16,512]{1,0:T(8,128)S(1)} %shard_map.107), channel_id=1, source_target_pairs={{0,2},{6,4},{9,11},{15,13},{17,19},{23,21},{24,26},{30,28}} | collective-permute-start | bytes 98312 | tf_op jit(solution)/shard_map/ppermute | solution.py:291
  104.2 1.3 %collective-permute-start.15 = (f32[16,512]{1,0:T(8,128)S(1)}, f32[16,512]{1,0:T(8,128)S(1)}, u32[]{:S(2)}, u32[]{:S(2)}) collective-permute-start(f32[16,512]{1,0:T(8,128)S(1)} %shard_map.107), channel_id=1, source_target_pairs={{0,3},{6,5},{9,8},{15,14},{17,16},{23,22},{24,27},{30,29}} | collective-permute-start | bytes 98312 | tf_op jit(solution)/shard_map/ppermute | solution.py:291
  105.5 0.3 collective-permute-done.14.c
  105.7 1.3 %collective-permute-done.15.d = f32[16,512]{1,0:T(8,128)S(1)} collective-permute-done((f32[16,512]{1,0:T(8,128)S(1)}, f32[16,512]{1,0:T(8,128)S(1)}, u32[]{:S(2)}, u32[]{:S(2)}) %collective-permute-start.15) | collective-permute-done | bytes 32800 | tf_op jit(solution)/shard_map/ppermute | solution.py:291
  107.0 0.1 shard_map.108
  107.2 0.1 collective-permute-start.16
  107.3 1.2 collective-permute-done.16
  108.5 0.0 collective-permute-start.17
  108.5 0.6 collective-permute-start.18
  109.0 2.9 %collective-permute-start.19 = (f32[24,256]{1,0:T(8,128)S(1)}, f32[24,256]{1,0:T(8,128)S(1)}, u32[]{:S(2)}, u32[]{:S(2)}) collective-permute-start(f32[24,256]{1,0:T(8,128)S(1)} %add.68.refs_0_), channel_id=1, source_target_pairs={{0,24},{1,25},{2,26},{3,27},{4,28},{5,29},{6,30},{7,31},{8,16},{9,... | collective-permute-start | bytes 73736 | tf_op jit(solution)/shard_map/ppermute | solution.py:291
  111.9 0.3 collective-permute-done.17.refs_1_
  112.3 0.1 collective-permute-done.18.refs_2_
  112.4 1.4 %collective-permute-done.19.refs_3_ = f32[24,256]{1,0:T(8,128)S(1)} collective-permute-done((f32[24,256]{1,0:T(8,128)S(1)}, f32[24,256]{1,0:T(8,128)S(1)}, u32[]{:S(2)}, u32[]{:S(2)}) %collective-permute-start.19) | collective-permute-done | bytes 24608 | tf_op jit(solution)/shard_map/ppermute | solution.py:291
  113.8 0.2 shard_map.109
  113.9 0.0 collective-permute-start.20
  114.0 4.7 %collective-permute-start.21 = (f32[16,128]{1,0:T(8,128)S(1)}, f32[16,128]{1,0:T(8,128)S(1)}, u32[]{:S(2)}, u32[]{:S(2)}) collective-permute-start(f32[16,128]{1,0:T(8,128)S(1)} %get-tuple-element.52), channel_id=1, source_target_pairs={{0,2},{1,3},{2,0},{3,1},{4,6},{5,7},{6,4},{7,5},{8,10},{9,11},{10,... | collective-permute-start | bytes 24584 | tf_op jit(solution)/shard_map/ppermute | solution.py:291
  118.6 0.2 collective-permute-start.22
  118.8 0.9 collective-permute-done.20
  119.7 0.6 collective-permute-done.21
  120.2 2.0 %collective-permute-done.22 = f32[16,128]{1,0:T(8,128)S(1)} collective-permute-done((f32[16,128]{1,0:T(8,128)S(1)}, f32[16,128]{1,0:T(8,128)S(1)}, u32[]{:S(2)}, u32[]{:S(2)}) %collective-permute-start.22) | collective-permute-done | bytes 8224 | tf_op jit(solution)/shard_map/ppermute | solution.py:291
  122.3 0.6 subtract_bitcast_fusion
  (29 shorter events, 0.1 us)
Async XLA Ops:
  0.6 2.9 %copy-start = (f32[1,512,512]{2,1,0:T(8,128)S(1)}, f32[1,512,512]{2,1,0:T(8,128)}, u32[]{:S(2)}) copy-start(f32[1,512,512]{2,1,0:T(8,128)} %param.9) | copy-start | bytes 3145732
  0.6 2.9 %copy-start.6 = (f32[1,16,512]{2,1,0:T(8,128)S(1)}, f32[1,16,512]{2,1,0:T(8,128)}, u32[]{:S(2)}) copy-start(f32[1,16,512]{2,1,0:T(8,128)} %param.10) | copy-start | bytes 98308
  2.8 8.8 %collective-permute-start = (f32[1344,128]{1,0:T(8,128)}, f32[1344,128]{1,0:T(8,128)S(1)}, u32[]{:S(2)}, u32[]{:S(2)}) collective-permute-start(f32[1344,128]{1,0:T(8,128)} %shard_map.95), channel_id=1, source_target_pairs={{2,6},{3,7},{4,8},{5,9},{10,14},{11,15},{12,16},{13,17},{18,22},{1... | collective-permute-start | bytes 2064392 | tf_op jit(solution)/shard_map/ppermute | solution.py:291
  8.7 8.1 %collective-permute-start.1 = (f32[1344,128]{1,0:T(8,128)S(1)}, f32[1344,128]{1,0:T(8,128)S(1)}, u32[]{:S(2)}, u32[]{:S(2)}) collective-permute-start(f32[1344,128]{1,0:T(8,128)S(1)} %shard_map.97), channel_id=1, source_target_pairs={{4,0},{5,1},{10,6},{11,7},{12,8},{13,9},{18,14},{19,15},{20,16},{2... | collective-permute-start | bytes 2064392 | tf_op jit(solution)/shard_map/ppermute | solution.py:291
  10.0 22.2 %collective-permute-start.9 = (f32[512,512]{1,0:T(8,128)}, f32[512,512]{1,0:T(8,128)}, u32[]{:S(2)}, u32[]{:S(2)}) collective-permute-start(f32[512,512]{1,0:T(8,128)} %bitcast.3.lower), channel_id=1, source_target_pairs={{5,9},{11,15},{12,16},{13,17},{18,22},{19,23},{20,24},{26,30}} | collective-permute-start | bytes 3145736 | tf_op jit(solution)/shard_map/ppermute | solution.py:291
  16.8 3.9 %copy-start.9 = (s32[16]{0:T(128)S(1)}, s32[16]{0:T(128)}, u32[]{:S(2)}) copy-start(s32[16]{0:T(128)} %param.13) | copy-start | bytes 196
  17.9 6.9 %copy-start.4 = (f32[512,512]{1,0:T(8,128)}, f32[512,512]{1,0:T(8,128)S(1)}, u32[]{:S(2)}) copy-start(f32[512,512]{1,0:T(8,128)S(1)} %get-tuple-element.30.block) | copy-start | bytes 3145732
  17.9 44.0 %collective-permute-start.4 = (f32[1344,128]{1,0:T(8,128)}, f32[1344,128]{1,0:T(8,128)}, u32[]{:S(2)}, u32[]{:S(2)}) collective-permute-start(f32[1344,128]{1,0:T(8,128)} %get-tuple-element.34), channel_id=1, source_target_pairs={{1,9},{7,15},{9,17},{15,23},{16,24},{22,30}} | collective-permute-start | bytes 2064392 | tf_op jit(solution)/shard_map/ppermute | solution.py:291
  19.4 47.9 %collective-permute-start.3 = (f32[512,512]{1,0:T(8,128)}, f32[512,512]{1,0:T(8,128)}, u32[]{:S(2)}, u32[]{:S(2)}) collective-permute-start(f32[512,512]{1,0:T(8,128)} %bitcast.3.lower), channel_id=1, source_target_pairs={{4,0},{10,6},{13,9},{19,15},{21,17},{27,23},{28,24}} | collective-permute-start | bytes 3145736 | tf_op jit(solution)/shard_map/ppermute | solution.py:291
  20.9 5.2 %copy-start.7 = (bf16[1024,256]{1,0:T(8,128)(2,1)S(1)}, bf16[1024,256]{1,0:T(8,128)(2,1)}, u32[]{:S(2)}) copy-start(bf16[1024,256]{1,0:T(8,128)(2,1)} %param.14) | copy-start | bytes 1572868
  20.9 5.3 %copy-start.8 = (s32[1024]{0:T(1024)S(1)}, s32[1024]{0:T(1024)}, u32[]{:S(2)}) copy-start(s32[1024]{0:T(1024)} %param.12) | copy-start | bytes 12292
  24.8 42.5 %collective-permute-start.2 = (f32[1344,128]{1,0:T(8,128)S(1)}, f32[1344,128]{1,0:T(8,128)}, u32[]{:S(2)}, u32[]{:S(2)}) collective-permute-start(f32[1344,128]{1,0:T(8,128)S(1)} %shard_map.99.after), channel_id=1, source_target_pairs={{8,0},{14,6},{17,9},{23,15},{25,17},{31,23}} | collective-permute-start | bytes 2064392 | tf_op jit(solution)/shard_map/ppermute | solution.py:291
  26.7 9.6 %collective-permute-start.5 = (f32[8,256]{1,0:T(8,128)S(1)}, f32[8,256]{1,0:T(8,128)S(1)}, u32[]{:S(2)}, u32[]{:S(2)}) collective-permute-start(f32[8,256]{1,0:T(8,128)S(1)} %fusion), channel_id=1, source_target_pairs={{0,4},{1,5},{2,6},{3,7},{4,0},{5,1},{6,2},{7,3},{8,12},{9,13},{10,... | collective-permute-start | bytes 24584 | tf_op jit(solution)/shard_map/ppermute | solution.py:291
  35.4 45.6 %collective-permute-start.11 = (f32[512,512]{1,0:T(8,128)}, f32[512,512]{1,0:T(8,128)S(1)}, u32[]{:S(2)}, u32[]{:S(2)}) collective-permute-start(f32[512,512]{1,0:T(8,128)} %shard_map.100.lower), channel_id=1, source_target_pairs={{9,17},{15,23},{16,24},{22,30}} | collective-permute-start | bytes 3145736 | tf_op jit(solution)/shard_map/ppermute | solution.py:291
  36.4 5.7 %collective-permute-start.6 = (f32[8,256]{1,0:T(8,128)S(1)}, f32[8,256]{1,0:T(8,128)S(1)}, u32[]{:S(2)}, u32[]{:S(2)}) collective-permute-start(f32[8,256]{1,0:T(8,128)S(1)} %add.63), channel_id=1, source_target_pairs={{0,8},{1,9},{2,10},{3,11},{4,12},{5,13},{6,14},{7,15},{8,0},{9,1},... | collective-permute-start | bytes 24584 | tf_op jit(solution)/shard_map/ppermute | solution.py:291
  42.1 14.2 %collective-permute-start.7 = (f32[8,256]{1,0:T(8,128)S(1)}, f32[8,256]{1,0:T(8,128)S(1)}, u32[]{:S(2)}, u32[]{:S(2)}) collective-permute-start(f32[8,256]{1,0:T(8,128)S(1)} %add.63), channel_id=1, source_target_pairs={{0,16},{1,17},{2,18},{3,19},{4,20},{5,21},{6,22},{7,23},{8,24},{9,... | collective-permute-start | bytes 24584 | tf_op jit(solution)/shard_map/ppermute | solution.py:291
  56.3 5.6 %collective-permute-start.8 = (f32[8,256]{1,0:T(8,128)S(1)}, f32[8,256]{1,0:T(8,128)S(1)}, u32[]{:S(2)}, u32[]{:S(2)}) collective-permute-start(f32[8,256]{1,0:T(8,128)S(1)} %add.63), channel_id=1, source_target_pairs={{0,24},{1,25},{2,26},{3,27},{4,28},{5,29},{6,30},{7,31},{8,16},{9,... | collective-permute-start | bytes 24584 | tf_op jit(solution)/shard_map/ppermute | solution.py:291
  61.9 5.5 %copy-start.5 = (f32[512,512]{1,0:T(8,128)S(1)}, f32[512,512]{1,0:T(8,128)}, u32[]{:S(2)}) copy-start(f32[512,512]{1,0:T(8,128)} %copy-done.4) | copy-start | bytes 3145732
  71.7 16.8 %collective-permute-start.10 = (f32[1344,128]{1,0:T(8,128)}, f32[1344,128]{1,0:T(8,128)S(1)}, u32[]{:S(2)}, u32[]{:S(2)}) collective-permute-start(f32[1344,128]{1,0:T(8,128)} %get-tuple-element.37), channel_id=1, source_target_pairs={{0,17},{6,23},{9,24},{15,30}} | collective-permute-start | bytes 2064392 | tf_op jit(solution)/shard_map/ppermute | solution.py:291
  81.0 6.3 %copy-start.10 = (s32[8]{0:T(128)S(1)}, s32[8]{0:T(128)}, u32[]{:S(2)}) copy-start(s32[8]{0:T(128)} %constant.38.clone) | copy-start | bytes 100
  84.8 1.0 copy-start.1
  85.8 13.9 %collective-permute-start.12 = (f32[1344,128]{1,0:T(8,128)}, f32[1344,128]{1,0:T(8,128)S(1)}, u32[]{:S(2)}, u32[]{:S(2)}) collective-permute-start(f32[1344,128]{1,0:T(8,128)} %get-tuple-element.46), channel_id=1, source_target_pairs={{17,0},{23,6},{24,9},{30,15}} | collective-permute-start | bytes 2064392 | tf_op jit(solution)/shard_map/ppermute | solution.py:291
  90.7 1.2 copy-start.2
  93.8 13.3 %copy-start.3 = (bf16[1,512,256]{2,1,0:T(8,128)(2,1)S(1)}, bf16[1,512,256]{2,1,0:T(8,128)(2,1)}, u32[]{:S(2)}) copy-start(bf16[1,512,256]{2,1,0:T(8,128)(2,1)} %param.11) | copy-start | bytes 786436
  101.6 3.9 %collective-permute-start.13 = (f32[16,512]{1,0:T(8,128)S(1)}, f32[16,512]{1,0:T(8,128)S(1)}, u32[]{:S(2)}, u32[]{:S(2)}) collective-permute-start(f32[16,512]{1,0:T(8,128)S(1)} %shard_map.107), channel_id=1, source_target_pairs={{0,1},{6,7},{9,10},{15,12},{17,18},{23,20},{24,25},{30,31}} | collective-permute-start | bytes 98312 | tf_op jit(solution)/shard_map/ppermute | solution.py:291
  102.9 2.9 %collective-permute-start.14 = (f32[16,512]{1,0:T(8,128)S(1)}, f32[16,512]{1,0:T(8,128)S(1)}, u32[]{:S(2)}, u32[]{:S(2)}) collective-permute-start(f32[16,512]{1,0:T(8,128)S(1)} %shard_map.107), channel_id=1, source_target_pairs={{0,2},{6,4},{9,11},{15,13},{17,19},{23,21},{24,26},{30,28}} | collective-permute-start | bytes 98312 | tf_op jit(solution)/shard_map/ppermute | solution.py:291
  104.2 2.9 %collective-permute-start.15 = (f32[16,512]{1,0:T(8,128)S(1)}, f32[16,512]{1,0:T(8,128)S(1)}, u32[]{:S(2)}, u32[]{:S(2)}) collective-permute-start(f32[16,512]{1,0:T(8,128)S(1)} %shard_map.107), channel_id=1, source_target_pairs={{0,3},{6,5},{9,8},{15,14},{17,16},{23,22},{24,27},{30,29}} | collective-permute-start | bytes 98312 | tf_op jit(solution)/shard_map/ppermute | solution.py:291
  107.2 1.3 %collective-permute-start.16 = (f32[24,256]{1,0:T(8,128)S(1)}, f32[24,256]{1,0:T(8,128)S(1)}, u32[]{:S(2)}, u32[]{:S(2)}) collective-permute-start(f32[24,256]{1,0:T(8,128)S(1)} %get-tuple-element.49), channel_id=1, source_target_pairs={{0,4},{1,5},{2,6},{3,7},{4,0},{5,1},{6,2},{7,3},{8,12},{9,13},{10,... | collective-permute-start | bytes 73736 | tf_op jit(solution)/shard_map/ppermute | solution.py:291
  108.5 3.8 %collective-permute-start.17 = (f32[24,256]{1,0:T(8,128)S(1)}, f32[24,256]{1,0:T(8,128)S(1)}, u32[]{:S(2)}, u32[]{:S(2)}) collective-permute-start(f32[24,256]{1,0:T(8,128)S(1)} %add.68.refs_0_), channel_id=1, source_target_pairs={{0,8},{1,9},{2,10},{3,11},{4,12},{5,13},{6,14},{7,15},{8,0},{9,1},... | collective-permute-start | bytes 73736 | tf_op jit(solution)/shard_map/ppermute | solution.py:291
  108.5 3.9 %collective-permute-start.18 = (f32[24,256]{1,0:T(8,128)S(1)}, f32[24,256]{1,0:T(8,128)S(1)}, u32[]{:S(2)}, u32[]{:S(2)}) collective-permute-start(f32[24,256]{1,0:T(8,128)S(1)} %add.68.refs_0_), channel_id=1, source_target_pairs={{0,16},{1,17},{2,18},{3,19},{4,20},{5,21},{6,22},{7,23},{8,24},{9,... | collective-permute-start | bytes 73736 | tf_op jit(solution)/shard_map/ppermute | solution.py:291
  109.0 4.7 %collective-permute-start.19 = (f32[24,256]{1,0:T(8,128)S(1)}, f32[24,256]{1,0:T(8,128)S(1)}, u32[]{:S(2)}, u32[]{:S(2)}) collective-permute-start(f32[24,256]{1,0:T(8,128)S(1)} %add.68.refs_0_), channel_id=1, source_target_pairs={{0,24},{1,25},{2,26},{3,27},{4,28},{5,29},{6,30},{7,31},{8,16},{9,... | collective-permute-start | bytes 73736 | tf_op jit(solution)/shard_map/ppermute | solution.py:291
  113.9 5.8 %collective-permute-start.20 = (f32[16,128]{1,0:T(8,128)S(1)}, f32[16,128]{1,0:T(8,128)S(1)}, u32[]{:S(2)}, u32[]{:S(2)}) collective-permute-start(f32[16,128]{1,0:T(8,128)S(1)} %get-tuple-element.51), channel_id=1, source_target_pairs={{0,1},{1,2},{2,3},{3,0},{4,5},{5,6},{6,7},{7,4},{8,9},{9,10},{10,1... | collective-permute-start | bytes 24584 | tf_op jit(solution)/shard_map/ppermute | solution.py:291
  114.0 6.3 %collective-permute-start.21 = (f32[16,128]{1,0:T(8,128)S(1)}, f32[16,128]{1,0:T(8,128)S(1)}, u32[]{:S(2)}, u32[]{:S(2)}) collective-permute-start(f32[16,128]{1,0:T(8,128)S(1)} %get-tuple-element.52), channel_id=1, source_target_pairs={{0,2},{1,3},{2,0},{3,1},{4,6},{5,7},{6,4},{7,5},{8,10},{9,11},{10,... | collective-permute-start | bytes 24584 | tf_op jit(solution)/shard_map/ppermute | solution.py:291
  118.6 3.7 %collective-permute-start.22 = (f32[16,128]{1,0:T(8,128)S(1)}, f32[16,128]{1,0:T(8,128)S(1)}, u32[]{:S(2)}, u32[]{:S(2)}) collective-permute-start(f32[16,128]{1,0:T(8,128)S(1)} %get-tuple-element.53), channel_id=1, source_target_pairs={{0,3},{1,0},{2,1},{3,2},{4,7},{5,4},{6,5},{7,6},{8,11},{9,8},{10,9... | collective-permute-start | bytes 24584 | tf_op jit(solution)/shard_map/ppermute | solution.py:291

commit v3 on v2

--- a/solution.py
+++ b/solution.py
@@ -133,19 +133,40 @@
         packed[start : start + rows, :] = value
 
 
-def own_kernel(block, thin, lower, packed, stack, out):
+def first_own_kernel(block, thin, lower_hbm, packed, stack, out, lower, sem):
+    copy = pltpu.make_async_copy(lower_hbm, lower, sem)
+    copy.start()
+    own_kernel(block, thin, lower, packed, stack, out, copy)
+
+
+def own_kernel(block, thin, lower, packed, stack, out, copy=None):
     size = block.shape[0]
     inverse = inverse_of(block[...])
+    if copy is not None:
+        copy.wait()
     stack[0:size, :] = lower[...].T
     stack[size:, :] = thin[...]
     _, out[...] = schur(stack[...], inverse, lower[...], dot)
     pack(packed, out, out.at[size:, :])
 
 
-def receive_kernel(packed, lower, through, full, stack, whole):
+def bracket_kernel(block, thin, lower, packed, done, stack, out):
+    own_kernel(block, thin, lower, packed, stack, out)
+    done[...] = jnp.zeros_like(done)
+
+
+def first_receive_kernel(packed, lower_hbm, through, full, stack, whole, lower, sem):
+    copy = pltpu.make_async_copy(lower_hbm, lower, sem)
+    copy.start()
+    receive_kernel(packed, lower, through, full, stack, whole, copy)
+
+
+def receive_kernel(packed, lower, through, full, stack, whole, copy=None):
     size = lower.shape[0]
     unpack(packed, whole, stack.at[size:, :])
     inverse = inverse_of(whole[...])
+    if copy is not None:
+        copy.wait()
     stack[0:size, :] = lower[...]
     half, full[...] = schur(stack[...], inverse, lower[...], dot_t)
     through[...] = half[0:size, :]
@@ -167,36 +188,45 @@
     unpack(packed, block_out, thin_out)
 
 
-def whole_inverse_kernel(block, inverse):
-    inverse[...] = inverse_of(block[...])
-
-
-def invert_kernel(packed, inverse, thin, block):
-    unpack(packed, block, thin)
-    inverse[...] = inverse_of(block[...])
+def whole_inverse_kernel(needed, block, inverse):
+    @pl.when(needed())
+    def _():
+        inverse[...] = inverse_of(block[...])
 
 
 def lower_kernel(through, passed, after, lower):
     lower[...] = -times(split(through[...]), split(passed[...]))
 
 
-def last_lower_kernel(through, passed, inverse, thin, lower, packed, stack, out):
+def last_lower_kernel(needed, through, passed, inverse, thin, lower, packed, stack, out):
     size = inverse.shape[0]
-    value = -times(split(through[...]), split(passed[...]))
-    lower[...] = value
-    stack[0:size, :] = value.T
-    stack[size:, :] = thin[...]
-    _, out[...] = schur(stack[...], inverse[...], value, dot)
-    pack(packed, out, out.at[size:, :])
-
-
-def last_receive_kernel(inverse, thin_passed, lower, block, thin, block_out, thin_out, stack):
-    size = block.shape[0]
-    stack[0:size, :] = lower[...]
-    stack[size:, :] = thin_passed[...]
-    _, full = schur(stack[...], inverse[...], lower[...], dot_t)
-    block_out[...] = block[...] - full[0:size, :]
-    thin_out[...] = thin[...] - full[size:, :]
+
+    @pl.when(needed())
+    def _():
+        value = -times(split(through[...]), split(passed[...]))
+        lower[...] = value
+        stack[0:size, :] = value.T
+        stack[size:, :] = thin[...]
+        _, out[...] = schur(stack[...], inverse[...], value, dot)
+        pack(packed, out, out.at[size:, :])
+
+
+def last_receive_kernel(needed, packed, lower, block, thin, block_out, thin_out, stack, whole):
+    size = block.shape[0]
+
+    @pl.when(needed())
+    def _():
+        unpack(packed, whole, stack.at[size:, :])
+        inverse = inverse_of(whole[...])
+        stack[0:size, :] = lower[...]
+        _, full = schur(stack[...], inverse, lower[...], dot_t)
+        block_out[...] = block[...] - full[0:size, :]
+        thin_out[...] = thin[...] - full[size:, :]
+
+    @pl.when(jnp.logical_not(needed()))
+    def _():
+        block_out[...] = block[...]
+        thin_out[...] = thin[...]
 
 
 def solve_kernel(block, thin, above, solution, whole, own):
@@ -216,28 +246,49 @@
     solution[...] = now
 
 
-def modal_kernel(a, b, c, d, modes, shares, whole, payload):
-    value = a[...] + b[...] + c[...] + d[...]
+def shares_kernel(regime, joints, participation, shares):
+    sections, count = shares.shape[0], joints.shape[1]
+    bucket = lax.broadcasted_iota(jnp.int32, (1, count), 1) // BUCKET
+    rate = jnp.zeros((1, count), f32)
+    for b in range(count // BUCKET):
+        value = jnp.float32(0.0)
+        for index, known in enumerate(RATES):
+            value = jnp.where(regime[b] == index, jnp.float32(known), value)
+        rate = jnp.where(bucket == b, value, rate)
+    section = lax.broadcasted_iota(jnp.int32, (sections, count), 0)
+    weights = jnp.where(section == joints[...], rate, 0.0)
+    squares = participation[...].astype(f32)
+    shares[...] = times(split(weights), split(squares * squares))
+
+
+def modal_kernel(home, a, b, c, d, modes, shares, whole, payload):
+    position, plane = lax.axis_index("sec"), lax.axis_index("mode")
+    own = jnp.where(home(position) == plane, a[...], 0.0)
+    value = own + b[...] + c[...] + d[...]
     whole[...] = value
     amplitude = jnp.sqrt(jnp.sum(value * value, keepdims=True) / value.size + 1e-06)
-    rows = value.shape[0]
-    payload[...] = jnp.zeros_like(payload)
+    rows, sections = value.shape[0], shares.shape[0]
     payload[0:rows, :] = dot(value.astype(bf16), modes[...])
-    payload[rows : rows + 1, :] = shares[...] * (amplitude / (1.0 + amplitude))
-
-
-def back_kernel_of(count, place, *refs):
+    payload[rows : rows + sections, :] = shares[...]
+    mine = lax.broadcasted_iota(jnp.int32, shares.shape, 0) == position
+    payload[rows + sections :, :] = jnp.where(mine, amplitude / (1.0 + amplitude), 0.0)
+
+
+def back_kernel_of(count, *refs):
+    plane = lax.axis_index("mode")
     parts, modes, pieces, scratch = refs[:count], refs[count], refs[count + 1 : -1], refs[-1]
     total = parts[0][...]
     for part in parts[1:]:
         total = total + part[...]
     rows = scratch.shape[0]
-    damping = total[rows : rows + 1, :]
+    sections = (total.shape[0] - rows) // 2
+    parts = total[rows : rows + sections, :] * total[rows + sections :, :]
+    damping = jnp.sum(parts, axis=0, keepdims=True)
     removed = (total[0:rows, :] * (damping / (1.0 + damping))).astype(bf16)
     scratch[...] = dot_t(removed, modes[...])
     width = pieces[0].shape[1]
     for k, piece in enumerate(pieces):
-        start = lax.rem(place[0] + k, len(pieces)) * width
+        start = lax.rem(plane + k, len(pieces)) * width
         piece[...] = scratch[:, pl.ds(pl.multiple_of(start, width), width)]
 
 
@@ -245,32 +296,32 @@
     cells = len(upper(block.shape[0])) + block.shape[0] // TILE
     return pl.pallas_call(
         pack_kernel,
-        out_shape=jax.ShapeDtypeStruct(packed, f32),
+        out_shape=pltpu.VMEM(packed, f32),
         in_specs=[pl.BlockSpec(memory_space=pl.ANY)] * 2,
         out_specs=pl.BlockSpec(memory_space=pltpu.VMEM),
         scratch_shapes=[pltpu.SemaphoreType.DMA((cells,))],
     )(block, thin)
 
 
-def call(kernel, outs, scratch, args, flops, smem=0, after=0):
+def call(kernel, outs, scratch, args, flops, smem=0, hbm=0):
     vmem, scalar = pl.BlockSpec(memory_space=pltpu.VMEM), pl.BlockSpec(memory_space=pltpu.SMEM)
+    moved = sum(a.size * a.dtype.itemsize for a in args) + sum(4 * o[0] * o[1] for o in outs)
     single = len(outs) == 1
     shapes = [jax.ShapeDtypeStruct(o, f32) for o in outs]
     return pl.pallas_call(
         kernel,
         out_shape=shapes[0] if single else tuple(shapes),
         in_specs=[scalar] * smem
-        + [vmem] * (len(args) - smem - after)
-        + [pl.BlockSpec(memory_space=pl.ANY)] * after,
+        + [vmem] * (len(args) - smem - hbm)
+        + [pl.BlockSpec(memory_space=pl.ANY)] * hbm,
         out_specs=vmem if single else tuple([vmem] * len(outs)),
-        scratch_shapes=[pltpu.VMEM(s, f32) for s in scratch],
-        compiler_params=pltpu.CompilerParams(vmem_limit_bytes=20 << 20),
-        cost_estimate=pl.CostEstimate(flops=int(flops), transcendentals=0, bytes_accessed=1024),
+        scratch_shapes=[pltpu.VMEM(s, f32) for s in scratch] + [pltpu.SemaphoreType.DMA] * hbm,
+        compiler_params=pltpu.CompilerParams(vmem_limit_bytes=14 << 20),
+        cost_estimate=pl.CostEstimate(flops=int(flops), transcendentals=0, bytes_accessed=moved),
     )(*args)
 
 
 def per_device(coupling, stiffness, loads, modes, joint_section, regime, participation):
-    position, plane = lax.axis_index("sec"), lax.axis_index("mode")
     sections, groups = lax.axis_size("sec"), lax.axis_size("mode")
     assert groups == 4 and LEVELS == 3
     size, columns = stiffness.shape[1], loads.shape[1]
@@ -278,7 +329,7 @@
     cells = len(upper(size))
     packed = (TILE * cells + columns * (size // TILE), TILE)
     square, stacked, thin_shape = (size, size), (size + columns, size), (columns, size)
-    product = 0.05 * 6 * size**3
+    product = 0.1 * 6 * size**3
     long = 1.0 * 6 * size**3
 
     def sent_to(value, where):
@@ -298,14 +349,13 @@
 
     block, thin, lower = stiffness[0], loads[0], coupling[0]
 
-    matches = (jnp.arange(sections, dtype=jnp.int32)[:, None] == joint_section[None, :]).astype(f32)
-    joint_regime = jnp.broadcast_to(regime[:, None], (regime.shape[0], BUCKET)).reshape(-1)
-    joint_rate = jnp.zeros(joint_regime.shape, f32)
-    for value_index, rate_value in enumerate(RATES):
-        joint_rate = joint_rate + (joint_regime == value_index).astype(f32) * rate_value
-    weights = participation.astype(f32)
-    shares = jnp.dot(
-        matches * joint_rate[None, :], weights * weights, precision=lax.Precision.HIGHEST
+    shares = call(
+        shares_kernel,
+        [(sections, participation.shape[1])],
+        [],
+        (regime, joint_section[None, :], participation),
+        product // 32,
+        smem=1,
     )
     bits = sections.bit_length() - 1
     rounds = [[1]] + [[1 << b, 2 << b, 3 << b] if b + 1 < bits else [1 << b] for b in range(1, bits, 2)]
@@ -319,9 +369,6 @@
             parts = [value] + [sent_to(value, lambda s, m, k=k: (s ^ k, m)) for k in steps]
         return parts
 
-    shares = sum(summed_over_sections(shares))
-    shares = lax.dynamic_slice_in_dim(shares, position, 1, 0)
-
     packed_down = packed_from_hbm(block, thin, packed)
     lower_sent, packed_down = lax.optimization_barrier((lower, packed_down))
     packed_down = sent_to(packed_down, lambda s, m: (s + 1, m) if parity(s + 1, m) else None)
@@ -331,18 +378,24 @@
 
     lower_down = sent_to(lower_sent, lambda s, m: (s + 1, m) if s >= 1 and needs_lower(s + 1, m) else None)
     lower_up = sent_to(lower_sent, lambda s, m: (s - 1, m) if s >= 1 and m == home(s - 1) else None)
-    up = call(own_kernel, [packed], [stacked, stacked], (block, thin, lower), 6 * product)
+    up = call(
+        first_own_kernel, [packed], [stacked, stacked, square], (block, thin, lower), 6 * product, hbm=1
+    )
     up = sent_to(up, lambda s, m: (s - 1, m) if parity(s - 1, m) else None)
-    through, full = call(receive_kernel, [square, stacked], [stacked, square], (packed_down, lower), 6 * long)
+    through, full = call(
+        first_receive_kernel, [square, stacked], [stacked, square, square], (packed_down, lower), 6 * long, hbm=1
+    )
     sent, block, thin = call(fold_kernel, [packed, square, thin_shape], [], (block, thin, full, up), 0)
 
     packed_down = sent_to(sent, lambda s, m: (s + 2, m) if m == home(s + 2) else None)
-    bracket = call(own_kernel, [packed], [stacked, stacked], (block, thin, through), 6 * product)
-    up = sent_to(bracket, lambda s, m: (s - 2, m) if m == home(s - 2) else None)
-    lower = call(lower_kernel, [square], [], (through, lower_down, bracket), product, after=1)
+    up, done = call(
+        bracket_kernel, [packed, (8, TILE)], [stacked, stacked], (block, thin, through), 6 * product
+    )
+    up = sent_to(up, lambda s, m: (s - 2, m) if m == home(s - 2) else None)
+    lower = call(lower_kernel, [square], [], (through, lower_down, done), product)
     lower_down = sent_to(lower, lambda s, m: (s + 2, m) if s >= 2 and m == home(s + 2) else None)
-    packed_down, shares = lax.optimization_barrier((packed_down, shares))
-    through, full = call(receive_kernel, [square, stacked], [stacked, square], (packed_down, lower), 6 * long)
+    packed_down, lower_up, shares = lax.optimization_barrier((packed_down, lower_up, shares))
+    through, full = call(receive_kernel, [square, stacked], [stacked, square], (packed_down, lower), 60 * product)
     sent, block, thin = call(
         fold_above_kernel,
         [packed, square, thin_shape],
@@ -351,17 +404,20 @@
         2 * long,
     )
 
+    sent, lower_down = lax.optimization_barrier((sent, lower_down))
     packed_down = sent_to(sent, lambda s, m: (s + 4, home(s + 4)) if m == home(s) else None)
-    inverse = call(whole_inverse_kernel, [square], [], (block,), 4 * long)
+    has_before = lambda: lax.axis_index("sec") >= 4
+    inverse = call(functools.partial(whole_inverse_kernel, has_before), [square], [], (block,), 4 * long)
     lower, up = call(
-        last_lower_kernel, [square, packed], [stacked, stacked], (through, lower_down, inverse, thin), 3 * product
+        functools.partial(last_lower_kernel, has_before), [square, packed], [stacked, stacked], (through, lower_down, inverse, thin), 3 * product
     )
     up = sent_to(up, lambda s, m: (s - 4, home(s - 4)) if m == home(s) else None)
-    inverse, thin_down = call(
-        invert_kernel, [square, thin_shape], [square], (packed_down,), 4 * product
-    )
     block, thin = call(
-        last_receive_kernel, [square, thin_shape], [stacked], (inverse, thin_down, lower, block, thin), 2 * product
+        functools.partial(last_receive_kernel, has_before),
+        [square, thin_shape],
+        [stacked, square],
+        (packed_down, lower, block, thin),
+        6 * product,
     )
     solved = call(solve_kernel, [thin_shape], [square, thin_shape], (block, thin, up), product)
 
@@ -369,25 +425,25 @@
         sent_to(solved, lambda s, m, k=k: (s, (m + k) % groups) if m == home(s) else None)
         for k in range(1, groups)
     ]
-    homes = jnp.asarray([home(s) for s in range(sections)], jnp.int32)
-    solved = jnp.where(homes[position] == plane, solved, 0.0)
-    padded = (columns + 8, modes.shape[2])
     whole, payload = call(
-        modal_kernel, [thin_shape, padded], [], (solved, *parts, modes[0], shares), product // 32
+        functools.partial(modal_kernel, home),
+        [thin_shape, (columns + 2 * sections, modes.shape[2])],
+        [],
+        (solved, *parts, modes[0], shares),
+        product // 32,
     )
     parts = summed_over_sections(payload)
     pieces = call(
         functools.partial(back_kernel_of, len(parts)),
         [(columns, width)] * groups,
         [thin_shape],
-        (plane.reshape(1), *parts, modes[0]),
+        (*parts, modes[0]),
         product // 32,
-        smem=1,
     )
     summed = pieces[0]
     for k in range(1, groups):
         summed = summed + sent_to(pieces[k], lambda s, m, k=k: (s, (m + k) % groups))
-    own_columns = lax.dynamic_slice_in_dim(whole, plane * width, width, 1)
+    own_columns = lax.dynamic_slice_in_dim(whole, lax.axis_index("mode") * width, width, 1)
     return (own_columns[None], (own_columns - summed)[None])
 
 

time: 123 us -> 89.2 us (0.73)
  starting transfers between devices: 53.9 us -> 32.1 us
  Pallas kernels: 42.4 us -> 23.7 us
  waiting for transfers between devices: 20.7 us -> 31.4 us
  local copies, waits for them, and re-layouts: 2.98 us -> 0.03 us
    ppermute x23 -> x19, starting transfers between devices: 53.9 us -> 32.1 us  [sent_to(): return lax.ppermute(value, AXES, pairs)]
    pallas_call x14, Pallas kernels: 40.2 us -> 22.4 us  [call(): pl.pallas_call(kernel, out_shape=shapes[0] if single else tuple(shapes),...]
    ppermute x23 -> x19, waiting for transfers between devices: 20.7 us -> 31.4 us  [sent_to(): return lax.ppermute(value, AXES, pairs)]
    unnamed x22 -> x12, local copies, waits for them, and re-layouts: 2.25 us -> 0.03 us
  transfers between devices with their start and end apart: 23 -> 19, of which waited for: 13 -> 13; matrix products, arithmetic and copies ran while one was open for 1% -> 0% of each run, Pallas kernels for 31% -> 23%
where the time goes in v3:
time: 89.2 us; the launch traced here: 88.8 us
  starting transfers between devices  32.1 us (36%)
  waiting for transfers between devices  31.4 us (35%)
  Pallas kernels  23.7 us (27%)
  between operations  0.95 us (1%)
    ppermute x19, starting transfers between devices, sent_to(): return lax.ppermute(value, AXES, pairs)  32.1 us
    ppermute x19, waiting for transfers between devices, sent_to(): return lax.ppermute(value, AXES, pairs)  31.4 us
    pallas_call x14, Pallas kernels, call(): pl.pallas_call(kernel, out_shape=shapes[0] if single else tuple(shapes),...  22.4 us
  transfers between devices with their start and end apart: 19, of which 13 were waited for; matrix products, arithmetic and copies ran while one was open for 0% of the time, Pallas kernels for 23%

profile of v3, /device:TPU:0, one launch (start us, length us, event | category | flops | bytes accessed | tf_op | source)
XLA Modules:
  0.0 88.8 jit_solution(13031797881405719466)
XLA Ops:
  0.6 0.0 copy-start
  0.6 0.0 copy-start.3
  0.6 1.3 %shard_map.86 = f32[1344,128]{1,0:T(8,128)S(1)} custom-call(f32[512,512]{1,0:T(8,128)} %bitcast.9, f32[16,512]{1,0:T(8,128)} %bitcast.14), custom_call_target="tpu_custom_call" | custom-call | tf_op jit(solution)/shard_map/pallas_call | solution.py:297
  2.0 0.7 collective-permute-start
  2.7 0.7 collective-permute-start.5
  3.4 0.0 copy-done
  3.5 0.0 copy-done.3
  3.5 4.0 %shard_map.88 = f32[1344,128]{1,0:T(8,128)S(1)} custom-call(f32[512,512]{1,0:T(8,128)S(1)} %bitcast.10, f32[16,512]{1,0:T(8,128)S(1)} %bitcast.15, f32[512,512]{1,0:T(8,128)} %bitcast.2.lower_hbm), custom_call_target="tpu_custom_call" | custom-call | flops 483183808 | bytes 2818048 | tf_op jit(solution)/shard_map/pallas_call | solution.py:311
  7.5 1.3 %collective-permute-start.1 = (f32[1344,128]{1,0:T(8,128)S(1)}, f32[1344,128]{1,0:T(8,128)S(1)}, u32[]{:S(2)}, u32[]{:S(2)}) collective-permute-start(f32[1344,128]{1,0:T(8,128)S(1)} %shard_map.88), channel_id=1, source_target_pairs={{4,0},{5,1},{10,6},{11,7},{12,8},{13,9},{18,14},{19,15},{20,16},{2... | collective-permute-start | bytes 2064392 | tf_op jit(solution)/shard_map/ppermute | solution.py:342
  8.8 1.3 %collective-permute-start.4 = (f32[512,512]{1,0:T(8,128)}, f32[512,512]{1,0:T(8,128)S(1)}, u32[]{:S(2)}, u32[]{:S(2)}) collective-permute-start(f32[512,512]{1,0:T(8,128)} %bitcast.2.lower_hbm), channel_id=1, source_target_pairs={{4,0},{10,6},{13,9},{19,15},{21,17},{27,23},{28,24}} | collective-permute-start | bytes 3145736 | tf_op jit(solution)/shard_map/ppermute | solution.py:342
  10.1 0.0 collective-permute-done.packed
  10.1 4.0 %shard_map.87 = (f32[512,512]{1,0:T(8,128)S(1)}, f32[528,512]{1,0:T(8,128)S(1)}) custom-call(f32[1344,128]{1,0:T(8,128)S(1)} %collective-permute-done.packed, f32[512,512]{1,0:T(8,128)} %bitcast.2.lower_hbm), custom_call_target="tpu_custom_call" | custom-call | flops 4831838208 | bytes 3866624 | tf_op jit(solution)/shard_map/pallas_call | solution.py:311
  14.1 0.6 collective-permute-done.1.above
  14.7 0.2 shard_map.89
  14.9 0.7 collective-permute-start.3
  15.6 3.9 %shard_map.90 = (f32[1344,128]{1,0:T(8,128)S(1)}, f32[8,128]{1,0:T(8,128)S(1)}) custom-call(f32[512,512]{1,0:T(8,128)S(1)} %get-tuple-element.33.block, f32[16,512]{1,0:T(8,128)S(1)} %get-tuple-element.34.thin, f32[512,512]{1,0:T(8,128)S(1)} %get-tuple-element.35.lower.through), custom_call_target="tpu_custom_call" | custom-call | flops 483183808 | bytes 2822144 | tf_op jit(solution)/shard_map/pallas_call | solution.py:311
  19.6 0.0 collective-permute-done.5.passed
  19.6 0.0 copy-start.2
  19.6 0.0 copy-start.4
  19.6 0.0 copy-start.5
  19.6 1.0 %shard_map.92.lower = f32[512,512]{1,0:T(8,128)S(1)} custom-call(f32[512,512]{1,0:T(8,128)S(1)} %get-tuple-element.35.lower.through, f32[512,512]{1,0:T(8,128)S(1)} %collective-permute-done.5.passed, f32[8,128]{1,0:T(8,128)S(1)} %get-tuple-element.41.after), custom_call_target="tpu_custom_call" | custom-call | flops 80530640 | bytes 3149824 | tf_op jit(solution)/shard_map/pallas_call | solution.py:311
  20.6 0.7 collective-permute-start.6
  21.4 1.5 %collective-permute-start.2 = (f32[1344,128]{1,0:T(8,128)S(1)}, f32[1344,128]{1,0:T(8,128)S(1)}, u32[]{:S(2)}, u32[]{:S(2)}) collective-permute-start(f32[1344,128]{1,0:T(8,128)S(1)} %get-tuple-element.36), channel_id=1, source_target_pairs={{8,0},{14,6},{17,9},{23,15},{25,17},{31,23}} | collective-permute-start | bytes 2064392 | tf_op jit(solution)/shard_map/ppermute | solution.py:342
  22.8 0.0 copy-done.2
  22.8 0.0 copy-done.4
  22.9 0.0 copy-done.5
  22.9 0.9 %shard_map.91.shares = f32[8,256]{1,0:T(8,128)S(1)} custom-call(s32[16]{0:T(128)S(1)} %copy-done.5, s32[1,1024]{1,0:T(1,128)S(1)} %bitcast.17, bf16[1024,256]{1,0:T(8,128)(2,1)S(1)} %copy-done.2), custom_call_target="tpu_custom_call" | custom-call | flops 2516582 | bytes 536640 | tf_op jit(solution)/shard_map/pallas_call | solution.py:311
  23.8 0.0 collective-permute-done.4.passed
  23.8 0.0 collective-permute-done.3.packed
  23.8 3.9 %shard_map.93 = (f32[512,512]{1,0:T(8,128)S(1)}, f32[528,512]{1,0:T(8,128)S(1)}) custom-call(f32[1344,128]{1,0:T(8,128)S(1)} %collective-permute-done.3.packed, f32[512,512]{1,0:T(8,128)S(1)} %shard_map.92.lower), custom_call_target="tpu_custom_call" | custom-call | flops 4831838208 | bytes 3866624 | tf_op jit(solution)/shard_map/pallas_call | solution.py:311
  27.7 10.3 %collective-permute-done.2.packed_above = f32[1344,128]{1,0:T(8,128)S(1)} collective-permute-done((f32[1344,128]{1,0:T(8,128)S(1)}, f32[1344,128]{1,0:T(8,128)S(1)}, u32[]{:S(2)}, u32[]{:S(2)}) %collective-permute-start.2) | collective-permute-done | bytes 688160 | tf_op jit(solution)/shard_map/ppermute | solution.py:342
  38.0 2.1 %shard_map.94 = (f32[1344,128]{1,0:T(8,128)S(1)}, f32[512,512]{1,0:T(8,128)S(1)}, f32[16,512]{1,0:T(8,128)S(1)}) custom-call(f32[1344,128]{1,0:T(8,128)S(1)} %collective-permute-done.2.packed_above, f32[512,512]{1,0:T(8,128)S(1)} %collective-permute-done.4.passed, f32[512,512]{1,0:T(8,128)S(1)} %get-tuple-element.33.block, ...), custom_call_target="tpu_custom_call" | custom-call | flops 1610612736 | bytes 5668864 | tf_op jit(solution)/shard_map/pallas_call | solution.py:311
  40.1 0.0 collective-permute-done.6.passed
  40.1 11.3 %collective-permute-start.7 = (f32[1344,128]{1,0:T(8,128)S(1)}, f32[1344,128]{1,0:T(8,128)S(1)}, u32[]{:S(2)}, u32[]{:S(2)}) collective-permute-start(f32[1344,128]{1,0:T(8,128)S(1)} %get-tuple-element.44), channel_id=1, source_target_pairs={{0,17},{6,23},{9,24},{15,30}} | collective-permute-start | bytes 2064392 | tf_op jit(solution)/shard_map/ppermute | solution.py:342
  51.5 1.3 %collective-permute-start.8 = (f32[1344,128]{1,0:T(8,128)S(1)}, f32[1344,128]{1,0:T(8,128)S(1)}, u32[]{:S(2)}, u32[]{:S(2)}) collective-permute-start(f32[1344,128]{1,0:T(8,128)S(1)} %get-tuple-element.52), channel_id=1, source_target_pairs={{17,0},{23,6},{24,9},{30,15}} | collective-permute-start | bytes 2064392 | tf_op jit(solution)/shard_map/ppermute | solution.py:342
  52.8 7.0 %collective-permute-done.7.packed = f32[1344,128]{1,0:T(8,128)S(1)} collective-permute-done((f32[1344,128]{1,0:T(8,128)S(1)}, f32[1344,128]{1,0:T(8,128)S(1)}, u32[]{:S(2)}, u32[]{:S(2)}) %collective-permute-start.7) | collective-permute-done | bytes 688160 | tf_op jit(solution)/shard_map/ppermute | solution.py:342
  59.9 0.1 shard_map.97
  60.0 0.0 copy-start.1
  60.0 6.1 %collective-permute-done.8.above = f32[1344,128]{1,0:T(8,128)S(1)} collective-permute-done((f32[1344,128]{1,0:T(8,128)S(1)}, f32[1344,128]{1,0:T(8,128)S(1)}, u32[]{:S(2)}, u32[]{:S(2)}) %collective-permute-start.8) | collective-permute-done | bytes 688160 | tf_op jit(solution)/shard_map/ppermute | solution.py:342
  66.1 1.9 %shard_map.98.a = f32[16,512]{1,0:T(8,128)S(1)} custom-call(f32[512,512]{1,0:T(8,128)S(1)} %get-tuple-element.50.block, f32[16,512]{1,0:T(8,128)S(1)} %get-tuple-element.51.thin, f32[1344,128]{1,0:T(8,128)S(1)} %collective-permute-done.8.above), custom_call_target="tpu_custom_call" | custom-call | flops 80530640 | bytes 1802240 | tf_op jit(solution)/shard_map/pallas_call | solution.py:311
  67.9 1.3 %collective-permute-start.10 = (f32[16,512]{1,0:T(8,128)S(1)}, f32[16,512]{1,0:T(8,128)S(1)}, u32[]{:S(2)}, u32[]{:S(2)}) collective-permute-start(f32[16,512]{1,0:T(8,128)S(1)} %shard_map.98.a), channel_id=1, source_target_pairs={{0,2},{6,4},{9,11},{15,13},{17,19},{23,21},{24,26},{30,28}} | collective-permute-start | bytes 98312 | tf_op jit(solution)/shard_map/ppermute | solution.py:342
  69.2 1.3 %collective-permute-start.11 = (f32[16,512]{1,0:T(8,128)S(1)}, f32[16,512]{1,0:T(8,128)S(1)}, u32[]{:S(2)}, u32[]{:S(2)}) collective-permute-start(f32[16,512]{1,0:T(8,128)S(1)} %shard_map.98.a), channel_id=1, source_target_pairs={{0,3},{6,5},{9,8},{15,14},{17,16},{23,22},{24,27},{30,29}} | collective-permute-start | bytes 98312 | tf_op jit(solution)/shard_map/ppermute | solution.py:342
  70.5 1.3 %collective-permute-start.9 = (f32[16,512]{1,0:T(8,128)S(1)}, f32[16,512]{1,0:T(8,128)S(1)}, u32[]{:S(2)}, u32[]{:S(2)}) collective-permute-start(f32[16,512]{1,0:T(8,128)S(1)} %shard_map.98.a), channel_id=1, source_target_pairs={{0,1},{6,7},{9,10},{15,12},{17,18},{23,20},{24,25},{30,31}} | collective-permute-start | bytes 98312 | tf_op jit(solution)/shard_map/ppermute | solution.py:342
  71.8 0.0 collective-permute-done.10.c
  71.8 0.3 collective-permute-done.11.d
  72.1 1.3 %collective-permute-done.9.b = f32[16,512]{1,0:T(8,128)S(1)} collective-permute-done((f32[16,512]{1,0:T(8,128)S(1)}, f32[16,512]{1,0:T(8,128)S(1)}, u32[]{:S(2)}, u32[]{:S(2)}) %collective-permute-start.9) | collective-permute-done | bytes 32800 | tf_op jit(solution)/shard_map/ppermute | solution.py:342
  73.4 0.0 copy-done.1
  73.4 0.2 shard_map.99
  73.6 0.1 collective-permute-start.12
  73.7 1.2 %collective-permute-done.12 = f32[32,256]{1,0:T(8,128)S(1)} collective-permute-done((f32[32,256]{1,0:T(8,128)S(1)}, f32[32,256]{1,0:T(8,128)S(1)}, u32[]{:S(2)}, u32[]{:S(2)}) %collective-permute-start.12) | collective-permute-done | bytes 32800 | tf_op jit(solution)/shard_map/ppermute | solution.py:342
  74.9 0.0 collective-permute-start.13
  74.9 1.3 %collective-permute-start.14 = (f32[32,256]{1,0:T(8,128)S(1)}, f32[32,256]{1,0:T(8,128)S(1)}, u32[]{:S(2)}, u32[]{:S(2)}) collective-permute-start(f32[32,256]{1,0:T(8,128)S(1)} %add.16.refs_0_), channel_id=1, source_target_pairs={{0,16},{1,17},{2,18},{3,19},{4,20},{5,21},{6,22},{7,23},{8,24},{9,... | collective-permute-start | bytes 98312 | tf_op jit(solution)/shard_map/ppermute | solution.py:342
  76.2 2.2 %collective-permute-start.15 = (f32[32,256]{1,0:T(8,128)S(1)}, f32[32,256]{1,0:T(8,128)S(1)}, u32[]{:S(2)}, u32[]{:S(2)}) collective-permute-start(f32[32,256]{1,0:T(8,128)S(1)} %add.16.refs_0_), channel_id=1, source_target_pairs={{0,24},{1,25},{2,26},{3,27},{4,28},{5,29},{6,30},{7,31},{8,16},{9,... | collective-permute-start | bytes 98312 | tf_op jit(solution)/shard_map/ppermute | solution.py:342
  78.4 0.4 collective-permute-done.13.refs_1_
  78.8 0.1 collective-permute-done.14.refs_2_
  78.9 2.1 %collective-permute-done.15.refs_3_ = f32[32,256]{1,0:T(8,128)S(1)} collective-permute-done((f32[32,256]{1,0:T(8,128)S(1)}, f32[32,256]{1,0:T(8,128)S(1)}, u32[]{:S(2)}, u32[]{:S(2)}) %collective-permute-start.15) | collective-permute-done | bytes 32800 | tf_op jit(solution)/shard_map/ppermute | solution.py:342
  81.0 0.2 shard_map.100
  81.2 2.3 %collective-permute-start.16 = (f32[16,128]{1,0:T(8,128)S(1)}, f32[16,128]{1,0:T(8,128)S(1)}, u32[]{:S(2)}, u32[]{:S(2)}) collective-permute-start(f32[16,128]{1,0:T(8,128)S(1)} %get-tuple-element.57), channel_id=1, source_target_pairs={{0,1},{1,2},{2,3},{3,0},{4,5},{5,6},{6,7},{7,4},{8,9},{9,10},{10,1... | collective-permute-start | bytes 24584 | tf_op jit(solution)/shard_map/ppermute | solution.py:342
  83.5 1.1 %collective-permute-start.17 = (f32[16,128]{1,0:T(8,128)S(1)}, f32[16,128]{1,0:T(8,128)S(1)}, u32[]{:S(2)}, u32[]{:S(2)}) collective-permute-start(f32[16,128]{1,0:T(8,128)S(1)} %get-tuple-element.58), channel_id=1, source_target_pairs={{0,2},{1,3},{2,0},{3,1},{4,6},{5,7},{6,4},{7,5},{8,10},{9,11},{10,... | collective-permute-start | bytes 24584 | tf_op jit(solution)/shard_map/ppermute | solution.py:342
  84.6 1.7 %collective-permute-start.18 = (f32[16,128]{1,0:T(8,128)S(1)}, f32[16,128]{1,0:T(8,128)S(1)}, u32[]{:S(2)}, u32[]{:S(2)}) collective-permute-start(f32[16,128]{1,0:T(8,128)S(1)} %get-tuple-element.59), channel_id=1, source_target_pairs={{0,3},{1,0},{2,1},{3,2},{4,7},{5,4},{6,5},{7,6},{8,11},{9,8},{10,9... | collective-permute-start | bytes 24584 | tf_op jit(solution)/shard_map/ppermute | solution.py:342
  86.3 0.3 collective-permute-done.16
  86.6 1.4 %collective-permute-done.17 = f32[16,128]{1,0:T(8,128)S(1)} collective-permute-done((f32[16,128]{1,0:T(8,128)S(1)}, f32[16,128]{1,0:T(8,128)S(1)}, u32[]{:S(2)}, u32[]{:S(2)}) %collective-permute-start.17) | collective-permute-done | bytes 8224 | tf_op jit(solution)/shard_map/ppermute | solution.py:342
  88.1 0.2 collective-permute-done.18
  88.2 0.6 subtract_bitcast_fusion
  (3 shorter events, 0.0 us)
Async XLA Ops:
  0.6 2.8 %copy-start = (f32[1,512,512]{2,1,0:T(8,128)S(1)}, f32[1,512,512]{2,1,0:T(8,128)}, u32[]{:S(2)}) copy-start(f32[1,512,512]{2,1,0:T(8,128)} %param.8) | copy-start | bytes 3145732
  0.6 2.8 %copy-start.3 = (f32[1,16,512]{2,1,0:T(8,128)S(1)}, f32[1,16,512]{2,1,0:T(8,128)}, u32[]{:S(2)}) copy-start(f32[1,16,512]{2,1,0:T(8,128)} %param.9) | copy-start | bytes 98308
  2.0 8.1 %collective-permute-start = (f32[1344,128]{1,0:T(8,128)S(1)}, f32[1344,128]{1,0:T(8,128)S(1)}, u32[]{:S(2)}, u32[]{:S(2)}) collective-permute-start(f32[1344,128]{1,0:T(8,128)S(1)} %shard_map.86), channel_id=1, source_target_pairs={{2,6},{3,7},{4,8},{5,9},{10,14},{11,15},{12,16},{13,17},{18,22},{1... | collective-permute-start | bytes 2064392 | tf_op jit(solution)/shard_map/ppermute | solution.py:342
  2.7 16.9 %collective-permute-start.5 = (f32[512,512]{1,0:T(8,128)}, f32[512,512]{1,0:T(8,128)S(1)}, u32[]{:S(2)}, u32[]{:S(2)}) collective-permute-start(f32[512,512]{1,0:T(8,128)} %bitcast.2.lower_hbm), channel_id=1, source_target_pairs={{5,9},{11,15},{12,16},{13,17},{18,22},{19,23},{20,24},{26,30}} | collective-permute-start | bytes 3145736 | tf_op jit(solution)/shard_map/ppermute | solution.py:342
  7.5 7.2 %collective-permute-start.1 = (f32[1344,128]{1,0:T(8,128)S(1)}, f32[1344,128]{1,0:T(8,128)S(1)}, u32[]{:S(2)}, u32[]{:S(2)}) collective-permute-start(f32[1344,128]{1,0:T(8,128)S(1)} %shard_map.88), channel_id=1, source_target_pairs={{4,0},{5,1},{10,6},{11,7},{12,8},{13,9},{18,14},{19,15},{20,16},{2... | collective-permute-start | bytes 2064392 | tf_op jit(solution)/shard_map/ppermute | solution.py:342
  8.8 15.0 %collective-permute-start.4 = (f32[512,512]{1,0:T(8,128)}, f32[512,512]{1,0:T(8,128)S(1)}, u32[]{:S(2)}, u32[]{:S(2)}) collective-permute-start(f32[512,512]{1,0:T(8,128)} %bitcast.2.lower_hbm), channel_id=1, source_target_pairs={{4,0},{10,6},{13,9},{19,15},{21,17},{27,23},{28,24}} | collective-permute-start | bytes 3145736 | tf_op jit(solution)/shard_map/ppermute | solution.py:342
  14.9 8.9 %collective-permute-start.3 = (f32[1344,128]{1,0:T(8,128)S(1)}, f32[1344,128]{1,0:T(8,128)S(1)}, u32[]{:S(2)}, u32[]{:S(2)}) collective-permute-start(f32[1344,128]{1,0:T(8,128)S(1)} %get-tuple-element.37), channel_id=1, source_target_pairs={{1,9},{7,15},{9,17},{15,23},{16,24},{22,30}} | collective-permute-start | bytes 2064392 | tf_op jit(solution)/shard_map/ppermute | solution.py:342
  19.6 3.3 %copy-start.2 = (bf16[1024,256]{1,0:T(8,128)(2,1)S(1)}, bf16[1024,256]{1,0:T(8,128)(2,1)}, u32[]{:S(2)}) copy-start(bf16[1024,256]{1,0:T(8,128)(2,1)} %participation.1) | copy-start | bytes 1572868
  19.6 3.3 %copy-start.4 = (s32[1024]{0:T(1024)S(1)}, s32[1024]{0:T(1024)}, u32[]{:S(2)}) copy-start(s32[1024]{0:T(1024)} %param.11) | copy-start | bytes 12292
  19.6 3.3 %copy-start.5 = (s32[16]{0:T(128)S(1)}, s32[16]{0:T(128)}, u32[]{:S(2)}) copy-start(s32[16]{0:T(128)} %regime.1) | copy-start | bytes 196
  20.6 19.5 %collective-permute-start.6 = (f32[512,512]{1,0:T(8,128)S(1)}, f32[512,512]{1,0:T(8,128)S(1)}, u32[]{:S(2)}, u32[]{:S(2)}) collective-permute-start(f32[512,512]{1,0:T(8,128)S(1)} %shard_map.92.lower), channel_id=1, source_target_pairs={{9,17},{15,23},{16,24},{22,30}} | collective-permute-start | bytes 3145736 | tf_op jit(solution)/shard_map/ppermute | solution.py:342
  21.4 16.7 %collective-permute-start.2 = (f32[1344,128]{1,0:T(8,128)S(1)}, f32[1344,128]{1,0:T(8,128)S(1)}, u32[]{:S(2)}, u32[]{:S(2)}) collective-permute-start(f32[1344,128]{1,0:T(8,128)S(1)} %get-tuple-element.36), channel_id=1, source_target_pairs={{8,0},{14,6},{17,9},{23,15},{25,17},{31,23}} | collective-permute-start | bytes 2064392 | tf_op jit(solution)/shard_map/ppermute | solution.py:342
  40.1 19.7 %collective-permute-start.7 = (f32[1344,128]{1,0:T(8,128)S(1)}, f32[1344,128]{1,0:T(8,128)S(1)}, u32[]{:S(2)}, u32[]{:S(2)}) collective-permute-start(f32[1344,128]{1,0:T(8,128)S(1)} %get-tuple-element.44), channel_id=1, source_target_pairs={{0,17},{6,23},{9,24},{15,30}} | collective-permute-start | bytes 2064392 | tf_op jit(solution)/shard_map/ppermute | solution.py:342
  51.5 14.5 %collective-permute-start.8 = (f32[1344,128]{1,0:T(8,128)S(1)}, f32[1344,128]{1,0:T(8,128)S(1)}, u32[]{:S(2)}, u32[]{:S(2)}) collective-permute-start(f32[1344,128]{1,0:T(8,128)S(1)} %get-tuple-element.52), channel_id=1, source_target_pairs={{17,0},{23,6},{24,9},{30,15}} | collective-permute-start | bytes 2064392 | tf_op jit(solution)/shard_map/ppermute | solution.py:342
  60.0 13.5 %copy-start.1 = (bf16[1,512,256]{2,1,0:T(8,128)(2,1)S(1)}, bf16[1,512,256]{2,1,0:T(8,128)(2,1)}, u32[]{:S(2)}) copy-start(bf16[1,512,256]{2,1,0:T(8,128)(2,1)} %param.10) | copy-start | bytes 786436
  67.9 3.9 %collective-permute-start.10 = (f32[16,512]{1,0:T(8,128)S(1)}, f32[16,512]{1,0:T(8,128)S(1)}, u32[]{:S(2)}, u32[]{:S(2)}) collective-permute-start(f32[16,512]{1,0:T(8,128)S(1)} %shard_map.98.a), channel_id=1, source_target_pairs={{0,2},{6,4},{9,11},{15,13},{17,19},{23,21},{24,26},{30,28}} | collective-permute-start | bytes 98312 | tf_op jit(solution)/shard_map/ppermute | solution.py:342
  69.2 2.9 %collective-permute-start.11 = (f32[16,512]{1,0:T(8,128)S(1)}, f32[16,512]{1,0:T(8,128)S(1)}, u32[]{:S(2)}, u32[]{:S(2)}) collective-permute-start(f32[16,512]{1,0:T(8,128)S(1)} %shard_map.98.a), channel_id=1, source_target_pairs={{0,3},{6,5},{9,8},{15,14},{17,16},{23,22},{24,27},{30,29}} | collective-permute-start | bytes 98312 | tf_op jit(solution)/shard_map/ppermute | solution.py:342
  70.5 2.9 %collective-permute-start.9 = (f32[16,512]{1,0:T(8,128)S(1)}, f32[16,512]{1,0:T(8,128)S(1)}, u32[]{:S(2)}, u32[]{:S(2)}) collective-permute-start(f32[16,512]{1,0:T(8,128)S(1)} %shard_map.98.a), channel_id=1, source_target_pairs={{0,1},{6,7},{9,10},{15,12},{17,18},{23,20},{24,25},{30,31}} | collective-permute-start | bytes 98312 | tf_op jit(solution)/shard_map/ppermute | solution.py:342
  73.6 1.3 %collective-permute-start.12 = (f32[32,256]{1,0:T(8,128)S(1)}, f32[32,256]{1,0:T(8,128)S(1)}, u32[]{:S(2)}, u32[]{:S(2)}) collective-permute-start(f32[32,256]{1,0:T(8,128)S(1)} %get-tuple-element.55), channel_id=1, source_target_pairs={{0,4},{1,5},{2,6},{3,7},{4,0},{5,1},{6,2},{7,3},{8,12},{9,13},{10,... | collective-permute-start | bytes 98312 | tf_op jit(solution)/shard_map/ppermute | solution.py:342
  74.9 3.9 %collective-permute-start.13 = (f32[32,256]{1,0:T(8,128)S(1)}, f32[32,256]{1,0:T(8,128)S(1)}, u32[]{:S(2)}, u32[]{:S(2)}) collective-permute-start(f32[32,256]{1,0:T(8,128)S(1)} %add.16.refs_0_), channel_id=1, source_target_pairs={{0,8},{1,9},{2,10},{3,11},{4,12},{5,13},{6,14},{7,15},{8,0},{9,1},... | collective-permute-start | bytes 98312 | tf_op jit(solution)/shard_map/ppermute | solution.py:342
  74.9 4.0 %collective-permute-start.14 = (f32[32,256]{1,0:T(8,128)S(1)}, f32[32,256]{1,0:T(8,128)S(1)}, u32[]{:S(2)}, u32[]{:S(2)}) collective-permute-start(f32[32,256]{1,0:T(8,128)S(1)} %add.16.refs_0_), channel_id=1, source_target_pairs={{0,16},{1,17},{2,18},{3,19},{4,20},{5,21},{6,22},{7,23},{8,24},{9,... | collective-permute-start | bytes 98312 | tf_op jit(solution)/shard_map/ppermute | solution.py:342
  76.2 4.8 %collective-permute-start.15 = (f32[32,256]{1,0:T(8,128)S(1)}, f32[32,256]{1,0:T(8,128)S(1)}, u32[]{:S(2)}, u32[]{:S(2)}) collective-permute-start(f32[32,256]{1,0:T(8,128)S(1)} %add.16.refs_0_), channel_id=1, source_target_pairs={{0,24},{1,25},{2,26},{3,27},{4,28},{5,29},{6,30},{7,31},{8,16},{9,... | collective-permute-start | bytes 98312 | tf_op jit(solution)/shard_map/ppermute | solution.py:342
  81.2 5.5 %collective-permute-start.16 = (f32[16,128]{1,0:T(8,128)S(1)}, f32[16,128]{1,0:T(8,128)S(1)}, u32[]{:S(2)}, u32[]{:S(2)}) collective-permute-start(f32[16,128]{1,0:T(8,128)S(1)} %get-tuple-element.57), channel_id=1, source_target_pairs={{0,1},{1,2},{2,3},{3,0},{4,5},{5,6},{6,7},{7,4},{8,9},{9,10},{10,1... | collective-permute-start | bytes 24584 | tf_op jit(solution)/shard_map/ppermute | solution.py:342
  83.5 4.5 %collective-permute-start.17 = (f32[16,128]{1,0:T(8,128)S(1)}, f32[16,128]{1,0:T(8,128)S(1)}, u32[]{:S(2)}, u32[]{:S(2)}) collective-permute-start(f32[16,128]{1,0:T(8,128)S(1)} %get-tuple-element.58), channel_id=1, source_target_pairs={{0,2},{1,3},{2,0},{3,1},{4,6},{5,7},{6,4},{7,5},{8,10},{9,11},{10,... | collective-permute-start | bytes 24584 | tf_op jit(solution)/shard_map/ppermute | solution.py:342
  84.6 3.7 %collective-permute-start.18 = (f32[16,128]{1,0:T(8,128)S(1)}, f32[16,128]{1,0:T(8,128)S(1)}, u32[]{:S(2)}, u32[]{:S(2)}) collective-permute-start(f32[16,128]{1,0:T(8,128)S(1)} %get-tuple-element.59), channel_id=1, source_target_pairs={{0,3},{1,0},{2,1},{3,2},{4,7},{5,4},{6,5},{7,6},{8,11},{9,8},{10,9... | collective-permute-start | bytes 24584 | tf_op jit(solution)/shard_map/ppermute | solution.py:342

commit v4 on v3

--- a/solution.py
+++ b/solution.py
@@ -246,8 +246,10 @@
     solution[...] = now
 
 
-def shares_kernel(regime, joints, participation, shares):
-    sections, count = shares.shape[0], joints.shape[1]
+def shares_kernel(regime, joints, participation, modes, out):
+    depth = modes.shape[0]
+    sections, count = out.shape[0] - depth, joints.shape[1]
+    out[0:depth, :] = modes[...].astype(f32)
     bucket = lax.broadcasted_iota(jnp.int32, (1, count), 1) // BUCKET
     rate = jnp.zeros((1, count), f32)
     for b in range(count // BUCKET):
@@ -258,38 +260,44 @@
     section = lax.broadcasted_iota(jnp.int32, (sections, count), 0)
     weights = jnp.where(section == joints[...], rate, 0.0)
     squares = participation[...].astype(f32)
-    shares[...] = times(split(weights), split(squares * squares))
-
-
-def modal_kernel(home, a, b, c, d, modes, shares, whole, payload):
+    out[depth:, :] = times(split(weights), split(squares * squares))
+
+
+def modal_kernel(home, a, b, c, d, local, other, whole, payload):
     position, plane = lax.axis_index("sec"), lax.axis_index("mode")
     own = jnp.where(home(position) == plane, a[...], 0.0)
     value = own + b[...] + c[...] + d[...]
     whole[...] = value
     amplitude = jnp.sqrt(jnp.sum(value * value, keepdims=True) / value.size + 1e-06)
-    rows, sections = value.shape[0], shares.shape[0]
-    payload[0:rows, :] = dot(value.astype(bf16), modes[...])
-    payload[rows : rows + sections, :] = shares[...]
-    mine = lax.broadcasted_iota(jnp.int32, shares.shape, 0) == position
+    (rows, depth), width = value.shape, local.shape[1]
+    sections = local.shape[0] - depth
+    rounded = value.astype(bf16)
+    for k, source in enumerate((local, other)):
+        columns = slice(width * k, width * k + width)
+        payload[0:rows, columns] = dot(rounded, source[0:depth, :].astype(bf16))
+        payload[rows : rows + sections, columns] = source[depth:, :]
+    mine = lax.broadcasted_iota(jnp.int32, (sections, 2 * width), 0) == position
     payload[rows + sections :, :] = jnp.where(mine, amplitude / (1.0 + amplitude), 0.0)
 
 
 def back_kernel_of(count, *refs):
     plane = lax.axis_index("mode")
-    parts, modes, pieces, scratch = refs[:count], refs[count], refs[count + 1 : -1], refs[-1]
+    parts, (local, other), (keep, give), scratch = refs[:count], refs[count : count + 2], refs[count + 2 : -1], refs[-1]
     total = parts[0][...]
     for part in parts[1:]:
         total = total + part[...]
-    rows = scratch.shape[0]
+    rows, depth = scratch.shape
     sections = (total.shape[0] - rows) // 2
-    parts = total[rows : rows + sections, :] * total[rows + sections :, :]
-    damping = jnp.sum(parts, axis=0, keepdims=True)
+    products = total[rows : rows + sections, :] * total[rows + sections :, :]
+    damping = jnp.sum(products, axis=0, keepdims=True)
     removed = (total[0:rows, :] * (damping / (1.0 + damping))).astype(bf16)
-    scratch[...] = dot_t(removed, modes[...])
-    width = pieces[0].shape[1]
-    for k, piece in enumerate(pieces):
-        start = lax.rem(plane + k, len(pieces)) * width
-        piece[...] = scratch[:, pl.ds(pl.multiple_of(start, width), width)]
+    half = local.shape[1]
+    scratch[...] = dot_t(removed[:, 0:half], local[0:depth, :].astype(bf16)) + dot_t(
+        removed[:, half:], other[0:depth, :].astype(bf16)
+    )
+    width = keep.shape[1]
+    for out, owner in ((keep, plane), (give, plane ^ 2)):
+        out[...] = scratch[:, pl.ds(pl.multiple_of(owner * width, width), width)]
 
 
 def packed_from_hbm(block, thin, packed):
@@ -349,11 +357,11 @@
 
     block, thin, lower = stiffness[0], loads[0], coupling[0]
 
-    shares = call(
+    local = call(
         shares_kernel,
-        [(sections, participation.shape[1])],
+        [(size + sections, participation.shape[1])],
         [],
-        (regime, joint_section[None, :], participation),
+        (regime, joint_section[None, :], participation, modes[0]),
         product // 32,
         smem=1,
     )
@@ -382,6 +390,7 @@
         first_own_kernel, [packed], [stacked, stacked, square], (block, thin, lower), 6 * product, hbm=1
     )
     up = sent_to(up, lambda s, m: (s - 1, m) if parity(s - 1, m) else None)
+    other = sent_to(local, lambda s, m: (s, m ^ 1))
     through, full = call(
         first_receive_kernel, [square, stacked], [stacked, square, square], (packed_down, lower), 6 * long, hbm=1
     )
@@ -392,9 +401,10 @@
         bracket_kernel, [packed, (8, TILE)], [stacked, stacked], (block, thin, through), 6 * product
     )
     up = sent_to(up, lambda s, m: (s - 2, m) if m == home(s - 2) else None)
+    lower_down, other = lax.optimization_barrier((lower_down, other))
     lower = call(lower_kernel, [square], [], (through, lower_down, done), product)
     lower_down = sent_to(lower, lambda s, m: (s + 2, m) if s >= 2 and m == home(s + 2) else None)
-    packed_down, lower_up, shares = lax.optimization_barrier((packed_down, lower_up, shares))
+    packed_down, lower_up = lax.optimization_barrier((packed_down, lower_up))
     through, full = call(receive_kernel, [square, stacked], [stacked, square], (packed_down, lower), 60 * product)
     sent, block, thin = call(
         fold_above_kernel,
@@ -427,22 +437,20 @@
     ]
     whole, payload = call(
         functools.partial(modal_kernel, home),
-        [thin_shape, (columns + 2 * sections, modes.shape[2])],
+        [thin_shape, (columns + 2 * sections, 2 * modes.shape[2])],
         [],
-        (solved, *parts, modes[0], shares),
+        (solved, *parts, local, other),
         product // 32,
     )
     parts = summed_over_sections(payload)
-    pieces = call(
+    keep, give = call(
         functools.partial(back_kernel_of, len(parts)),
-        [(columns, width)] * groups,
+        [(columns, width)] * 2,
         [thin_shape],
-        (*parts, modes[0]),
+        (*parts, local, other),
         product // 32,
     )
-    summed = pieces[0]
-    for k in range(1, groups):
-        summed = summed + sent_to(pieces[k], lambda s, m, k=k: (s, (m + k) % groups))
+    summed = keep + sent_to(give, lambda s, m: (s, m ^ 2))
     own_columns = lax.dynamic_slice_in_dim(whole, lax.axis_index("mode") * width, width, 1)
     return (own_columns[None], (own_columns - summed)[None])
 

time: 89.2 us -> 88.1 us (0.988)
  starting transfers between devices: 32.1 us -> 29 us
  waiting for transfers between devices: 31.4 us -> 33.3 us
    ppermute x19 -> x18, starting transfers between devices: 32.1 us -> 29 us  [sent_to(): return lax.ppermute(value, AXES, pairs)]
    ppermute x19 -> x18, waiting for transfers between devices: 31.4 us -> 33.3 us  [sent_to(): return lax.ppermute(value, AXES, pairs)]
  transfers between devices with their start and end apart: 19 -> 18, of which waited for: 13 -> 11; matrix products, arithmetic and copies ran while one was open for 0% -> 0% of each run, Pallas kernels for 23% -> 23%
where the time goes in v4:
time: 88.1 us; the launch traced here: 87.8 us
  waiting for transfers between devices  33.3 us (38%)
  starting transfers between devices  29 us (33%)
  Pallas kernels  23.8 us (27%)
  between operations  0.95 us (1%)
    ppermute x18, waiting for transfers between devices, sent_to(): return lax.ppermute(value, AXES, pairs)  33.3 us
    ppermute x18, starting transfers between devices, sent_to(): return lax.ppermute(value, AXES, pairs)  29 us
    pallas_call x14, Pallas kernels, call(): pl.pallas_call(kernel, out_shape=shapes[0] if single else tuple(shapes),...  22.5 us
  transfers between devices with their start and end apart: 18, of which 11 were waited for; matrix products, arithmetic and copies ran while one was open for 0% of the time, Pallas kernels for 23%

profile of v4, /device:TPU:0, one launch (start us, length us, event | category | flops | bytes accessed | tf_op | source)
XLA Modules:
  0.0 87.8 jit_solution(12309294945122492914)
XLA Ops:
  0.6 0.0 copy-start
  0.6 0.0 copy-start.2
  0.6 1.3 %shard_map.86 = f32[1344,128]{1,0:T(8,128)S(1)} custom-call(f32[512,512]{1,0:T(8,128)} %bitcast.9, f32[16,512]{1,0:T(8,128)} %bitcast.12), custom_call_target="tpu_custom_call" | custom-call | tf_op jit(solution)/shard_map/pallas_call | solution.py:305
  2.0 0.0 copy-start.1
  2.0 0.0 copy-start.3
  2.0 0.0 copy-start.4
  2.0 0.0 copy-start.5
  2.0 0.8 collective-permute-start
  2.9 0.7 collective-permute-start.5
  3.6 0.0 copy-done
  3.6 0.0 copy-done.2
  3.6 4.0 %shard_map.88 = f32[1344,128]{1,0:T(8,128)S(1)} custom-call(f32[512,512]{1,0:T(8,128)S(1)} %bitcast.10, f32[16,512]{1,0:T(8,128)S(1)} %bitcast.13, f32[512,512]{1,0:T(8,128)} %bitcast.2.lower_hbm), custom_call_target="tpu_custom_call" | custom-call | flops 483183808 | bytes 2818048 | tf_op jit(solution)/shard_map/pallas_call | solution.py:319
  7.7 1.3 %collective-permute-start.1 = (f32[1344,128]{1,0:T(8,128)S(1)}, f32[1344,128]{1,0:T(8,128)S(1)}, u32[]{:S(2)}, u32[]{:S(2)}) collective-permute-start(f32[1344,128]{1,0:T(8,128)S(1)} %shard_map.88), channel_id=1, source_target_pairs={{4,0},{5,1},{10,6},{11,7},{12,8},{13,9},{18,14},{19,15},{20,16},{2... | collective-permute-start | bytes 2064392 | tf_op jit(solution)/shard_map/ppermute | solution.py:350
  9.0 1.3 %collective-permute-start.4 = (f32[512,512]{1,0:T(8,128)}, f32[512,512]{1,0:T(8,128)S(1)}, u32[]{:S(2)}, u32[]{:S(2)}) collective-permute-start(f32[512,512]{1,0:T(8,128)} %bitcast.2.lower_hbm), channel_id=1, source_target_pairs={{4,0},{10,6},{13,9},{19,15},{21,17},{27,23},{28,24}} | collective-permute-start | bytes 3145736 | tf_op jit(solution)/shard_map/ppermute | solution.py:350
  10.3 0.0 copy-done.1
  10.3 0.0 copy-done.3
  10.3 0.0 copy-done.4
  10.3 0.0 copy-done.5
  10.3 0.9 %shard_map.91.local.refs_4_ = f32[520,256]{1,0:T(8,128)S(1)} custom-call(s32[16]{0:T(128)S(1)} %copy-done.5, s32[1,1024]{1,0:T(1,128)S(1)} %bitcast.16, bf16[1024,256]{1,0:T(8,128)(2,1)S(1)} %copy-done.1, bf16[512,256]{1,0:T(8,128)(2,1)S(1)} %bitcast.15), custom_call_target="tpu_custom_call" | custom-call | flops 2516582 | bytes 1323072 | tf_op jit(solution)/shard_map/pallas_call | solution.py:319
  11.3 2.5 %collective-permute-start.6 = (f32[520,256]{1,0:T(8,128)S(1)}, f32[520,256]{1,0:T(8,128)S(1)}, u32[]{:S(2)}, u32[]{:S(2)}) collective-permute-start(f32[520,256]{1,0:T(8,128)S(1)} %shard_map.91.local.refs_4_), channel_id=1, source_target_pairs={{0,1},{1,0},{2,3},{3,2},{4,5},{5,4},{6,7},{7,6},{8,9},{9,8},{10,11... | collective-permute-start | bytes 1597448 | tf_op jit(solution)/shard_map/ppermute | solution.py:350
  13.8 0.0 collective-permute-done.packed
  13.8 4.0 %shard_map.87 = (f32[512,512]{1,0:T(8,128)S(1)}, f32[528,512]{1,0:T(8,128)S(1)}) custom-call(f32[1344,128]{1,0:T(8,128)S(1)} %collective-permute-done.packed, f32[512,512]{1,0:T(8,128)} %bitcast.2.lower_hbm), custom_call_target="tpu_custom_call" | custom-call | flops 4831838208 | bytes 3866624 | tf_op jit(solution)/shard_map/pallas_call | solution.py:319
  17.8 0.0 collective-permute-done.1.above
  17.8 0.2 shard_map.89
  18.0 0.7 collective-permute-start.3
  18.7 3.9 %shard_map.90 = (f32[1344,128]{1,0:T(8,128)S(1)}, f32[8,128]{1,0:T(8,128)S(1)}) custom-call(f32[512,512]{1,0:T(8,128)S(1)} %get-tuple-element.32.block, f32[16,512]{1,0:T(8,128)S(1)} %get-tuple-element.33.thin, f32[512,512]{1,0:T(8,128)S(1)} %get-tuple-element.34.lower.through), custom_call_target="tpu_custom_call" | custom-call | flops 483183808 | bytes 2822144 | tf_op jit(solution)/shard_map/pallas_call | solution.py:319
  22.6 1.0 %collective-permute-done.6.other.refs_5_ = f32[520,256]{1,0:T(8,128)S(1)} collective-permute-done((f32[520,256]{1,0:T(8,128)S(1)}, f32[520,256]{1,0:T(8,128)S(1)}, u32[]{:S(2)}, u32[]{:S(2)}) %collective-permute-start.6) | collective-permute-done | bytes 532512 | tf_op jit(solution)/shard_map/ppermute | solution.py:350
  23.7 0.0 collective-permute-done.5.passed
  23.7 1.0 %shard_map.92.lower = f32[512,512]{1,0:T(8,128)S(1)} custom-call(f32[512,512]{1,0:T(8,128)S(1)} %get-tuple-element.34.lower.through, f32[512,512]{1,0:T(8,128)S(1)} %collective-permute-done.5.passed, f32[8,128]{1,0:T(8,128)S(1)} %get-tuple-element.41.after), custom_call_target="tpu_custom_call" | custom-call | flops 80530640 | bytes 3149824 | tf_op jit(solution)/shard_map/pallas_call | solution.py:319
  24.7 0.7 collective-permute-start.7
  25.4 1.5 %collective-permute-start.2 = (f32[1344,128]{1,0:T(8,128)S(1)}, f32[1344,128]{1,0:T(8,128)S(1)}, u32[]{:S(2)}, u32[]{:S(2)}) collective-permute-start(f32[1344,128]{1,0:T(8,128)S(1)} %get-tuple-element.35), channel_id=1, source_target_pairs={{8,0},{14,6},{17,9},{23,15},{25,17},{31,23}} | collective-permute-start | bytes 2064392 | tf_op jit(solution)/shard_map/ppermute | solution.py:350
  26.9 0.0 collective-permute-done.4.passed
  26.9 0.0 collective-permute-done.3.packed
  26.9 3.9 %shard_map.93 = (f32[512,512]{1,0:T(8,128)S(1)}, f32[528,512]{1,0:T(8,128)S(1)}) custom-call(f32[1344,128]{1,0:T(8,128)S(1)} %collective-permute-done.3.packed, f32[512,512]{1,0:T(8,128)S(1)} %shard_map.92.lower), custom_call_target="tpu_custom_call" | custom-call | flops 4831838208 | bytes 3866624 | tf_op jit(solution)/shard_map/pallas_call | solution.py:319
  30.8 9.3 %collective-permute-done.2.packed_above = f32[1344,128]{1,0:T(8,128)S(1)} collective-permute-done((f32[1344,128]{1,0:T(8,128)S(1)}, f32[1344,128]{1,0:T(8,128)S(1)}, u32[]{:S(2)}, u32[]{:S(2)}) %collective-permute-start.2) | collective-permute-done | bytes 688160 | tf_op jit(solution)/shard_map/ppermute | solution.py:350
  40.1 2.1 %shard_map.94 = (f32[1344,128]{1,0:T(8,128)S(1)}, f32[512,512]{1,0:T(8,128)S(1)}, f32[16,512]{1,0:T(8,128)S(1)}) custom-call(f32[1344,128]{1,0:T(8,128)S(1)} %collective-permute-done.2.packed_above, f32[512,512]{1,0:T(8,128)S(1)} %collective-permute-done.4.passed, f32[512,512]{1,0:T(8,128)S(1)} %get-tuple-element.32.block, ...), custom_call_target="tpu_custom_call" | custom-call | flops 1610612736 | bytes 5668864 | tf_op jit(solution)/shard_map/pallas_call | solution.py:319
  42.2 0.0 collective-permute-done.7.passed
  42.2 9.5 %collective-permute-start.8 = (f32[1344,128]{1,0:T(8,128)S(1)}, f32[1344,128]{1,0:T(8,128)S(1)}, u32[]{:S(2)}, u32[]{:S(2)}) collective-permute-start(f32[1344,128]{1,0:T(8,128)S(1)} %get-tuple-element.44), channel_id=1, source_target_pairs={{0,17},{6,23},{9,24},{15,30}} | collective-permute-start | bytes 2064392 | tf_op jit(solution)/shard_map/ppermute | solution.py:350
  51.7 1.3 %collective-permute-start.9 = (f32[1344,128]{1,0:T(8,128)S(1)}, f32[1344,128]{1,0:T(8,128)S(1)}, u32[]{:S(2)}, u32[]{:S(2)}) collective-permute-start(f32[1344,128]{1,0:T(8,128)S(1)} %get-tuple-element.52), channel_id=1, source_target_pairs={{17,0},{23,6},{24,9},{30,15}} | collective-permute-start | bytes 2064392 | tf_op jit(solution)/shard_map/ppermute | solution.py:350
  53.0 7.0 %collective-permute-done.8.packed = f32[1344,128]{1,0:T(8,128)S(1)} collective-permute-done((f32[1344,128]{1,0:T(8,128)S(1)}, f32[1344,128]{1,0:T(8,128)S(1)}, u32[]{:S(2)}, u32[]{:S(2)}) %collective-permute-start.8) | collective-permute-done | bytes 688160 | tf_op jit(solution)/shard_map/ppermute | solution.py:350
  60.1 0.1 shard_map.97
  60.1 6.1 %collective-permute-done.9.above = f32[1344,128]{1,0:T(8,128)S(1)} collective-permute-done((f32[1344,128]{1,0:T(8,128)S(1)}, f32[1344,128]{1,0:T(8,128)S(1)}, u32[]{:S(2)}, u32[]{:S(2)}) %collective-permute-start.9) | collective-permute-done | bytes 688160 | tf_op jit(solution)/shard_map/ppermute | solution.py:350
  66.2 1.9 %shard_map.98.a = f32[16,512]{1,0:T(8,128)S(1)} custom-call(f32[512,512]{1,0:T(8,128)S(1)} %get-tuple-element.50.block, f32[16,512]{1,0:T(8,128)S(1)} %get-tuple-element.51.thin, f32[1344,128]{1,0:T(8,128)S(1)} %collective-permute-done.9.above), custom_call_target="tpu_custom_call" | custom-call | flops 80530640 | bytes 1802240 | tf_op jit(solution)/shard_map/pallas_call | solution.py:319
  68.1 1.3 %collective-permute-start.10 = (f32[16,512]{1,0:T(8,128)S(1)}, f32[16,512]{1,0:T(8,128)S(1)}, u32[]{:S(2)}, u32[]{:S(2)}) collective-permute-start(f32[16,512]{1,0:T(8,128)S(1)} %shard_map.98.a), channel_id=1, source_target_pairs={{0,1},{6,7},{9,10},{15,12},{17,18},{23,20},{24,25},{30,31}} | collective-permute-start | bytes 98312 | tf_op jit(solution)/shard_map/ppermute | solution.py:350
  69.4 1.3 %collective-permute-start.11 = (f32[16,512]{1,0:T(8,128)S(1)}, f32[16,512]{1,0:T(8,128)S(1)}, u32[]{:S(2)}, u32[]{:S(2)}) collective-permute-start(f32[16,512]{1,0:T(8,128)S(1)} %shard_map.98.a), channel_id=1, source_target_pairs={{0,2},{6,4},{9,11},{15,13},{17,19},{23,21},{24,26},{30,28}} | collective-permute-start | bytes 98312 | tf_op jit(solution)/shard_map/ppermute | solution.py:350
  70.7 1.3 %collective-permute-start.12 = (f32[16,512]{1,0:T(8,128)S(1)}, f32[16,512]{1,0:T(8,128)S(1)}, u32[]{:S(2)}, u32[]{:S(2)}) collective-permute-start(f32[16,512]{1,0:T(8,128)S(1)} %shard_map.98.a), channel_id=1, source_target_pairs={{0,3},{6,5},{9,8},{15,14},{17,16},{23,22},{24,27},{30,29}} | collective-permute-start | bytes 98312 | tf_op jit(solution)/shard_map/ppermute | solution.py:350
  72.0 0.0 collective-permute-done.10.b
  72.0 0.3 collective-permute-done.11.c
  72.3 1.3 %collective-permute-done.12.d = f32[16,512]{1,0:T(8,128)S(1)} collective-permute-done((f32[16,512]{1,0:T(8,128)S(1)}, f32[16,512]{1,0:T(8,128)S(1)}, u32[]{:S(2)}, u32[]{:S(2)}) %collective-permute-start.12) | collective-permute-done | bytes 32800 | tf_op jit(solution)/shard_map/ppermute | solution.py:350
  73.6 0.2 shard_map.99
  73.8 0.1 collective-permute-start.13
  73.9 1.2 %collective-permute-done.13 = f32[32,512]{1,0:T(8,128)S(1)} collective-permute-done((f32[32,512]{1,0:T(8,128)S(1)}, f32[32,512]{1,0:T(8,128)S(1)}, u32[]{:S(2)}, u32[]{:S(2)}) %collective-permute-start.13) | collective-permute-done | bytes 65568 | tf_op jit(solution)/shard_map/ppermute | solution.py:350
  75.1 1.4 %collective-permute-start.14 = (f32[32,512]{1,0:T(8,128)S(1)}, f32[32,512]{1,0:T(8,128)S(1)}, u32[]{:S(2)}, u32[]{:S(2)}) collective-permute-start(f32[32,512]{1,0:T(8,128)S(1)} %add.10.refs_0_), channel_id=1, source_target_pairs={{0,8},{1,9},{2,10},{3,11},{4,12},{5,13},{6,14},{7,15},{8,0},{9,1},... | collective-permute-start | bytes 196616 | tf_op jit(solution)/shard_map/ppermute | solution.py:350
  76.5 0.7 collective-permute-start.15
  77.2 1.5 %collective-permute-start.16 = (f32[32,512]{1,0:T(8,128)S(1)}, f32[32,512]{1,0:T(8,128)S(1)}, u32[]{:S(2)}, u32[]{:S(2)}) collective-permute-start(f32[32,512]{1,0:T(8,128)S(1)} %add.10.refs_0_), channel_id=1, source_target_pairs={{0,24},{1,25},{2,26},{3,27},{4,28},{5,29},{6,30},{7,31},{8,16},{9,... | collective-permute-start | bytes 196616 | tf_op jit(solution)/shard_map/ppermute | solution.py:350
  78.7 0.8 collective-permute-done.14.refs_1_
  79.5 1.6 %collective-permute-done.15.refs_2_ = f32[32,512]{1,0:T(8,128)S(1)} collective-permute-done((f32[32,512]{1,0:T(8,128)S(1)}, f32[32,512]{1,0:T(8,128)S(1)}, u32[]{:S(2)}, u32[]{:S(2)}) %collective-permute-start.15) | collective-permute-done | bytes 65568 | tf_op jit(solution)/shard_map/ppermute | solution.py:350
  81.1 1.3 %collective-permute-done.16.refs_3_ = f32[32,512]{1,0:T(8,128)S(1)} collective-permute-done((f32[32,512]{1,0:T(8,128)S(1)}, f32[32,512]{1,0:T(8,128)S(1)}, u32[]{:S(2)}, u32[]{:S(2)}) %collective-permute-start.16) | collective-permute-done | bytes 65568 | tf_op jit(solution)/shard_map/ppermute | solution.py:350
  82.4 0.2 shard_map.100
  82.6 1.2 %collective-permute-start.17 = (f32[16,128]{1,0:T(8,128)S(1)}, f32[16,128]{1,0:T(8,128)S(1)}, u32[]{:S(2)}, u32[]{:S(2)}) collective-permute-start(f32[16,128]{1,0:T(8,128)S(1)} %get-tuple-element.57), channel_id=1, source_target_pairs={{0,2},{1,3},{2,0},{3,1},{4,6},{5,7},{6,4},{7,5},{8,10},{9,11},{10,... | collective-permute-start | bytes 24584 | tf_op jit(solution)/shard_map/ppermute | solution.py:350
  83.8 3.4 %collective-permute-done.17 = f32[16,128]{1,0:T(8,128)S(1)} collective-permute-done((f32[16,128]{1,0:T(8,128)S(1)}, f32[16,128]{1,0:T(8,128)S(1)}, u32[]{:S(2)}, u32[]{:S(2)}) %collective-permute-start.17) | collective-permute-done | bytes 8224 | tf_op jit(solution)/shard_map/ppermute | solution.py:350
  87.2 0.6 subtract_bitcast_fusion
  (3 shorter events, 0.0 us)
Async XLA Ops:
  0.6 3.0 %copy-start = (f32[1,512,512]{2,1,0:T(8,128)S(1)}, f32[1,512,512]{2,1,0:T(8,128)}, u32[]{:S(2)}) copy-start(f32[1,512,512]{2,1,0:T(8,128)} %param.8) | copy-start | bytes 3145732
  0.6 3.0 %copy-start.2 = (f32[1,16,512]{2,1,0:T(8,128)S(1)}, f32[1,16,512]{2,1,0:T(8,128)}, u32[]{:S(2)}) copy-start(f32[1,16,512]{2,1,0:T(8,128)} %param.9) | copy-start | bytes 98308
  2.0 8.3 %copy-start.1 = (bf16[1024,256]{1,0:T(8,128)(2,1)S(1)}, bf16[1024,256]{1,0:T(8,128)(2,1)}, u32[]{:S(2)}) copy-start(bf16[1024,256]{1,0:T(8,128)(2,1)} %participation.1) | copy-start | bytes 1572868
  2.0 8.3 %copy-start.3 = (bf16[1,512,256]{2,1,0:T(8,128)(2,1)S(1)}, bf16[1,512,256]{2,1,0:T(8,128)(2,1)}, u32[]{:S(2)}) copy-start(bf16[1,512,256]{2,1,0:T(8,128)(2,1)} %param.10) | copy-start | bytes 786436
  2.0 8.3 %copy-start.4 = (s32[1024]{0:T(1024)S(1)}, s32[1024]{0:T(1024)}, u32[]{:S(2)}) copy-start(s32[1024]{0:T(1024)} %param.11) | copy-start | bytes 12292
  2.0 8.3 %copy-start.5 = (s32[16]{0:T(128)S(1)}, s32[16]{0:T(128)}, u32[]{:S(2)}) copy-start(s32[16]{0:T(128)} %regime.1) | copy-start | bytes 196
  2.0 11.7 %collective-permute-start = (f32[1344,128]{1,0:T(8,128)S(1)}, f32[1344,128]{1,0:T(8,128)S(1)}, u32[]{:S(2)}, u32[]{:S(2)}) collective-permute-start(f32[1344,128]{1,0:T(8,128)S(1)} %shard_map.86), channel_id=1, source_target_pairs={{2,6},{3,7},{4,8},{5,9},{10,14},{11,15},{12,16},{13,17},{18,22},{1... | collective-permute-start | bytes 2064392 | tf_op jit(solution)/shard_map/ppermute | solution.py:350
  2.9 20.8 %collective-permute-start.5 = (f32[512,512]{1,0:T(8,128)}, f32[512,512]{1,0:T(8,128)S(1)}, u32[]{:S(2)}, u32[]{:S(2)}) collective-permute-start(f32[512,512]{1,0:T(8,128)} %bitcast.2.lower_hbm), channel_id=1, source_target_pairs={{5,9},{11,15},{12,16},{13,17},{18,22},{19,23},{20,24},{26,30}} | collective-permute-start | bytes 3145736 | tf_op jit(solution)/shard_map/ppermute | solution.py:350
  7.7 10.1 %collective-permute-start.1 = (f32[1344,128]{1,0:T(8,128)S(1)}, f32[1344,128]{1,0:T(8,128)S(1)}, u32[]{:S(2)}, u32[]{:S(2)}) collective-permute-start(f32[1344,128]{1,0:T(8,128)S(1)} %shard_map.88), channel_id=1, source_target_pairs={{4,0},{5,1},{10,6},{11,7},{12,8},{13,9},{18,14},{19,15},{20,16},{2... | collective-permute-start | bytes 2064392 | tf_op jit(solution)/shard_map/ppermute | solution.py:350
  9.0 17.9 %collective-permute-start.4 = (f32[512,512]{1,0:T(8,128)}, f32[512,512]{1,0:T(8,128)S(1)}, u32[]{:S(2)}, u32[]{:S(2)}) collective-permute-start(f32[512,512]{1,0:T(8,128)} %bitcast.2.lower_hbm), channel_id=1, source_target_pairs={{4,0},{10,6},{13,9},{19,15},{21,17},{27,23},{28,24}} | collective-permute-start | bytes 3145736 | tf_op jit(solution)/shard_map/ppermute | solution.py:350
  11.3 12.4 %collective-permute-start.6 = (f32[520,256]{1,0:T(8,128)S(1)}, f32[520,256]{1,0:T(8,128)S(1)}, u32[]{:S(2)}, u32[]{:S(2)}) collective-permute-start(f32[520,256]{1,0:T(8,128)S(1)} %shard_map.91.local.refs_4_), channel_id=1, source_target_pairs={{0,1},{1,0},{2,3},{3,2},{4,5},{5,4},{6,7},{7,6},{8,9},{9,8},{10,11... | collective-permute-start | bytes 1597448 | tf_op jit(solution)/shard_map/ppermute | solution.py:350
  18.0 8.9 %collective-permute-start.3 = (f32[1344,128]{1,0:T(8,128)S(1)}, f32[1344,128]{1,0:T(8,128)S(1)}, u32[]{:S(2)}, u32[]{:S(2)}) collective-permute-start(f32[1344,128]{1,0:T(8,128)S(1)} %get-tuple-element.36), channel_id=1, source_target_pairs={{1,9},{7,15},{9,17},{15,23},{16,24},{22,30}} | collective-permute-start | bytes 2064392 | tf_op jit(solution)/shard_map/ppermute | solution.py:350
  24.7 17.5 %collective-permute-start.7 = (f32[512,512]{1,0:T(8,128)S(1)}, f32[512,512]{1,0:T(8,128)S(1)}, u32[]{:S(2)}, u32[]{:S(2)}) collective-permute-start(f32[512,512]{1,0:T(8,128)S(1)} %shard_map.92.lower), channel_id=1, source_target_pairs={{9,17},{15,23},{16,24},{22,30}} | collective-permute-start | bytes 3145736 | tf_op jit(solution)/shard_map/ppermute | solution.py:350
  25.4 14.7 %collective-permute-start.2 = (f32[1344,128]{1,0:T(8,128)S(1)}, f32[1344,128]{1,0:T(8,128)S(1)}, u32[]{:S(2)}, u32[]{:S(2)}) collective-permute-start(f32[1344,128]{1,0:T(8,128)S(1)} %get-tuple-element.35), channel_id=1, source_target_pairs={{8,0},{14,6},{17,9},{23,15},{25,17},{31,23}} | collective-permute-start | bytes 2064392 | tf_op jit(solution)/shard_map/ppermute | solution.py:350
  42.2 17.9 %collective-permute-start.8 = (f32[1344,128]{1,0:T(8,128)S(1)}, f32[1344,128]{1,0:T(8,128)S(1)}, u32[]{:S(2)}, u32[]{:S(2)}) collective-permute-start(f32[1344,128]{1,0:T(8,128)S(1)} %get-tuple-element.44), channel_id=1, source_target_pairs={{0,17},{6,23},{9,24},{15,30}} | collective-permute-start | bytes 2064392 | tf_op jit(solution)/shard_map/ppermute | solution.py:350
  51.7 14.5 %collective-permute-start.9 = (f32[1344,128]{1,0:T(8,128)S(1)}, f32[1344,128]{1,0:T(8,128)S(1)}, u32[]{:S(2)}, u32[]{:S(2)}) collective-permute-start(f32[1344,128]{1,0:T(8,128)S(1)} %get-tuple-element.52), channel_id=1, source_target_pairs={{17,0},{23,6},{24,9},{30,15}} | collective-permute-start | bytes 2064392 | tf_op jit(solution)/shard_map/ppermute | solution.py:350
  68.1 3.9 %collective-permute-start.10 = (f32[16,512]{1,0:T(8,128)S(1)}, f32[16,512]{1,0:T(8,128)S(1)}, u32[]{:S(2)}, u32[]{:S(2)}) collective-permute-start(f32[16,512]{1,0:T(8,128)S(1)} %shard_map.98.a), channel_id=1, source_target_pairs={{0,1},{6,7},{9,10},{15,12},{17,18},{23,20},{24,25},{30,31}} | collective-permute-start | bytes 98312 | tf_op jit(solution)/shard_map/ppermute | solution.py:350
  69.4 2.9 %collective-permute-start.11 = (f32[16,512]{1,0:T(8,128)S(1)}, f32[16,512]{1,0:T(8,128)S(1)}, u32[]{:S(2)}, u32[]{:S(2)}) collective-permute-start(f32[16,512]{1,0:T(8,128)S(1)} %shard_map.98.a), channel_id=1, source_target_pairs={{0,2},{6,4},{9,11},{15,13},{17,19},{23,21},{24,26},{30,28}} | collective-permute-start | bytes 98312 | tf_op jit(solution)/shard_map/ppermute | solution.py:350
  70.7 2.9 %collective-permute-start.12 = (f32[16,512]{1,0:T(8,128)S(1)}, f32[16,512]{1,0:T(8,128)S(1)}, u32[]{:S(2)}, u32[]{:S(2)}) collective-permute-start(f32[16,512]{1,0:T(8,128)S(1)} %shard_map.98.a), channel_id=1, source_target_pairs={{0,3},{6,5},{9,8},{15,14},{17,16},{23,22},{24,27},{30,29}} | collective-permute-start | bytes 98312 | tf_op jit(solution)/shard_map/ppermute | solution.py:350
  73.8 1.3 %collective-permute-start.13 = (f32[32,512]{1,0:T(8,128)S(1)}, f32[32,512]{1,0:T(8,128)S(1)}, u32[]{:S(2)}, u32[]{:S(2)}) collective-permute-start(f32[32,512]{1,0:T(8,128)S(1)} %get-tuple-element.55), channel_id=1, source_target_pairs={{0,4},{1,5},{2,6},{3,7},{4,0},{5,1},{6,2},{7,3},{8,12},{9,13},{10,... | collective-permute-start | bytes 196616 | tf_op jit(solution)/shard_map/ppermute | solution.py:350
  75.1 4.3 %collective-permute-start.14 = (f32[32,512]{1,0:T(8,128)S(1)}, f32[32,512]{1,0:T(8,128)S(1)}, u32[]{:S(2)}, u32[]{:S(2)}) collective-permute-start(f32[32,512]{1,0:T(8,128)S(1)} %add.10.refs_0_), channel_id=1, source_target_pairs={{0,8},{1,9},{2,10},{3,11},{4,12},{5,13},{6,14},{7,15},{8,0},{9,1},... | collective-permute-start | bytes 196616 | tf_op jit(solution)/shard_map/ppermute | solution.py:350
  76.5 4.6 %collective-permute-start.15 = (f32[32,512]{1,0:T(8,128)S(1)}, f32[32,512]{1,0:T(8,128)S(1)}, u32[]{:S(2)}, u32[]{:S(2)}) collective-permute-start(f32[32,512]{1,0:T(8,128)S(1)} %add.10.refs_0_), channel_id=1, source_target_pairs={{0,16},{1,17},{2,18},{3,19},{4,20},{5,21},{6,22},{7,23},{8,24},{9,... | collective-permute-start | bytes 196616 | tf_op jit(solution)/shard_map/ppermute | solution.py:350
  77.2 5.2 %collective-permute-start.16 = (f32[32,512]{1,0:T(8,128)S(1)}, f32[32,512]{1,0:T(8,128)S(1)}, u32[]{:S(2)}, u32[]{:S(2)}) collective-permute-start(f32[32,512]{1,0:T(8,128)S(1)} %add.10.refs_0_), channel_id=1, source_target_pairs={{0,24},{1,25},{2,26},{3,27},{4,28},{5,29},{6,30},{7,31},{8,16},{9,... | collective-permute-start | bytes 196616 | tf_op jit(solution)/shard_map/ppermute | solution.py:350
  82.6 4.6 %collective-permute-start.17 = (f32[16,128]{1,0:T(8,128)S(1)}, f32[16,128]{1,0:T(8,128)S(1)}, u32[]{:S(2)}, u32[]{:S(2)}) collective-permute-start(f32[16,128]{1,0:T(8,128)S(1)} %get-tuple-element.57), channel_id=1, source_target_pairs={{0,2},{1,3},{2,0},{3,1},{4,6},{5,7},{6,4},{7,5},{8,10},{9,11},{10,... | collective-permute-start | bytes 24584 | tf_op jit(solution)/shard_map/ppermute | solution.py:350

commit v5 on v4

--- a/solution.py
+++ b/solution.py
@@ -177,15 +177,38 @@
     unpack(packed, block_out, thin_out)
 
 
-def fold_above_kernel(packed_above, passed, block, thin, full, packed, block_out, thin_out, stack, out, whole):
-    size = block.shape[0]
+def part_above(packed_above, passed, stack, out, whole):
+    size = passed.shape[0]
     unpack(packed_above, whole, stack.at[size:, :])
     right = split(passed[...])
     stack[0:size, :] = times(split(passed[...].T), split(whole[...]))
     stack[size:, :] = -stack[size:, :]
     out[...] = times(split(stack[...]), right)
+
+
+def fold_above_kernel(early, late, passed, block, thin, full, packed, block_out, thin_out, stack, out, whole, both):
+    both[...] = early[...] + late[...]
+    part_above(both, passed, stack, out, whole)
     folded(packed, block, thin, full, out)
     unpack(packed, block_out, thin_out)
+
+
+def fold_sent_kernel(needed, after, early, late, passed, block, thin, full, packed, block_out, thin_out, *scratch):
+    @pl.when(needed())
+    def _():
+        fold_above_kernel(early, late, passed, block, thin, full, packed, block_out, thin_out, *scratch)
+
+
+def fold_kept_kernel(needed, early, passed, block, thin, full, block_out, thin_out, inverse, stack, out, whole):
+    size = block.shape[0]
+
+    @pl.when(needed())
+    def _():
+        part_above(early, passed, stack, out, whole)
+        value = block[...] - full[0:size, :] - out[0:size, :]
+        block_out[...] = value
+        thin_out[...] = thin[...] - full[size:, :] - out[size:, :]
+        inverse[...] = inverse_of(value)
 
 
 def whole_inverse_kernel(needed, block, inverse):
@@ -211,7 +234,7 @@
         pack(packed, out, out.at[size:, :])
 
 
-def last_receive_kernel(needed, packed, lower, block, thin, block_out, thin_out, stack, whole):
+def last_receive_kernel(needed, packed, lower, block, thin, block_else, thin_else, block_out, thin_out, stack, whole):
     size = block.shape[0]
 
     @pl.when(needed())
@@ -225,8 +248,8 @@
 
     @pl.when(jnp.logical_not(needed()))
     def _():
-        block_out[...] = block[...]
-        thin_out[...] = thin[...]
+        block_out[...] = block_else[...]
+        thin_out[...] = thin_else[...]
 
 
 def solve_kernel(block, thin, above, solution, whole, own):
@@ -400,33 +423,53 @@
     up, done = call(
         bracket_kernel, [packed, (8, TILE)], [stacked, stacked], (block, thin, through), 6 * product
     )
-    up = sent_to(up, lambda s, m: (s - 2, m) if m == home(s - 2) else None)
+    early = sent_to(up, lambda s, m: (s - 2, m) if m == home(s - 2) and m != home(s) else None)
+    up_late = up
     lower_down, other = lax.optimization_barrier((lower_down, other))
     lower = call(lower_kernel, [square], [], (through, lower_down, done), product)
     lower_down = sent_to(lower, lambda s, m: (s + 2, m) if s >= 2 and m == home(s + 2) else None)
+    up_late, _ = lax.optimization_barrier((up_late, lower))
+    late = sent_to(up_late, lambda s, m: (s - 2, m) if m == home(s - 2) and m == home(s) else None)
     packed_down, lower_up = lax.optimization_barrier((packed_down, lower_up))
-    through, full = call(receive_kernel, [square, stacked], [stacked, square], (packed_down, lower), 60 * product)
-    sent, block, thin = call(
-        fold_above_kernel,
-        [packed, square, thin_shape],
-        [stacked, stacked, square],
-        (up, lower_up, block, thin, full),
-        2 * long,
-    )
+    through, full = call(receive_kernel, [square, stacked], [stacked, square], (packed_down, lower), 6 * product)
+    has_before = lambda: lax.axis_index("sec") >= 4
+    if sections == 8:
+        block_kept, thin_kept, inverse = call(
+            functools.partial(fold_kept_kernel, has_before),
+            [square, thin_shape, square],
+            [stacked, stacked, square],
+            (early, lower_up, block, thin, full),
+            2 * long,
+        )
+        sent, block, thin = call(
+            functools.partial(fold_sent_kernel, lambda: lax.axis_index("sec") < 4),
+            [packed, square, thin_shape],
+            [stacked, stacked, square, packed],
+            (thin_kept, early, late, lower_up, block, thin, full),
+            3 * long,
+        )
+    else:
+        sent, block, thin = call(
+            fold_above_kernel,
+            [packed, square, thin_shape],
+            [stacked, stacked, square, packed],
+            (early, late, lower_up, block, thin, full),
+            2 * long,
+        )
+        inverse = call(functools.partial(whole_inverse_kernel, has_before), [square], [], (block,), 4 * long)
+        block_kept, thin_kept = block, thin
 
     sent, lower_down = lax.optimization_barrier((sent, lower_down))
     packed_down = sent_to(sent, lambda s, m: (s + 4, home(s + 4)) if m == home(s) else None)
-    has_before = lambda: lax.axis_index("sec") >= 4
-    inverse = call(functools.partial(whole_inverse_kernel, has_before), [square], [], (block,), 4 * long)
     lower, up = call(
-        functools.partial(last_lower_kernel, has_before), [square, packed], [stacked, stacked], (through, lower_down, inverse, thin), 3 * product
+        functools.partial(last_lower_kernel, has_before), [square, packed], [stacked, stacked], (through, lower_down, inverse, thin_kept), 3 * product
     )
     up = sent_to(up, lambda s, m: (s - 4, home(s - 4)) if m == home(s) else None)
     block, thin = call(
         functools.partial(last_receive_kernel, has_before),
         [square, thin_shape],
         [stacked, square],
-        (packed_down, lower, block, thin),
+        (packed_down, lower, block_kept, thin_kept, block, thin),
         6 * product,
     )
     solved = call(solve_kernel, [thin_shape], [square, thin_shape], (block, thin, up), product)

time: 88.1 us -> 87.9 us (level)
  waiting for transfers between devices: 33.3 us -> 26.7 us
  starting transfers between devices: 29 us -> 34 us
  local copies, waits for them, and re-layouts: 0.03 us -> 1.25 us
    ppermute x18 -> x19, waiting for transfers between devices: 33.3 us -> 26.7 us  [sent_to(): return lax.ppermute(value, AXES, pairs)]
    ppermute x18 -> x19, starting transfers between devices: 29 us -> 34 us  [sent_to(): return lax.ppermute(value, AXES, pairs)]
    unnamed x12 -> x16, local copies, waits for them, and re-layouts: 0.03 us -> 1.25 us
  transfers between devices with their start and end apart: 18 -> 19, of which waited for: 11 -> 10; matrix products, arithmetic and copies ran while one was open for 0% -> 0% of each run, Pallas kernels for 23% -> 23%
where the time goes in v5:
time: 87.9 us; the launch traced here: 87.6 us
  starting transfers between devices  34 us (39%)
  waiting for transfers between devices  26.7 us (30%)
  Pallas kernels  24 us (27%)
  local copies, waits for them, and re-layouts  1.25 us (1%)
  between operations  0.97 us (1%)
    ppermute x19, starting transfers between devices, sent_to(): return lax.ppermute(value, AXES, pairs)  34 us
    ppermute x19, waiting for transfers between devices, sent_to(): return lax.ppermute(value, AXES, pairs)  26.7 us
    pallas_call x14, Pallas kernels, call(): pl.pallas_call(kernel, out_shape=shapes[0] if single else tuple(shapes),...  22.6 us
  transfers between devices with their start and end apart: 19, of which 10 were waited for; matrix products, arithmetic and copies ran while one was open for 0% of the time, Pallas kernels for 23%

profile of v5, /device:TPU:0, one launch (start us, length us, event | category | flops | bytes accessed | tf_op | source)
XLA Modules:
  0.0 87.6 jit_solution(16646074719875886507)
XLA Ops:
  0.6 0.0 copy-start
  0.6 0.0 copy-start.4
  0.6 1.3 %shard_map.86 = f32[1344,128]{1,0:T(8,128)S(1)} custom-call(f32[512,512]{1,0:T(8,128)} %bitcast.9, f32[16,512]{1,0:T(8,128)} %bitcast.16), custom_call_target="tpu_custom_call" | custom-call | tf_op jit(solution)/shard_map/pallas_call | solution.py:328
  2.0 0.0 copy-start.7
  2.0 0.7 collective-permute-start
  2.7 0.7 collective-permute-start.5
  3.5 0.0 copy-done
  3.5 0.0 copy-done.4
  3.5 0.0 copy-start.1
  3.5 1.2 %copy-done.1 = f32[1,512,512]{2,1,0:T(8,128)S(1)} copy-done((f32[1,512,512]{2,1,0:T(8,128)S(1)}, f32[1,512,512]{2,1,0:T(8,128)}, u32[]{:S(2)}) %copy-start.1) | copy-done | bytes 1048600
  4.7 4.1 %shard_map.88 = f32[1344,128]{1,0:T(8,128)S(1)} custom-call(f32[512,512]{1,0:T(8,128)S(1)} %bitcast.10, f32[16,512]{1,0:T(8,128)S(1)} %bitcast.17, f32[512,512]{1,0:T(8,128)S(1)} %bitcast.13), custom_call_target="tpu_custom_call" | custom-call | flops 483183808 | bytes 2818048 | tf_op jit(solution)/shard_map/pallas_call | solution.py:342
  8.8 0.0 copy-start.2
  8.8 1.4 %collective-permute-start.1 = (f32[1344,128]{1,0:T(8,128)S(1)}, f32[1344,128]{1,0:T(8,128)S(1)}, u32[]{:S(2)}, u32[]{:S(2)}) collective-permute-start(f32[1344,128]{1,0:T(8,128)S(1)} %shard_map.88), channel_id=1, source_target_pairs={{4,0},{5,1},{10,6},{11,7},{12,8},{13,9},{18,14},{19,15},{20,16},{2... | collective-permute-start | bytes 2064392 | tf_op jit(solution)/shard_map/ppermute | solution.py:373
  10.3 0.0 copy-done.7
  10.3 0.0 copy-done.3
  10.3 0.0 copy-done.5
  10.3 0.0 copy-done.6
  10.3 0.9 %shard_map.91.local.refs_4_ = f32[520,256]{1,0:T(8,128)S(1)} custom-call(s32[16]{0:T(128)S(1)} %copy-done.7, s32[1,1024]{1,0:T(1,128)S(1)} %bitcast.20, bf16[1024,256]{1,0:T(8,128)(2,1)S(1)} %copy-done.3, bf16[512,256]{1,0:T(8,128)(2,1)S(1)} %bitcast.19), custom_call_target="tpu_custom_call" | custom-call | flops 2516582 | bytes 1323072 | tf_op jit(solution)/shard_map/pallas_call | solution.py:342
  11.3 3.0 %collective-permute-start.6 = (f32[520,256]{1,0:T(8,128)S(1)}, f32[520,256]{1,0:T(8,128)S(1)}, u32[]{:S(2)}, u32[]{:S(2)}) collective-permute-start(f32[520,256]{1,0:T(8,128)S(1)} %shard_map.91.local.refs_4_), channel_id=1, source_target_pairs={{0,1},{1,0},{2,3},{3,2},{4,5},{5,4},{6,7},{7,6},{8,9},{9,8},{10,11... | collective-permute-start | bytes 1597448 | tf_op jit(solution)/shard_map/ppermute | solution.py:373
  14.3 1.3 %collective-permute-start.4 = (f32[512,512]{1,0:T(8,128)S(1)}, f32[512,512]{1,0:T(8,128)S(1)}, u32[]{:S(2)}, u32[]{:S(2)}) collective-permute-start(f32[512,512]{1,0:T(8,128)S(1)} %bitcast.14), channel_id=1, source_target_pairs={{4,0},{10,6},{13,9},{19,15},{21,17},{27,23},{28,24}} | collective-permute-start | bytes 3145736 | tf_op jit(solution)/shard_map/ppermute | solution.py:373
  15.6 0.0 collective-permute-done.packed
  15.6 4.1 %shard_map.87 = (f32[512,512]{1,0:T(8,128)S(1)}, f32[528,512]{1,0:T(8,128)S(1)}) custom-call(f32[1344,128]{1,0:T(8,128)S(1)} %collective-permute-done.packed, f32[512,512]{1,0:T(8,128)S(1)} %bitcast.15), custom_call_target="tpu_custom_call" | custom-call | flops 4831838208 | bytes 3866624 | tf_op jit(solution)/shard_map/pallas_call | solution.py:342
  19.7 0.0 collective-permute-done.1.above
  19.7 0.2 shard_map.89
  19.9 0.7 collective-permute-start.3
  20.6 3.9 %shard_map.90 = (f32[1344,128]{1,0:T(8,128)S(1)}, f32[8,128]{1,0:T(8,128)S(1)}) custom-call(f32[512,512]{1,0:T(8,128)S(1)} %get-tuple-element.36.block, f32[16,512]{1,0:T(8,128)S(1)} %get-tuple-element.37.thin, f32[512,512]{1,0:T(8,128)S(1)} %get-tuple-element.38.lower.through), custom_call_target="tpu_custom_call" | custom-call | flops 483183808 | bytes 2822144 | tf_op jit(solution)/shard_map/pallas_call | solution.py:342
  24.5 1.3 %collective-permute-start.2 = (f32[1344,128]{1,0:T(8,128)S(1)}, f32[1344,128]{1,0:T(8,128)S(1)}, u32[]{:S(2)}, u32[]{:S(2)}) collective-permute-start(f32[1344,128]{1,0:T(8,128)S(1)} %get-tuple-element.48), channel_id=1, source_target_pairs={{8,0},{14,6},{25,17},{31,23}} | collective-permute-start | bytes 2064392 | tf_op jit(solution)/shard_map/ppermute | solution.py:373
  25.8 0.0 collective-permute-done.6.other.refs_5_
  25.8 0.0 collective-permute-done.5.passed
  25.9 1.0 %shard_map.92.lower = f32[512,512]{1,0:T(8,128)S(1)} custom-call(f32[512,512]{1,0:T(8,128)S(1)} %get-tuple-element.38.lower.through, f32[512,512]{1,0:T(8,128)S(1)} %collective-permute-done.5.passed, f32[8,128]{1,0:T(8,128)S(1)} %get-tuple-element.45.after), custom_call_target="tpu_custom_call" | custom-call | flops 80530640 | bytes 3149824 | tf_op jit(solution)/shard_map/pallas_call | solution.py:342
  26.9 0.7 collective-permute-start.8
  27.6 0.9 %collective-permute-start.7 = (f32[1344,128]{1,0:T(8,128)S(1)}, f32[1344,128]{1,0:T(8,128)S(1)}, u32[]{:S(2)}, u32[]{:S(2)}) collective-permute-start(f32[1344,128]{1,0:T(8,128)S(1)} %get-tuple-element.48), channel_id=1, source_target_pairs={{17,9},{23,15}} | collective-permute-start | bytes 2064392 | tf_op jit(solution)/shard_map/ppermute | solution.py:373
  28.5 0.0 collective-permute-done.4.passed
  28.5 0.0 collective-permute-done.3.packed
  28.5 3.9 %shard_map.93 = (f32[512,512]{1,0:T(8,128)S(1)}, f32[528,512]{1,0:T(8,128)S(1)}) custom-call(f32[1344,128]{1,0:T(8,128)S(1)} %collective-permute-done.3.packed, f32[512,512]{1,0:T(8,128)S(1)} %shard_map.92.lower), custom_call_target="tpu_custom_call" | custom-call | flops 483183808 | bytes 3866624 | tf_op jit(solution)/shard_map/pallas_call | solution.py:342
  32.4 5.0 %collective-permute-done.2.early = f32[1344,128]{1,0:T(8,128)S(1)} collective-permute-done((f32[1344,128]{1,0:T(8,128)S(1)}, f32[1344,128]{1,0:T(8,128)S(1)}, u32[]{:S(2)}, u32[]{:S(2)}) %collective-permute-start.2) | collective-permute-done | bytes 688160 | tf_op jit(solution)/shard_map/ppermute | solution.py:373
  37.4 0.0 collective-permute-done.7.late
  37.4 2.1 %shard_map.95 = (f32[1344,128]{1,0:T(8,128)S(1)}, f32[512,512]{1,0:T(8,128)S(1)}, f32[16,512]{1,0:T(8,128)S(1)}) custom-call(f32[16,512]{1,0:T(8,128)S(1)} %get-tuple-element.47.after.thin, f32[1344,128]{1,0:T(8,128)S(1)} %collective-permute-done.2.early, f32[1344,128]{1,0:T(8,128)S(1)} %collective-permute-done.7.late, ...), custom_call_target="tpu_custom_call" | custom-call | flops 2415919104 | bytes 6389760 | tf_op jit(solution)/shard_map/pallas_call | solution.py:342
  39.5 0.0 collective-permute-done.8.passed
  39.5 11.9 %collective-permute-start.9 = (f32[1344,128]{1,0:T(8,128)S(1)}, f32[1344,128]{1,0:T(8,128)S(1)}, u32[]{:S(2)}, u32[]{:S(2)}) collective-permute-start(f32[1344,128]{1,0:T(8,128)S(1)} %get-tuple-element.50), channel_id=1, source_target_pairs={{0,17},{6,23},{9,24},{15,30}} | collective-permute-start | bytes 2064392 | tf_op jit(solution)/shard_map/ppermute | solution.py:373
  51.4 1.3 %collective-permute-start.10 = (f32[1344,128]{1,0:T(8,128)S(1)}, f32[1344,128]{1,0:T(8,128)S(1)}, u32[]{:S(2)}, u32[]{:S(2)}) collective-permute-start(f32[1344,128]{1,0:T(8,128)S(1)} %get-tuple-element.60), channel_id=1, source_target_pairs={{17,0},{23,6},{24,9},{30,15}} | collective-permute-start | bytes 2064392 | tf_op jit(solution)/shard_map/ppermute | solution.py:373
  52.7 7.1 %collective-permute-done.9.packed = f32[1344,128]{1,0:T(8,128)S(1)} collective-permute-done((f32[1344,128]{1,0:T(8,128)S(1)}, f32[1344,128]{1,0:T(8,128)S(1)}, u32[]{:S(2)}, u32[]{:S(2)}) %collective-permute-start.9) | collective-permute-done | bytes 688160 | tf_op jit(solution)/shard_map/ppermute | solution.py:373
  59.8 0.1 shard_map.97
  59.9 5.3 %collective-permute-done.10.above = f32[1344,128]{1,0:T(8,128)S(1)} collective-permute-done((f32[1344,128]{1,0:T(8,128)S(1)}, f32[1344,128]{1,0:T(8,128)S(1)}, u32[]{:S(2)}, u32[]{:S(2)}) %collective-permute-start.10) | collective-permute-done | bytes 688160 | tf_op jit(solution)/shard_map/ppermute | solution.py:373
  65.2 1.9 %shard_map.98.a = f32[16,512]{1,0:T(8,128)S(1)} custom-call(f32[512,512]{1,0:T(8,128)S(1)} %get-tuple-element.58.block, f32[16,512]{1,0:T(8,128)S(1)} %get-tuple-element.59.thin, f32[1344,128]{1,0:T(8,128)S(1)} %collective-permute-done.10.above), custom_call_target="tpu_custom_call" | custom-call | flops 80530640 | bytes 1802240 | tf_op jit(solution)/shard_map/pallas_call | solution.py:342
  67.0 1.3 %collective-permute-start.11 = (f32[16,512]{1,0:T(8,128)S(1)}, f32[16,512]{1,0:T(8,128)S(1)}, u32[]{:S(2)}, u32[]{:S(2)}) collective-permute-start(f32[16,512]{1,0:T(8,128)S(1)} %shard_map.98.a), channel_id=1, source_target_pairs={{0,1},{6,7},{9,10},{15,12},{17,18},{23,20},{24,25},{30,31}} | collective-permute-start | bytes 98312 | tf_op jit(solution)/shard_map/ppermute | solution.py:373
  68.3 1.3 %collective-permute-start.12 = (f32[16,512]{1,0:T(8,128)S(1)}, f32[16,512]{1,0:T(8,128)S(1)}, u32[]{:S(2)}, u32[]{:S(2)}) collective-permute-start(f32[16,512]{1,0:T(8,128)S(1)} %shard_map.98.a), channel_id=1, source_target_pairs={{0,2},{6,4},{9,11},{15,13},{17,19},{23,21},{24,26},{30,28}} | collective-permute-start | bytes 98312 | tf_op jit(solution)/shard_map/ppermute | solution.py:373
  69.6 1.3 %collective-permute-start.13 = (f32[16,512]{1,0:T(8,128)S(1)}, f32[16,512]{1,0:T(8,128)S(1)}, u32[]{:S(2)}, u32[]{:S(2)}) collective-permute-start(f32[16,512]{1,0:T(8,128)S(1)} %shard_map.98.a), channel_id=1, source_target_pairs={{0,3},{6,5},{9,8},{15,14},{17,16},{23,22},{24,27},{30,29}} | collective-permute-start | bytes 98312 | tf_op jit(solution)/shard_map/ppermute | solution.py:373
  70.9 0.0 collective-permute-done.11.b
  71.0 0.3 collective-permute-done.12.c
  71.2 1.3 %collective-permute-done.13.d = f32[16,512]{1,0:T(8,128)S(1)} collective-permute-done((f32[16,512]{1,0:T(8,128)S(1)}, f32[16,512]{1,0:T(8,128)S(1)}, u32[]{:S(2)}, u32[]{:S(2)}) %collective-permute-start.13) | collective-permute-done | bytes 32800 | tf_op jit(solution)/shard_map/ppermute | solution.py:373
  72.5 0.2 shard_map.99
  72.7 0.5 collective-permute-start.14
  73.3 0.9 %collective-permute-done.14 = f32[32,512]{1,0:T(8,128)S(1)} collective-permute-done((f32[32,512]{1,0:T(8,128)S(1)}, f32[32,512]{1,0:T(8,128)S(1)}, u32[]{:S(2)}, u32[]{:S(2)}) %collective-permute-start.14) | collective-permute-done | bytes 65568 | tf_op jit(solution)/shard_map/ppermute | solution.py:373
  74.2 1.9 %collective-permute-start.15 = (f32[32,512]{1,0:T(8,128)S(1)}, f32[32,512]{1,0:T(8,128)S(1)}, u32[]{:S(2)}, u32[]{:S(2)}) collective-permute-start(f32[32,512]{1,0:T(8,128)S(1)} %add.10.refs_0_), channel_id=1, source_target_pairs={{0,8},{1,9},{2,10},{3,11},{4,12},{5,13},{6,14},{7,15},{8,0},{9,1},... | collective-permute-start | bytes 196616 | tf_op jit(solution)/shard_map/ppermute | solution.py:373
  76.1 0.9 %collective-permute-start.16 = (f32[32,512]{1,0:T(8,128)S(1)}, f32[32,512]{1,0:T(8,128)S(1)}, u32[]{:S(2)}, u32[]{:S(2)}) collective-permute-start(f32[32,512]{1,0:T(8,128)S(1)} %add.10.refs_0_), channel_id=1, source_target_pairs={{0,16},{1,17},{2,18},{3,19},{4,20},{5,21},{6,22},{7,23},{8,24},{9,... | collective-permute-start | bytes 196616 | tf_op jit(solution)/shard_map/ppermute | solution.py:373
  77.0 1.4 %collective-permute-start.17 = (f32[32,512]{1,0:T(8,128)S(1)}, f32[32,512]{1,0:T(8,128)S(1)}, u32[]{:S(2)}, u32[]{:S(2)}) collective-permute-start(f32[32,512]{1,0:T(8,128)S(1)} %add.10.refs_0_), channel_id=1, source_target_pairs={{0,24},{1,25},{2,26},{3,27},{4,28},{5,29},{6,30},{7,31},{8,16},{9,... | collective-permute-start | bytes 196616 | tf_op jit(solution)/shard_map/ppermute | solution.py:373
  78.4 0.2 collective-permute-done.15.refs_1_
  78.6 1.7 %collective-permute-done.16.refs_2_ = f32[32,512]{1,0:T(8,128)S(1)} collective-permute-done((f32[32,512]{1,0:T(8,128)S(1)}, f32[32,512]{1,0:T(8,128)S(1)}, u32[]{:S(2)}, u32[]{:S(2)}) %collective-permute-start.16) | collective-permute-done | bytes 65568 | tf_op jit(solution)/shard_map/ppermute | solution.py:373
  80.3 1.8 %collective-permute-done.17.refs_3_ = f32[32,512]{1,0:T(8,128)S(1)} collective-permute-done((f32[32,512]{1,0:T(8,128)S(1)}, f32[32,512]{1,0:T(8,128)S(1)}, u32[]{:S(2)}, u32[]{:S(2)}) %collective-permute-start.17) | collective-permute-done | bytes 65568 | tf_op jit(solution)/shard_map/ppermute | solution.py:373
  82.1 0.2 shard_map.100
  82.4 1.4 %collective-permute-start.18 = (f32[16,128]{1,0:T(8,128)S(1)}, f32[16,128]{1,0:T(8,128)S(1)}, u32[]{:S(2)}, u32[]{:S(2)}) collective-permute-start(f32[16,128]{1,0:T(8,128)S(1)} %get-tuple-element.65), channel_id=1, source_target_pairs={{0,2},{1,3},{2,0},{3,1},{4,6},{5,7},{6,4},{7,5},{8,10},{9,11},{10,... | collective-permute-start | bytes 24584 | tf_op jit(solution)/shard_map/ppermute | solution.py:373
  83.8 3.1 %collective-permute-done.18 = f32[16,128]{1,0:T(8,128)S(1)} collective-permute-done((f32[16,128]{1,0:T(8,128)S(1)}, f32[16,128]{1,0:T(8,128)S(1)}, u32[]{:S(2)}, u32[]{:S(2)}) %collective-permute-start.18) | collective-permute-done | bytes 8224 | tf_op jit(solution)/shard_map/ppermute | solution.py:373
  86.9 0.6 subtract_bitcast_fusion
  (7 shorter events, 0.0 us)
Async XLA Ops:
  0.6 2.8 %copy-start = (f32[1,512,512]{2,1,0:T(8,128)S(1)}, f32[1,512,512]{2,1,0:T(8,128)}, u32[]{:S(2)}) copy-start(f32[1,512,512]{2,1,0:T(8,128)} %param.8) | copy-start | bytes 3145732
  0.6 2.8 %copy-start.4 = (f32[1,16,512]{2,1,0:T(8,128)S(1)}, f32[1,16,512]{2,1,0:T(8,128)}, u32[]{:S(2)}) copy-start(f32[1,16,512]{2,1,0:T(8,128)} %param.9) | copy-start | bytes 98308
  2.0 8.3 %copy-start.7 = (s32[16]{0:T(128)S(1)}, s32[16]{0:T(128)}, u32[]{:S(2)}) copy-start(s32[16]{0:T(128)} %regime.1) | copy-start | bytes 196
  2.0 13.6 %collective-permute-start = (f32[1344,128]{1,0:T(8,128)S(1)}, f32[1344,128]{1,0:T(8,128)S(1)}, u32[]{:S(2)}, u32[]{:S(2)}) collective-permute-start(f32[1344,128]{1,0:T(8,128)S(1)} %shard_map.86), channel_id=1, source_target_pairs={{2,6},{3,7},{4,8},{5,9},{10,14},{11,15},{12,16},{13,17},{18,22},{1... | collective-permute-start | bytes 2064392 | tf_op jit(solution)/shard_map/ppermute | solution.py:373
  2.7 23.1 %collective-permute-start.5 = (f32[512,512]{1,0:T(8,128)}, f32[512,512]{1,0:T(8,128)S(1)}, u32[]{:S(2)}, u32[]{:S(2)}) collective-permute-start(f32[512,512]{1,0:T(8,128)} %bitcast.12), channel_id=1, source_target_pairs={{5,9},{11,15},{12,16},{13,17},{18,22},{19,23},{20,24},{26,30}} | collective-permute-start | bytes 3145736 | tf_op jit(solution)/shard_map/ppermute | solution.py:373
  3.5 1.2 %copy-start.1 = (f32[1,512,512]{2,1,0:T(8,128)S(1)}, f32[1,512,512]{2,1,0:T(8,128)}, u32[]{:S(2)}) copy-start(f32[1,512,512]{2,1,0:T(8,128)} %param.7) | copy-start | bytes 3145732
  4.7 5.6 %copy-start.3 = (bf16[1024,256]{1,0:T(8,128)(2,1)S(1)}, bf16[1024,256]{1,0:T(8,128)(2,1)}, u32[]{:S(2)}) copy-start(bf16[1024,256]{1,0:T(8,128)(2,1)} %participation.1) | copy-start | bytes 1572868
  4.7 5.6 %copy-start.5 = (bf16[1,512,256]{2,1,0:T(8,128)(2,1)S(1)}, bf16[1,512,256]{2,1,0:T(8,128)(2,1)}, u32[]{:S(2)}) copy-start(bf16[1,512,256]{2,1,0:T(8,128)(2,1)} %param.10) | copy-start | bytes 786436
  4.7 5.6 %copy-start.6 = (s32[1024]{0:T(1024)S(1)}, s32[1024]{0:T(1024)}, u32[]{:S(2)}) copy-start(s32[1024]{0:T(1024)} %param.11) | copy-start | bytes 12292
  8.8 5.5 %copy-start.2 = (f32[1,512,512]{2,1,0:T(8,128)S(1)}, f32[1,512,512]{2,1,0:T(8,128)}, u32[]{:S(2)}) copy-start(f32[1,512,512]{2,1,0:T(8,128)} %param.7) | copy-start | bytes 3145732
  8.8 10.9 %collective-permute-start.1 = (f32[1344,128]{1,0:T(8,128)S(1)}, f32[1344,128]{1,0:T(8,128)S(1)}, u32[]{:S(2)}, u32[]{:S(2)}) collective-permute-start(f32[1344,128]{1,0:T(8,128)S(1)} %shard_map.88), channel_id=1, source_target_pairs={{4,0},{5,1},{10,6},{11,7},{12,8},{13,9},{18,14},{19,15},{20,16},{2... | collective-permute-start | bytes 2064392 | tf_op jit(solution)/shard_map/ppermute | solution.py:373
  11.3 14.6 %collective-permute-start.6 = (f32[520,256]{1,0:T(8,128)S(1)}, f32[520,256]{1,0:T(8,128)S(1)}, u32[]{:S(2)}, u32[]{:S(2)}) collective-permute-start(f32[520,256]{1,0:T(8,128)S(1)} %shard_map.91.local.refs_4_), channel_id=1, source_target_pairs={{0,1},{1,0},{2,3},{3,2},{4,5},{5,4},{6,7},{7,6},{8,9},{9,8},{10,11... | collective-permute-start | bytes 1597448 | tf_op jit(solution)/shard_map/ppermute | solution.py:373
  14.3 14.2 %collective-permute-start.4 = (f32[512,512]{1,0:T(8,128)S(1)}, f32[512,512]{1,0:T(8,128)S(1)}, u32[]{:S(2)}, u32[]{:S(2)}) collective-permute-start(f32[512,512]{1,0:T(8,128)S(1)} %bitcast.14), channel_id=1, source_target_pairs={{4,0},{10,6},{13,9},{19,15},{21,17},{27,23},{28,24}} | collective-permute-start | bytes 3145736 | tf_op jit(solution)/shard_map/ppermute | solution.py:373
  19.9 8.6 %collective-permute-start.3 = (f32[1344,128]{1,0:T(8,128)S(1)}, f32[1344,128]{1,0:T(8,128)S(1)}, u32[]{:S(2)}, u32[]{:S(2)}) collective-permute-start(f32[1344,128]{1,0:T(8,128)S(1)} %get-tuple-element.40), channel_id=1, source_target_pairs={{1,9},{7,15},{9,17},{15,23},{16,24},{22,30}} | collective-permute-start | bytes 2064392 | tf_op jit(solution)/shard_map/ppermute | solution.py:373
  24.5 12.8 %collective-permute-start.2 = (f32[1344,128]{1,0:T(8,128)S(1)}, f32[1344,128]{1,0:T(8,128)S(1)}, u32[]{:S(2)}, u32[]{:S(2)}) collective-permute-start(f32[1344,128]{1,0:T(8,128)S(1)} %get-tuple-element.48), channel_id=1, source_target_pairs={{8,0},{14,6},{25,17},{31,23}} | collective-permute-start | bytes 2064392 | tf_op jit(solution)/shard_map/ppermute | solution.py:373
  26.9 12.6 %collective-permute-start.8 = (f32[512,512]{1,0:T(8,128)S(1)}, f32[512,512]{1,0:T(8,128)S(1)}, u32[]{:S(2)}, u32[]{:S(2)}) collective-permute-start(f32[512,512]{1,0:T(8,128)S(1)} %shard_map.92.lower), channel_id=1, source_target_pairs={{9,17},{15,23},{16,24},{22,30}} | collective-permute-start | bytes 3145736 | tf_op jit(solution)/shard_map/ppermute | solution.py:373
  27.6 9.8 %collective-permute-start.7 = (f32[1344,128]{1,0:T(8,128)S(1)}, f32[1344,128]{1,0:T(8,128)S(1)}, u32[]{:S(2)}, u32[]{:S(2)}) collective-permute-start(f32[1344,128]{1,0:T(8,128)S(1)} %get-tuple-element.48), channel_id=1, source_target_pairs={{17,9},{23,15}} | collective-permute-start | bytes 2064392 | tf_op jit(solution)/shard_map/ppermute | solution.py:373
  39.5 20.3 %collective-permute-start.9 = (f32[1344,128]{1,0:T(8,128)S(1)}, f32[1344,128]{1,0:T(8,128)S(1)}, u32[]{:S(2)}, u32[]{:S(2)}) collective-permute-start(f32[1344,128]{1,0:T(8,128)S(1)} %get-tuple-element.50), channel_id=1, source_target_pairs={{0,17},{6,23},{9,24},{15,30}} | collective-permute-start | bytes 2064392 | tf_op jit(solution)/shard_map/ppermute | solution.py:373
  51.4 13.7 %collective-permute-start.10 = (f32[1344,128]{1,0:T(8,128)S(1)}, f32[1344,128]{1,0:T(8,128)S(1)}, u32[]{:S(2)}, u32[]{:S(2)}) collective-permute-start(f32[1344,128]{1,0:T(8,128)S(1)} %get-tuple-element.60), channel_id=1, source_target_pairs={{17,0},{23,6},{24,9},{30,15}} | collective-permute-start | bytes 2064392 | tf_op jit(solution)/shard_map/ppermute | solution.py:373
  67.0 3.9 %collective-permute-start.11 = (f32[16,512]{1,0:T(8,128)S(1)}, f32[16,512]{1,0:T(8,128)S(1)}, u32[]{:S(2)}, u32[]{:S(2)}) collective-permute-start(f32[16,512]{1,0:T(8,128)S(1)} %shard_map.98.a), channel_id=1, source_target_pairs={{0,1},{6,7},{9,10},{15,12},{17,18},{23,20},{24,25},{30,31}} | collective-permute-start | bytes 98312 | tf_op jit(solution)/shard_map/ppermute | solution.py:373
  68.3 2.9 %collective-permute-start.12 = (f32[16,512]{1,0:T(8,128)S(1)}, f32[16,512]{1,0:T(8,128)S(1)}, u32[]{:S(2)}, u32[]{:S(2)}) collective-permute-start(f32[16,512]{1,0:T(8,128)S(1)} %shard_map.98.a), channel_id=1, source_target_pairs={{0,2},{6,4},{9,11},{15,13},{17,19},{23,21},{24,26},{30,28}} | collective-permute-start | bytes 98312 | tf_op jit(solution)/shard_map/ppermute | solution.py:373
  69.6 2.9 %collective-permute-start.13 = (f32[16,512]{1,0:T(8,128)S(1)}, f32[16,512]{1,0:T(8,128)S(1)}, u32[]{:S(2)}, u32[]{:S(2)}) collective-permute-start(f32[16,512]{1,0:T(8,128)S(1)} %shard_map.98.a), channel_id=1, source_target_pairs={{0,3},{6,5},{9,8},{15,14},{17,16},{23,22},{24,27},{30,29}} | collective-permute-start | bytes 98312 | tf_op jit(solution)/shard_map/ppermute | solution.py:373
  72.7 1.4 %collective-permute-start.14 = (f32[32,512]{1,0:T(8,128)S(1)}, f32[32,512]{1,0:T(8,128)S(1)}, u32[]{:S(2)}, u32[]{:S(2)}) collective-permute-start(f32[32,512]{1,0:T(8,128)S(1)} %get-tuple-element.63), channel_id=1, source_target_pairs={{0,4},{1,5},{2,6},{3,7},{4,0},{5,1},{6,2},{7,3},{8,12},{9,13},{10,... | collective-permute-start | bytes 196616 | tf_op jit(solution)/shard_map/ppermute | solution.py:373
  74.2 4.4 %collective-permute-start.15 = (f32[32,512]{1,0:T(8,128)S(1)}, f32[32,512]{1,0:T(8,128)S(1)}, u32[]{:S(2)}, u32[]{:S(2)}) collective-permute-start(f32[32,512]{1,0:T(8,128)S(1)} %add.10.refs_0_), channel_id=1, source_target_pairs={{0,8},{1,9},{2,10},{3,11},{4,12},{5,13},{6,14},{7,15},{8,0},{9,1},... | collective-permute-start | bytes 196616 | tf_op jit(solution)/shard_map/ppermute | solution.py:373
  76.1 4.3 %collective-permute-start.16 = (f32[32,512]{1,0:T(8,128)S(1)}, f32[32,512]{1,0:T(8,128)S(1)}, u32[]{:S(2)}, u32[]{:S(2)}) collective-permute-start(f32[32,512]{1,0:T(8,128)S(1)} %add.10.refs_0_), channel_id=1, source_target_pairs={{0,16},{1,17},{2,18},{3,19},{4,20},{5,21},{6,22},{7,23},{8,24},{9,... | collective-permute-start | bytes 196616 | tf_op jit(solution)/shard_map/ppermute | solution.py:373
  77.0 5.2 %collective-permute-start.17 = (f32[32,512]{1,0:T(8,128)S(1)}, f32[32,512]{1,0:T(8,128)S(1)}, u32[]{:S(2)}, u32[]{:S(2)}) collective-permute-start(f32[32,512]{1,0:T(8,128)S(1)} %add.10.refs_0_), channel_id=1, source_target_pairs={{0,24},{1,25},{2,26},{3,27},{4,28},{5,29},{6,30},{7,31},{8,16},{9,... | collective-permute-start | bytes 196616 | tf_op jit(solution)/shard_map/ppermute | solution.py:373
  82.4 4.6 %collective-permute-start.18 = (f32[16,128]{1,0:T(8,128)S(1)}, f32[16,128]{1,0:T(8,128)S(1)}, u32[]{:S(2)}, u32[]{:S(2)}) collective-permute-start(f32[16,128]{1,0:T(8,128)S(1)} %get-tuple-element.65), channel_id=1, source_target_pairs={{0,2},{1,3},{2,0},{3,1},{4,6},{5,7},{6,4},{7,5},{8,10},{9,11},{10,... | collective-permute-start | bytes 24584 | tf_op jit(solution)/shard_map/ppermute | solution.py:373

commit v6 on v5

--- a/solution.py
+++ b/solution.py
@@ -133,10 +133,11 @@
         packed[start : start + rows, :] = value
 
 
-def first_own_kernel(block, thin, lower_hbm, packed, stack, out, lower, sem):
+def first_own_kernel(both, lower_hbm, packed, stack, out, lower, whole, thin, sem):
     copy = pltpu.make_async_copy(lower_hbm, lower, sem)
     copy.start()
-    own_kernel(block, thin, lower, packed, stack, out, copy)
+    unpack(both, whole, thin)
+    own_kernel(whole, thin, lower, packed, stack, out, copy)
 
 
 def own_kernel(block, thin, lower, packed, stack, out, copy=None):
@@ -172,8 +173,9 @@
     through[...] = half[0:size, :]
 
 
-def fold_kernel(block, thin, full, above, packed, block_out, thin_out):
-    folded(packed, block, thin, full, above)
+def fold_kernel(both, full, above, packed, block_out, thin_out):
+    unpack(both, block_out, thin_out)
+    folded(packed, block_out, thin_out, full, above)
     unpack(packed, block_out, thin_out)
 
 
@@ -400,9 +402,9 @@
             parts = [value] + [sent_to(value, lambda s, m, k=k: (s ^ k, m)) for k in steps]
         return parts
 
-    packed_down = packed_from_hbm(block, thin, packed)
-    lower_sent, packed_down = lax.optimization_barrier((lower, packed_down))
-    packed_down = sent_to(packed_down, lambda s, m: (s + 1, m) if parity(s + 1, m) else None)
+    first = packed_from_hbm(block, thin, packed)
+    lower_sent, first = lax.optimization_barrier((lower, first))
+    packed_down = sent_to(first, lambda s, m: (s + 1, m) if parity(s + 1, m) else None)
 
     def needs_lower(s, m):
         return m == home(s) or (s + 2 < sections and m == home(s + 2))
@@ -410,14 +412,19 @@
     lower_down = sent_to(lower_sent, lambda s, m: (s + 1, m) if s >= 1 and needs_lower(s + 1, m) else None)
     lower_up = sent_to(lower_sent, lambda s, m: (s - 1, m) if s >= 1 and m == home(s - 1) else None)
     up = call(
-        first_own_kernel, [packed], [stacked, stacked, square], (block, thin, lower), 6 * product, hbm=1
+        first_own_kernel,
+        [packed],
+        [stacked, stacked, square, square, thin_shape],
+        (first, lower),
+        6 * product,
+        hbm=1,
     )
     up = sent_to(up, lambda s, m: (s - 1, m) if parity(s - 1, m) else None)
     other = sent_to(local, lambda s, m: (s, m ^ 1))
     through, full = call(
         first_receive_kernel, [square, stacked], [stacked, square, square], (packed_down, lower), 6 * long, hbm=1
     )
-    sent, block, thin = call(fold_kernel, [packed, square, thin_shape], [], (block, thin, full, up), 0)
+    sent, block, thin = call(fold_kernel, [packed, square, thin_shape], [], (first, full, up), 0)
 
     packed_down = sent_to(sent, lambda s, m: (s + 2, m) if m == home(s + 2) else None)
     up, done = call(

time: 87.9 us -> 87.9 us (level)
  local copies, waits for them, and re-layouts: 1.25 us -> 0.03 us
    unnamed x16 -> x10, local copies, waits for them, and re-layouts: 1.25 us -> 0.03 us
where the time goes in v6:
time: 87.9 us; the launch traced here: 87.6 us
  starting transfers between devices  34.5 us (39%)
  waiting for transfers between devices  27.5 us (31%)
  Pallas kernels  24.1 us (27%)
  between operations  0.96 us (1%)
    ppermute x19, starting transfers between devices, sent_to(): return lax.ppermute(value, AXES, pairs)  34.5 us
    ppermute x19, waiting for transfers between devices, sent_to(): return lax.ppermute(value, AXES, pairs)  27.5 us
    pallas_call x14, Pallas kernels, call(): pl.pallas_call(kernel, out_shape=shapes[0] if single else tuple(shapes),...  22.8 us
  transfers between devices with their start and end apart: 19, of which 10 were waited for; matrix products, arithmetic and copies ran while one was open for 0% of the time, Pallas kernels for 23%

profile of v6, /device:TPU:0, one launch (start us, length us, event | category | flops | bytes accessed | tf_op | source)
XLA Modules:
  0.0 87.6 jit_solution(7633501077989395102)
XLA Ops:
  0.6 0.0 copy-start
  0.6 1.3 %shard_map.86.both = f32[1344,128]{1,0:T(8,128)S(1)} custom-call(f32[512,512]{1,0:T(8,128)} %bitcast.15, f32[16,512]{1,0:T(8,128)} %bitcast.16), custom_call_target="tpu_custom_call" | custom-call | tf_op jit(solution)/shard_map/pallas_call | solution.py:330
  2.0 0.0 copy-start.1
  2.0 0.0 copy-start.2
  2.0 0.0 copy-start.3
  2.0 0.0 copy-start.4
  2.0 0.8 collective-permute-start
  2.9 0.0 copy-done
  2.9 0.7 collective-permute-start.5
  3.6 4.1 %shard_map.88 = f32[1344,128]{1,0:T(8,128)S(1)} custom-call(f32[1344,128]{1,0:T(8,128)S(1)} %shard_map.86.both, f32[512,512]{1,0:T(8,128)S(1)} %bitcast.10), custom_call_target="tpu_custom_call" | custom-call | flops 483183808 | bytes 2424832 | tf_op jit(solution)/shard_map/pallas_call | solution.py:344
  7.7 1.3 %collective-permute-start.1 = (f32[1344,128]{1,0:T(8,128)S(1)}, f32[1344,128]{1,0:T(8,128)S(1)}, u32[]{:S(2)}, u32[]{:S(2)}) collective-permute-start(f32[1344,128]{1,0:T(8,128)S(1)} %shard_map.88), channel_id=1, source_target_pairs={{4,0},{5,1},{10,6},{11,7},{12,8},{13,9},{18,14},{19,15},{20,16},{2... | collective-permute-start | bytes 2064392 | tf_op jit(solution)/shard_map/ppermute | solution.py:375
  9.0 0.0 copy-done.1
  9.1 0.0 copy-done.2
  9.1 0.0 copy-done.3
  9.1 0.0 copy-done.4
  9.1 0.9 %shard_map.91.local.refs_4_ = f32[520,256]{1,0:T(8,128)S(1)} custom-call(s32[16]{0:T(128)S(1)} %copy-done.4, s32[1,1024]{1,0:T(1,128)S(1)} %bitcast.14, bf16[1024,256]{1,0:T(8,128)(2,1)S(1)} %copy-done.1, bf16[512,256]{1,0:T(8,128)(2,1)S(1)} %bitcast.13), custom_call_target="tpu_custom_call" | custom-call | flops 2516582 | bytes 1323072 | tf_op jit(solution)/shard_map/pallas_call | solution.py:344
  10.0 3.0 %collective-permute-start.6 = (f32[520,256]{1,0:T(8,128)S(1)}, f32[520,256]{1,0:T(8,128)S(1)}, u32[]{:S(2)}, u32[]{:S(2)}) collective-permute-start(f32[520,256]{1,0:T(8,128)S(1)} %shard_map.91.local.refs_4_), channel_id=1, source_target_pairs={{0,1},{1,0},{2,3},{3,2},{4,5},{5,4},{6,7},{7,6},{8,9},{9,8},{10,11... | collective-permute-start | bytes 1597448 | tf_op jit(solution)/shard_map/ppermute | solution.py:375
  13.1 1.3 %collective-permute-start.4 = (f32[512,512]{1,0:T(8,128)S(1)}, f32[512,512]{1,0:T(8,128)S(1)}, u32[]{:S(2)}, u32[]{:S(2)}) collective-permute-start(f32[512,512]{1,0:T(8,128)S(1)} %bitcast.11), channel_id=1, source_target_pairs={{4,0},{10,6},{13,9},{19,15},{21,17},{27,23},{28,24}} | collective-permute-start | bytes 3145736 | tf_op jit(solution)/shard_map/ppermute | solution.py:375
  14.4 0.0 collective-permute-done.packed
  14.4 4.1 %shard_map.87 = (f32[512,512]{1,0:T(8,128)S(1)}, f32[528,512]{1,0:T(8,128)S(1)}) custom-call(f32[1344,128]{1,0:T(8,128)S(1)} %collective-permute-done.packed, f32[512,512]{1,0:T(8,128)S(1)} %bitcast.12), custom_call_target="tpu_custom_call" | custom-call | flops 4831838208 | bytes 3866624 | tf_op jit(solution)/shard_map/pallas_call | solution.py:344
  18.5 0.0 collective-permute-done.1.above
  18.5 0.3 shard_map.89
  18.8 0.7 collective-permute-start.3
  19.5 3.9 %shard_map.90 = (f32[1344,128]{1,0:T(8,128)S(1)}, f32[8,128]{1,0:T(8,128)S(1)}) custom-call(f32[512,512]{1,0:T(8,128)S(1)} %get-tuple-element.36.block, f32[16,512]{1,0:T(8,128)S(1)} %get-tuple-element.37.thin, f32[512,512]{1,0:T(8,128)S(1)} %get-tuple-element.38.lower.through), custom_call_target="tpu_custom_call" | custom-call | flops 483183808 | bytes 2822144 | tf_op jit(solution)/shard_map/pallas_call | solution.py:344
  23.4 1.3 %collective-permute-start.2 = (f32[1344,128]{1,0:T(8,128)S(1)}, f32[1344,128]{1,0:T(8,128)S(1)}, u32[]{:S(2)}, u32[]{:S(2)}) collective-permute-start(f32[1344,128]{1,0:T(8,128)S(1)} %get-tuple-element.48), channel_id=1, source_target_pairs={{8,0},{14,6},{25,17},{31,23}} | collective-permute-start | bytes 2064392 | tf_op jit(solution)/shard_map/ppermute | solution.py:375
  24.7 0.0 collective-permute-done.6.other.refs_5_
  24.7 0.0 collective-permute-done.5.passed
  24.8 1.0 %shard_map.92.lower = f32[512,512]{1,0:T(8,128)S(1)} custom-call(f32[512,512]{1,0:T(8,128)S(1)} %get-tuple-element.38.lower.through, f32[512,512]{1,0:T(8,128)S(1)} %collective-permute-done.5.passed, f32[8,128]{1,0:T(8,128)S(1)} %get-tuple-element.45.after), custom_call_target="tpu_custom_call" | custom-call | flops 80530640 | bytes 3149824 | tf_op jit(solution)/shard_map/pallas_call | solution.py:344
  25.8 0.9 %collective-permute-start.8 = (f32[512,512]{1,0:T(8,128)S(1)}, f32[512,512]{1,0:T(8,128)S(1)}, u32[]{:S(2)}, u32[]{:S(2)}) collective-permute-start(f32[512,512]{1,0:T(8,128)S(1)} %shard_map.92.lower), channel_id=1, source_target_pairs={{9,17},{15,23},{16,24},{22,30}} | collective-permute-start | bytes 3145736 | tf_op jit(solution)/shard_map/ppermute | solution.py:375
  26.7 0.7 collective-permute-start.7
  27.4 0.0 collective-permute-done.4.passed
  27.4 0.0 collective-permute-done.3.packed
  27.4 3.9 %shard_map.93 = (f32[512,512]{1,0:T(8,128)S(1)}, f32[528,512]{1,0:T(8,128)S(1)}) custom-call(f32[1344,128]{1,0:T(8,128)S(1)} %collective-permute-done.3.packed, f32[512,512]{1,0:T(8,128)S(1)} %shard_map.92.lower), custom_call_target="tpu_custom_call" | custom-call | flops 483183808 | bytes 3866624 | tf_op jit(solution)/shard_map/pallas_call | solution.py:344
  31.3 5.3 %collective-permute-done.2.early = f32[1344,128]{1,0:T(8,128)S(1)} collective-permute-done((f32[1344,128]{1,0:T(8,128)S(1)}, f32[1344,128]{1,0:T(8,128)S(1)}, u32[]{:S(2)}, u32[]{:S(2)}) %collective-permute-start.2) | collective-permute-done | bytes 688160 | tf_op jit(solution)/shard_map/ppermute | solution.py:375
  36.6 0.0 collective-permute-done.7.late
  36.6 2.1 %shard_map.95 = (f32[1344,128]{1,0:T(8,128)S(1)}, f32[512,512]{1,0:T(8,128)S(1)}, f32[16,512]{1,0:T(8,128)S(1)}) custom-call(f32[16,512]{1,0:T(8,128)S(1)} %get-tuple-element.47.after.thin, f32[1344,128]{1,0:T(8,128)S(1)} %collective-permute-done.2.early, f32[1344,128]{1,0:T(8,128)S(1)} %collective-permute-done.7.late, ...), custom_call_target="tpu_custom_call" | custom-call | flops 2415919104 | bytes 6389760 | tf_op jit(solution)/shard_map/pallas_call | solution.py:344
  38.7 0.0 collective-permute-done.8.passed
  38.7 12.7 %collective-permute-start.9 = (f32[1344,128]{1,0:T(8,128)S(1)}, f32[1344,128]{1,0:T(8,128)S(1)}, u32[]{:S(2)}, u32[]{:S(2)}) collective-permute-start(f32[1344,128]{1,0:T(8,128)S(1)} %get-tuple-element.50), channel_id=1, source_target_pairs={{0,17},{6,23},{9,24},{15,30}} | collective-permute-start | bytes 2064392 | tf_op jit(solution)/shard_map/ppermute | solution.py:375
  51.5 1.3 %collective-permute-start.10 = (f32[1344,128]{1,0:T(8,128)S(1)}, f32[1344,128]{1,0:T(8,128)S(1)}, u32[]{:S(2)}, u32[]{:S(2)}) collective-permute-start(f32[1344,128]{1,0:T(8,128)S(1)} %get-tuple-element.60), channel_id=1, source_target_pairs={{17,0},{23,6},{24,9},{30,15}} | collective-permute-start | bytes 2064392 | tf_op jit(solution)/shard_map/ppermute | solution.py:375
  52.8 7.1 %collective-permute-done.9.packed = f32[1344,128]{1,0:T(8,128)S(1)} collective-permute-done((f32[1344,128]{1,0:T(8,128)S(1)}, f32[1344,128]{1,0:T(8,128)S(1)}, u32[]{:S(2)}, u32[]{:S(2)}) %collective-permute-start.9) | collective-permute-done | bytes 688160 | tf_op jit(solution)/shard_map/ppermute | solution.py:375
  59.9 0.1 shard_map.97
  59.9 5.3 %collective-permute-done.10.above = f32[1344,128]{1,0:T(8,128)S(1)} collective-permute-done((f32[1344,128]{1,0:T(8,128)S(1)}, f32[1344,128]{1,0:T(8,128)S(1)}, u32[]{:S(2)}, u32[]{:S(2)}) %collective-permute-start.10) | collective-permute-done | bytes 688160 | tf_op jit(solution)/shard_map/ppermute | solution.py:375
  65.2 1.9 %shard_map.98.a = f32[16,512]{1,0:T(8,128)S(1)} custom-call(f32[512,512]{1,0:T(8,128)S(1)} %get-tuple-element.58.block, f32[16,512]{1,0:T(8,128)S(1)} %get-tuple-element.59.thin, f32[1344,128]{1,0:T(8,128)S(1)} %collective-permute-done.10.above), custom_call_target="tpu_custom_call" | custom-call | flops 80530640 | bytes 1802240 | tf_op jit(solution)/shard_map/pallas_call | solution.py:344
  67.1 1.3 %collective-permute-start.11 = (f32[16,512]{1,0:T(8,128)S(1)}, f32[16,512]{1,0:T(8,128)S(1)}, u32[]{:S(2)}, u32[]{:S(2)}) collective-permute-start(f32[16,512]{1,0:T(8,128)S(1)} %shard_map.98.a), channel_id=1, source_target_pairs={{0,1},{6,7},{9,10},{15,12},{17,18},{23,20},{24,25},{30,31}} | collective-permute-start | bytes 98312 | tf_op jit(solution)/shard_map/ppermute | solution.py:375
  68.4 1.3 %collective-permute-start.12 = (f32[16,512]{1,0:T(8,128)S(1)}, f32[16,512]{1,0:T(8,128)S(1)}, u32[]{:S(2)}, u32[]{:S(2)}) collective-permute-start(f32[16,512]{1,0:T(8,128)S(1)} %shard_map.98.a), channel_id=1, source_target_pairs={{0,2},{6,4},{9,11},{15,13},{17,19},{23,21},{24,26},{30,28}} | collective-permute-start | bytes 98312 | tf_op jit(solution)/shard_map/ppermute | solution.py:375
  69.7 1.3 %collective-permute-start.13 = (f32[16,512]{1,0:T(8,128)S(1)}, f32[16,512]{1,0:T(8,128)S(1)}, u32[]{:S(2)}, u32[]{:S(2)}) collective-permute-start(f32[16,512]{1,0:T(8,128)S(1)} %shard_map.98.a), channel_id=1, source_target_pairs={{0,3},{6,5},{9,8},{15,14},{17,16},{23,22},{24,27},{30,29}} | collective-permute-start | bytes 98312 | tf_op jit(solution)/shard_map/ppermute | solution.py:375
  71.0 0.0 collective-permute-done.11.b
  71.0 0.3 collective-permute-done.12.c
  71.3 1.3 %collective-permute-done.13.d = f32[16,512]{1,0:T(8,128)S(1)} collective-permute-done((f32[16,512]{1,0:T(8,128)S(1)}, f32[16,512]{1,0:T(8,128)S(1)}, u32[]{:S(2)}, u32[]{:S(2)}) %collective-permute-start.13) | collective-permute-done | bytes 32800 | tf_op jit(solution)/shard_map/ppermute | solution.py:375
  72.6 0.2 shard_map.99
  72.8 0.1 collective-permute-start.14
  72.8 1.2 %collective-permute-done.14 = f32[32,512]{1,0:T(8,128)S(1)} collective-permute-done((f32[32,512]{1,0:T(8,128)S(1)}, f32[32,512]{1,0:T(8,128)S(1)}, u32[]{:S(2)}, u32[]{:S(2)}) %collective-permute-start.14) | collective-permute-done | bytes 65568 | tf_op jit(solution)/shard_map/ppermute | solution.py:375
  74.1 2.2 %collective-permute-start.15 = (f32[32,512]{1,0:T(8,128)S(1)}, f32[32,512]{1,0:T(8,128)S(1)}, u32[]{:S(2)}, u32[]{:S(2)}) collective-permute-start(f32[32,512]{1,0:T(8,128)S(1)} %add.10.refs_0_), channel_id=1, source_target_pairs={{0,8},{1,9},{2,10},{3,11},{4,12},{5,13},{6,14},{7,15},{8,0},{9,1},... | collective-permute-start | bytes 196616 | tf_op jit(solution)/shard_map/ppermute | solution.py:375
  76.3 0.7 collective-permute-start.16
  77.0 1.4 %collective-permute-start.17 = (f32[32,512]{1,0:T(8,128)S(1)}, f32[32,512]{1,0:T(8,128)S(1)}, u32[]{:S(2)}, u32[]{:S(2)}) collective-permute-start(f32[32,512]{1,0:T(8,128)S(1)} %add.10.refs_0_), channel_id=1, source_target_pairs={{0,24},{1,25},{2,26},{3,27},{4,28},{5,29},{6,30},{7,31},{8,16},{9,... | collective-permute-start | bytes 196616 | tf_op jit(solution)/shard_map/ppermute | solution.py:375
  78.4 0.3 collective-permute-done.15.refs_1_
  78.7 2.1 %collective-permute-done.16.refs_2_ = f32[32,512]{1,0:T(8,128)S(1)} collective-permute-done((f32[32,512]{1,0:T(8,128)S(1)}, f32[32,512]{1,0:T(8,128)S(1)}, u32[]{:S(2)}, u32[]{:S(2)}) %collective-permute-start.16) | collective-permute-done | bytes 65568 | tf_op jit(solution)/shard_map/ppermute | solution.py:375
  80.8 1.4 %collective-permute-done.17.refs_3_ = f32[32,512]{1,0:T(8,128)S(1)} collective-permute-done((f32[32,512]{1,0:T(8,128)S(1)}, f32[32,512]{1,0:T(8,128)S(1)}, u32[]{:S(2)}, u32[]{:S(2)}) %collective-permute-start.17) | collective-permute-done | bytes 65568 | tf_op jit(solution)/shard_map/ppermute | solution.py:375
  82.2 0.2 shard_map.100
  82.4 1.4 %collective-permute-start.18 = (f32[16,128]{1,0:T(8,128)S(1)}, f32[16,128]{1,0:T(8,128)S(1)}, u32[]{:S(2)}, u32[]{:S(2)}) collective-permute-start(f32[16,128]{1,0:T(8,128)S(1)} %get-tuple-element.65), channel_id=1, source_target_pairs={{0,2},{1,3},{2,0},{3,1},{4,6},{5,7},{6,4},{7,5},{8,10},{9,11},{10,... | collective-permute-start | bytes 24584 | tf_op jit(solution)/shard_map/ppermute | solution.py:375
  83.8 3.2 %collective-permute-done.18 = f32[16,128]{1,0:T(8,128)S(1)} collective-permute-done((f32[16,128]{1,0:T(8,128)S(1)}, f32[16,128]{1,0:T(8,128)S(1)}, u32[]{:S(2)}, u32[]{:S(2)}) %collective-permute-start.18) | collective-permute-done | bytes 8224 | tf_op jit(solution)/shard_map/ppermute | solution.py:375
  87.0 0.6 subtract_bitcast_fusion
  (3 shorter events, 0.0 us)
Async XLA Ops:
  0.6 2.2 %copy-start = (f32[1,512,512]{2,1,0:T(8,128)S(1)}, f32[1,512,512]{2,1,0:T(8,128)}, u32[]{:S(2)}) copy-start(f32[1,512,512]{2,1,0:T(8,128)} %param.7) | copy-start | bytes 3145732
  2.0 7.1 %copy-start.1 = (bf16[1024,256]{1,0:T(8,128)(2,1)S(1)}, bf16[1024,256]{1,0:T(8,128)(2,1)}, u32[]{:S(2)}) copy-start(bf16[1024,256]{1,0:T(8,128)(2,1)} %participation.1) | copy-start | bytes 1572868
  2.0 7.1 %copy-start.2 = (bf16[1,512,256]{2,1,0:T(8,128)(2,1)S(1)}, bf16[1,512,256]{2,1,0:T(8,128)(2,1)}, u32[]{:S(2)}) copy-start(bf16[1,512,256]{2,1,0:T(8,128)(2,1)} %param.10) | copy-start | bytes 786436
  2.0 7.1 %copy-start.3 = (s32[1024]{0:T(1024)S(1)}, s32[1024]{0:T(1024)}, u32[]{:S(2)}) copy-start(s32[1024]{0:T(1024)} %param.11) | copy-start | bytes 12292
  2.0 7.1 %copy-start.4 = (s32[16]{0:T(128)S(1)}, s32[16]{0:T(128)}, u32[]{:S(2)}) copy-start(s32[16]{0:T(128)} %regime.1) | copy-start | bytes 196
  2.0 12.3 %collective-permute-start = (f32[1344,128]{1,0:T(8,128)S(1)}, f32[1344,128]{1,0:T(8,128)S(1)}, u32[]{:S(2)}, u32[]{:S(2)}) collective-permute-start(f32[1344,128]{1,0:T(8,128)S(1)} %shard_map.86.both), channel_id=1, source_target_pairs={{2,6},{3,7},{4,8},{5,9},{10,14},{11,15},{12,16},{13,17},{18,22},{1... | collective-permute-start | bytes 2064392 | tf_op jit(solution)/shard_map/ppermute | solution.py:375
  2.9 21.9 %collective-permute-start.5 = (f32[512,512]{1,0:T(8,128)S(1)}, f32[512,512]{1,0:T(8,128)S(1)}, u32[]{:S(2)}, u32[]{:S(2)}) collective-permute-start(f32[512,512]{1,0:T(8,128)S(1)} %bitcast.9), channel_id=1, source_target_pairs={{5,9},{11,15},{12,16},{13,17},{18,22},{19,23},{20,24},{26,30}} | collective-permute-start | bytes 3145736 | tf_op jit(solution)/shard_map/ppermute | solution.py:375
  7.7 10.7 %collective-permute-start.1 = (f32[1344,128]{1,0:T(8,128)S(1)}, f32[1344,128]{1,0:T(8,128)S(1)}, u32[]{:S(2)}, u32[]{:S(2)}) collective-permute-start(f32[1344,128]{1,0:T(8,128)S(1)} %shard_map.88), channel_id=1, source_target_pairs={{4,0},{5,1},{10,6},{11,7},{12,8},{13,9},{18,14},{19,15},{20,16},{2... | collective-permute-start | bytes 2064392 | tf_op jit(solution)/shard_map/ppermute | solution.py:375
  10.0 14.7 %collective-permute-start.6 = (f32[520,256]{1,0:T(8,128)S(1)}, f32[520,256]{1,0:T(8,128)S(1)}, u32[]{:S(2)}, u32[]{:S(2)}) collective-permute-start(f32[520,256]{1,0:T(8,128)S(1)} %shard_map.91.local.refs_4_), channel_id=1, source_target_pairs={{0,1},{1,0},{2,3},{3,2},{4,5},{5,4},{6,7},{7,6},{8,9},{9,8},{10,11... | collective-permute-start | bytes 1597448 | tf_op jit(solution)/shard_map/ppermute | solution.py:375
  13.1 14.3 %collective-permute-start.4 = (f32[512,512]{1,0:T(8,128)S(1)}, f32[512,512]{1,0:T(8,128)S(1)}, u32[]{:S(2)}, u32[]{:S(2)}) collective-permute-start(f32[512,512]{1,0:T(8,128)S(1)} %bitcast.11), channel_id=1, source_target_pairs={{4,0},{10,6},{13,9},{19,15},{21,17},{27,23},{28,24}} | collective-permute-start | bytes 3145736 | tf_op jit(solution)/shard_map/ppermute | solution.py:375
  18.8 8.6 %collective-permute-start.3 = (f32[1344,128]{1,0:T(8,128)S(1)}, f32[1344,128]{1,0:T(8,128)S(1)}, u32[]{:S(2)}, u32[]{:S(2)}) collective-permute-start(f32[1344,128]{1,0:T(8,128)S(1)} %get-tuple-element.40), channel_id=1, source_target_pairs={{1,9},{7,15},{9,17},{15,23},{16,24},{22,30}} | collective-permute-start | bytes 2064392 | tf_op jit(solution)/shard_map/ppermute | solution.py:375
  23.4 13.2 %collective-permute-start.2 = (f32[1344,128]{1,0:T(8,128)S(1)}, f32[1344,128]{1,0:T(8,128)S(1)}, u32[]{:S(2)}, u32[]{:S(2)}) collective-permute-start(f32[1344,128]{1,0:T(8,128)S(1)} %get-tuple-element.48), channel_id=1, source_target_pairs={{8,0},{14,6},{25,17},{31,23}} | collective-permute-start | bytes 2064392 | tf_op jit(solution)/shard_map/ppermute | solution.py:375
  25.8 12.9 %collective-permute-start.8 = (f32[512,512]{1,0:T(8,128)S(1)}, f32[512,512]{1,0:T(8,128)S(1)}, u32[]{:S(2)}, u32[]{:S(2)}) collective-permute-start(f32[512,512]{1,0:T(8,128)S(1)} %shard_map.92.lower), channel_id=1, source_target_pairs={{9,17},{15,23},{16,24},{22,30}} | collective-permute-start | bytes 3145736 | tf_op jit(solution)/shard_map/ppermute | solution.py:375
  26.7 9.9 %collective-permute-start.7 = (f32[1344,128]{1,0:T(8,128)S(1)}, f32[1344,128]{1,0:T(8,128)S(1)}, u32[]{:S(2)}, u32[]{:S(2)}) collective-permute-start(f32[1344,128]{1,0:T(8,128)S(1)} %get-tuple-element.48), channel_id=1, source_target_pairs={{17,9},{23,15}} | collective-permute-start | bytes 2064392 | tf_op jit(solution)/shard_map/ppermute | solution.py:375
  38.7 21.1 %collective-permute-start.9 = (f32[1344,128]{1,0:T(8,128)S(1)}, f32[1344,128]{1,0:T(8,128)S(1)}, u32[]{:S(2)}, u32[]{:S(2)}) collective-permute-start(f32[1344,128]{1,0:T(8,128)S(1)} %get-tuple-element.50), channel_id=1, source_target_pairs={{0,17},{6,23},{9,24},{15,30}} | collective-permute-start | bytes 2064392 | tf_op jit(solution)/shard_map/ppermute | solution.py:375
  51.5 13.7 %collective-permute-start.10 = (f32[1344,128]{1,0:T(8,128)S(1)}, f32[1344,128]{1,0:T(8,128)S(1)}, u32[]{:S(2)}, u32[]{:S(2)}) collective-permute-start(f32[1344,128]{1,0:T(8,128)S(1)} %get-tuple-element.60), channel_id=1, source_target_pairs={{17,0},{23,6},{24,9},{30,15}} | collective-permute-start | bytes 2064392 | tf_op jit(solution)/shard_map/ppermute | solution.py:375
  67.1 3.9 %collective-permute-start.11 = (f32[16,512]{1,0:T(8,128)S(1)}, f32[16,512]{1,0:T(8,128)S(1)}, u32[]{:S(2)}, u32[]{:S(2)}) collective-permute-start(f32[16,512]{1,0:T(8,128)S(1)} %shard_map.98.a), channel_id=1, source_target_pairs={{0,1},{6,7},{9,10},{15,12},{17,18},{23,20},{24,25},{30,31}} | collective-permute-start | bytes 98312 | tf_op jit(solution)/shard_map/ppermute | solution.py:375
  68.4 2.9 %collective-permute-start.12 = (f32[16,512]{1,0:T(8,128)S(1)}, f32[16,512]{1,0:T(8,128)S(1)}, u32[]{:S(2)}, u32[]{:S(2)}) collective-permute-start(f32[16,512]{1,0:T(8,128)S(1)} %shard_map.98.a), channel_id=1, source_target_pairs={{0,2},{6,4},{9,11},{15,13},{17,19},{23,21},{24,26},{30,28}} | collective-permute-start | bytes 98312 | tf_op jit(solution)/shard_map/ppermute | solution.py:375
  69.7 2.9 %collective-permute-start.13 = (f32[16,512]{1,0:T(8,128)S(1)}, f32[16,512]{1,0:T(8,128)S(1)}, u32[]{:S(2)}, u32[]{:S(2)}) collective-permute-start(f32[16,512]{1,0:T(8,128)S(1)} %shard_map.98.a), channel_id=1, source_target_pairs={{0,3},{6,5},{9,8},{15,14},{17,16},{23,22},{24,27},{30,29}} | collective-permute-start | bytes 98312 | tf_op jit(solution)/shard_map/ppermute | solution.py:375
  72.8 1.3 %collective-permute-start.14 = (f32[32,512]{1,0:T(8,128)S(1)}, f32[32,512]{1,0:T(8,128)S(1)}, u32[]{:S(2)}, u32[]{:S(2)}) collective-permute-start(f32[32,512]{1,0:T(8,128)S(1)} %get-tuple-element.63), channel_id=1, source_target_pairs={{0,4},{1,5},{2,6},{3,7},{4,0},{5,1},{6,2},{7,3},{8,12},{9,13},{10,... | collective-permute-start | bytes 196616 | tf_op jit(solution)/shard_map/ppermute | solution.py:375
  74.1 4.6 %collective-permute-start.15 = (f32[32,512]{1,0:T(8,128)S(1)}, f32[32,512]{1,0:T(8,128)S(1)}, u32[]{:S(2)}, u32[]{:S(2)}) collective-permute-start(f32[32,512]{1,0:T(8,128)S(1)} %add.10.refs_0_), channel_id=1, source_target_pairs={{0,8},{1,9},{2,10},{3,11},{4,12},{5,13},{6,14},{7,15},{8,0},{9,1},... | collective-permute-start | bytes 196616 | tf_op jit(solution)/shard_map/ppermute | solution.py:375
  76.3 4.5 %collective-permute-start.16 = (f32[32,512]{1,0:T(8,128)S(1)}, f32[32,512]{1,0:T(8,128)S(1)}, u32[]{:S(2)}, u32[]{:S(2)}) collective-permute-start(f32[32,512]{1,0:T(8,128)S(1)} %add.10.refs_0_), channel_id=1, source_target_pairs={{0,16},{1,17},{2,18},{3,19},{4,20},{5,21},{6,22},{7,23},{8,24},{9,... | collective-permute-start | bytes 196616 | tf_op jit(solution)/shard_map/ppermute | solution.py:375
  77.0 5.2 %collective-permute-start.17 = (f32[32,512]{1,0:T(8,128)S(1)}, f32[32,512]{1,0:T(8,128)S(1)}, u32[]{:S(2)}, u32[]{:S(2)}) collective-permute-start(f32[32,512]{1,0:T(8,128)S(1)} %add.10.refs_0_), channel_id=1, source_target_pairs={{0,24},{1,25},{2,26},{3,27},{4,28},{5,29},{6,30},{7,31},{8,16},{9,... | collective-permute-start | bytes 196616 | tf_op jit(solution)/shard_map/ppermute | solution.py:375
  82.4 4.6 %collective-permute-start.18 = (f32[16,128]{1,0:T(8,128)S(1)}, f32[16,128]{1,0:T(8,128)S(1)}, u32[]{:S(2)}, u32[]{:S(2)}) collective-permute-start(f32[16,128]{1,0:T(8,128)S(1)} %get-tuple-element.65), channel_id=1, source_target_pairs={{0,2},{1,3},{2,0},{3,1},{4,6},{5,7},{6,4},{7,5},{8,10},{9,11},{10,... | collective-permute-start | bytes 24584 | tf_op jit(solution)/shard_map/ppermute | solution.py:375

commit v7 on v6

--- a/solution.py
+++ b/solution.py
@@ -483,7 +483,7 @@
 
     parts = [
         sent_to(solved, lambda s, m, k=k: (s, (m + k) % groups) if m == home(s) else None)
-        for k in range(1, groups)
+        for k in (3, 2, 1)
     ]
     whole, payload = call(
         functools.partial(modal_kernel, home),

time: 87.9 us -> 87.6 us (level)
  no operation moved by 1% of the time
where the time goes in v7:
time: 87.6 us; the launch traced here: 87.3 us
  starting transfers between devices  34.6 us (39%)
  waiting for transfers between devices  27 us (31%)
  Pallas kernels  24.1 us (28%)
  between operations  0.96 us (1%)
    ppermute x19, starting transfers between devices, sent_to(): return lax.ppermute(value, AXES, pairs)  34.6 us
    ppermute x19, waiting for transfers between devices, sent_to(): return lax.ppermute(value, AXES, pairs)  27 us
    pallas_call x14, Pallas kernels, call(): pl.pallas_call(kernel, out_shape=shapes[0] if single else tuple(shapes),...  22.8 us
  transfers between devices with their start and end apart: 19, of which 10 were waited for; matrix products, arithmetic and copies ran while one was open for 0% of the time, Pallas kernels for 23%

profile of v7, /device:TPU:0, one launch (start us, length us, event | category | flops | bytes accessed | tf_op | source)
XLA Modules:
  0.0 87.3 jit_solution(7110861731018684084)
XLA Ops:
  0.6 0.0 copy-start
  0.6 1.3 %shard_map.86.both = f32[1344,128]{1,0:T(8,128)S(1)} custom-call(f32[512,512]{1,0:T(8,128)} %bitcast.15, f32[16,512]{1,0:T(8,128)} %bitcast.16), custom_call_target="tpu_custom_call" | custom-call | tf_op jit(solution)/shard_map/pallas_call | solution.py:330
  2.0 0.0 copy-start.1
  2.0 0.0 copy-start.2
  2.0 0.0 copy-start.3
  2.0 0.0 copy-start.4
  2.0 0.8 collective-permute-start
  2.9 0.0 copy-done
  2.9 0.7 collective-permute-start.5
  3.6 4.1 %shard_map.88 = f32[1344,128]{1,0:T(8,128)S(1)} custom-call(f32[1344,128]{1,0:T(8,128)S(1)} %shard_map.86.both, f32[512,512]{1,0:T(8,128)S(1)} %bitcast.10), custom_call_target="tpu_custom_call" | custom-call | flops 483183808 | bytes 2424832 | tf_op jit(solution)/shard_map/pallas_call | solution.py:344
  7.7 1.3 %collective-permute-start.1 = (f32[1344,128]{1,0:T(8,128)S(1)}, f32[1344,128]{1,0:T(8,128)S(1)}, u32[]{:S(2)}, u32[]{:S(2)}) collective-permute-start(f32[1344,128]{1,0:T(8,128)S(1)} %shard_map.88), channel_id=1, source_target_pairs={{4,0},{5,1},{10,6},{11,7},{12,8},{13,9},{18,14},{19,15},{20,16},{2... | collective-permute-start | bytes 2064392 | tf_op jit(solution)/shard_map/ppermute | solution.py:375
  9.0 0.0 copy-done.1
  9.1 0.0 copy-done.2
  9.1 0.0 copy-done.3
  9.1 0.0 copy-done.4
  9.1 0.9 %shard_map.91.local.refs_4_ = f32[520,256]{1,0:T(8,128)S(1)} custom-call(s32[16]{0:T(128)S(1)} %copy-done.4, s32[1,1024]{1,0:T(1,128)S(1)} %bitcast.14, bf16[1024,256]{1,0:T(8,128)(2,1)S(1)} %copy-done.1, bf16[512,256]{1,0:T(8,128)(2,1)S(1)} %bitcast.13), custom_call_target="tpu_custom_call" | custom-call | flops 2516582 | bytes 1323072 | tf_op jit(solution)/shard_map/pallas_call | solution.py:344
  10.0 3.0 %collective-permute-start.6 = (f32[520,256]{1,0:T(8,128)S(1)}, f32[520,256]{1,0:T(8,128)S(1)}, u32[]{:S(2)}, u32[]{:S(2)}) collective-permute-start(f32[520,256]{1,0:T(8,128)S(1)} %shard_map.91.local.refs_4_), channel_id=1, source_target_pairs={{0,1},{1,0},{2,3},{3,2},{4,5},{5,4},{6,7},{7,6},{8,9},{9,8},{10,11... | collective-permute-start | bytes 1597448 | tf_op jit(solution)/shard_map/ppermute | solution.py:375
  13.1 1.3 %collective-permute-start.4 = (f32[512,512]{1,0:T(8,128)S(1)}, f32[512,512]{1,0:T(8,128)S(1)}, u32[]{:S(2)}, u32[]{:S(2)}) collective-permute-start(f32[512,512]{1,0:T(8,128)S(1)} %bitcast.11), channel_id=1, source_target_pairs={{4,0},{10,6},{13,9},{19,15},{21,17},{27,23},{28,24}} | collective-permute-start | bytes 3145736 | tf_op jit(solution)/shard_map/ppermute | solution.py:375
  14.4 0.0 collective-permute-done.packed
  14.4 4.1 %shard_map.87 = (f32[512,512]{1,0:T(8,128)S(1)}, f32[528,512]{1,0:T(8,128)S(1)}) custom-call(f32[1344,128]{1,0:T(8,128)S(1)} %collective-permute-done.packed, f32[512,512]{1,0:T(8,128)S(1)} %bitcast.12), custom_call_target="tpu_custom_call" | custom-call | flops 4831838208 | bytes 3866624 | tf_op jit(solution)/shard_map/pallas_call | solution.py:344
  18.5 0.0 collective-permute-done.1.above
  18.5 0.3 shard_map.89
  18.8 0.7 collective-permute-start.3
  19.5 3.9 %shard_map.90 = (f32[1344,128]{1,0:T(8,128)S(1)}, f32[8,128]{1,0:T(8,128)S(1)}) custom-call(f32[512,512]{1,0:T(8,128)S(1)} %get-tuple-element.36.block, f32[16,512]{1,0:T(8,128)S(1)} %get-tuple-element.37.thin, f32[512,512]{1,0:T(8,128)S(1)} %get-tuple-element.38.lower.through), custom_call_target="tpu_custom_call" | custom-call | flops 483183808 | bytes 2822144 | tf_op jit(solution)/shard_map/pallas_call | solution.py:344
  23.4 1.3 %collective-permute-start.2 = (f32[1344,128]{1,0:T(8,128)S(1)}, f32[1344,128]{1,0:T(8,128)S(1)}, u32[]{:S(2)}, u32[]{:S(2)}) collective-permute-start(f32[1344,128]{1,0:T(8,128)S(1)} %get-tuple-element.48), channel_id=1, source_target_pairs={{8,0},{14,6},{25,17},{31,23}} | collective-permute-start | bytes 2064392 | tf_op jit(solution)/shard_map/ppermute | solution.py:375
  24.7 0.0 collective-permute-done.6.other.refs_5_
  24.7 0.0 collective-permute-done.5.passed
  24.8 1.0 %shard_map.92.lower = f32[512,512]{1,0:T(8,128)S(1)} custom-call(f32[512,512]{1,0:T(8,128)S(1)} %get-tuple-element.38.lower.through, f32[512,512]{1,0:T(8,128)S(1)} %collective-permute-done.5.passed, f32[8,128]{1,0:T(8,128)S(1)} %get-tuple-element.45.after), custom_call_target="tpu_custom_call" | custom-call | flops 80530640 | bytes 3149824 | tf_op jit(solution)/shard_map/pallas_call | solution.py:344
  25.8 0.9 %collective-permute-start.8 = (f32[512,512]{1,0:T(8,128)S(1)}, f32[512,512]{1,0:T(8,128)S(1)}, u32[]{:S(2)}, u32[]{:S(2)}) collective-permute-start(f32[512,512]{1,0:T(8,128)S(1)} %shard_map.92.lower), channel_id=1, source_target_pairs={{9,17},{15,23},{16,24},{22,30}} | collective-permute-start | bytes 3145736 | tf_op jit(solution)/shard_map/ppermute | solution.py:375
  26.7 0.7 collective-permute-start.7
  27.4 0.0 collective-permute-done.4.passed
  27.4 0.0 collective-permute-done.3.packed
  27.4 3.9 %shard_map.93 = (f32[512,512]{1,0:T(8,128)S(1)}, f32[528,512]{1,0:T(8,128)S(1)}) custom-call(f32[1344,128]{1,0:T(8,128)S(1)} %collective-permute-done.3.packed, f32[512,512]{1,0:T(8,128)S(1)} %shard_map.92.lower), custom_call_target="tpu_custom_call" | custom-call | flops 483183808 | bytes 3866624 | tf_op jit(solution)/shard_map/pallas_call | solution.py:344
  31.3 5.3 %collective-permute-done.2.early = f32[1344,128]{1,0:T(8,128)S(1)} collective-permute-done((f32[1344,128]{1,0:T(8,128)S(1)}, f32[1344,128]{1,0:T(8,128)S(1)}, u32[]{:S(2)}, u32[]{:S(2)}) %collective-permute-start.2) | collective-permute-done | bytes 688160 | tf_op jit(solution)/shard_map/ppermute | solution.py:375
  36.6 0.0 collective-permute-done.7.late
  36.6 2.1 %shard_map.95 = (f32[1344,128]{1,0:T(8,128)S(1)}, f32[512,512]{1,0:T(8,128)S(1)}, f32[16,512]{1,0:T(8,128)S(1)}) custom-call(f32[16,512]{1,0:T(8,128)S(1)} %get-tuple-element.47.after.thin, f32[1344,128]{1,0:T(8,128)S(1)} %collective-permute-done.2.early, f32[1344,128]{1,0:T(8,128)S(1)} %collective-permute-done.7.late, ...), custom_call_target="tpu_custom_call" | custom-call | flops 2415919104 | bytes 6389760 | tf_op jit(solution)/shard_map/pallas_call | solution.py:344
  38.7 0.0 collective-permute-done.8.passed
  38.7 12.7 %collective-permute-start.9 = (f32[1344,128]{1,0:T(8,128)S(1)}, f32[1344,128]{1,0:T(8,128)S(1)}, u32[]{:S(2)}, u32[]{:S(2)}) collective-permute-start(f32[1344,128]{1,0:T(8,128)S(1)} %get-tuple-element.50), channel_id=1, source_target_pairs={{0,17},{6,23},{9,24},{15,30}} | collective-permute-start | bytes 2064392 | tf_op jit(solution)/shard_map/ppermute | solution.py:375
  51.5 1.3 %collective-permute-start.10 = (f32[1344,128]{1,0:T(8,128)S(1)}, f32[1344,128]{1,0:T(8,128)S(1)}, u32[]{:S(2)}, u32[]{:S(2)}) collective-permute-start(f32[1344,128]{1,0:T(8,128)S(1)} %get-tuple-element.60), channel_id=1, source_target_pairs={{17,0},{23,6},{24,9},{30,15}} | collective-permute-start | bytes 2064392 | tf_op jit(solution)/shard_map/ppermute | solution.py:375
  52.8 7.1 %collective-permute-done.9.packed = f32[1344,128]{1,0:T(8,128)S(1)} collective-permute-done((f32[1344,128]{1,0:T(8,128)S(1)}, f32[1344,128]{1,0:T(8,128)S(1)}, u32[]{:S(2)}, u32[]{:S(2)}) %collective-permute-start.9) | collective-permute-done | bytes 688160 | tf_op jit(solution)/shard_map/ppermute | solution.py:375
  59.9 0.1 shard_map.97
  59.9 5.3 %collective-permute-done.10.above = f32[1344,128]{1,0:T(8,128)S(1)} collective-permute-done((f32[1344,128]{1,0:T(8,128)S(1)}, f32[1344,128]{1,0:T(8,128)S(1)}, u32[]{:S(2)}, u32[]{:S(2)}) %collective-permute-start.10) | collective-permute-done | bytes 688160 | tf_op jit(solution)/shard_map/ppermute | solution.py:375
  65.2 1.9 %shard_map.98.a = f32[16,512]{1,0:T(8,128)S(1)} custom-call(f32[512,512]{1,0:T(8,128)S(1)} %get-tuple-element.58.block, f32[16,512]{1,0:T(8,128)S(1)} %get-tuple-element.59.thin, f32[1344,128]{1,0:T(8,128)S(1)} %collective-permute-done.10.above), custom_call_target="tpu_custom_call" | custom-call | flops 80530640 | bytes 1802240 | tf_op jit(solution)/shard_map/pallas_call | solution.py:344
  67.1 1.3 %collective-permute-start.11 = (f32[16,512]{1,0:T(8,128)S(1)}, f32[16,512]{1,0:T(8,128)S(1)}, u32[]{:S(2)}, u32[]{:S(2)}) collective-permute-start(f32[16,512]{1,0:T(8,128)S(1)} %shard_map.98.a), channel_id=1, source_target_pairs={{0,3},{6,5},{9,8},{15,14},{17,16},{23,22},{24,27},{30,29}} | collective-permute-start | bytes 98312 | tf_op jit(solution)/shard_map/ppermute | solution.py:375
  68.4 1.3 %collective-permute-start.12 = (f32[16,512]{1,0:T(8,128)S(1)}, f32[16,512]{1,0:T(8,128)S(1)}, u32[]{:S(2)}, u32[]{:S(2)}) collective-permute-start(f32[16,512]{1,0:T(8,128)S(1)} %shard_map.98.a), channel_id=1, source_target_pairs={{0,2},{6,4},{9,11},{15,13},{17,19},{23,21},{24,26},{30,28}} | collective-permute-start | bytes 98312 | tf_op jit(solution)/shard_map/ppermute | solution.py:375
  69.7 1.3 %collective-permute-start.13 = (f32[16,512]{1,0:T(8,128)S(1)}, f32[16,512]{1,0:T(8,128)S(1)}, u32[]{:S(2)}, u32[]{:S(2)}) collective-permute-start(f32[16,512]{1,0:T(8,128)S(1)} %shard_map.98.a), channel_id=1, source_target_pairs={{0,1},{6,7},{9,10},{15,12},{17,18},{23,20},{24,25},{30,31}} | collective-permute-start | bytes 98312 | tf_op jit(solution)/shard_map/ppermute | solution.py:375
  71.0 0.0 collective-permute-done.11.b
  71.0 0.3 collective-permute-done.12.c
  71.3 1.3 %collective-permute-done.13.d = f32[16,512]{1,0:T(8,128)S(1)} collective-permute-done((f32[16,512]{1,0:T(8,128)S(1)}, f32[16,512]{1,0:T(8,128)S(1)}, u32[]{:S(2)}, u32[]{:S(2)}) %collective-permute-start.13) | collective-permute-done | bytes 32800 | tf_op jit(solution)/shard_map/ppermute | solution.py:375
  72.6 0.2 shard_map.99
  72.8 0.1 collective-permute-start.14
  72.8 1.2 %collective-permute-done.14 = f32[32,512]{1,0:T(8,128)S(1)} collective-permute-done((f32[32,512]{1,0:T(8,128)S(1)}, f32[32,512]{1,0:T(8,128)S(1)}, u32[]{:S(2)}, u32[]{:S(2)}) %collective-permute-start.14) | collective-permute-done | bytes 65568 | tf_op jit(solution)/shard_map/ppermute | solution.py:375
  74.1 1.6 %collective-permute-start.15 = (f32[32,512]{1,0:T(8,128)S(1)}, f32[32,512]{1,0:T(8,128)S(1)}, u32[]{:S(2)}, u32[]{:S(2)}) collective-permute-start(f32[32,512]{1,0:T(8,128)S(1)} %add.10.refs_0_), channel_id=1, source_target_pairs={{0,8},{1,9},{2,10},{3,11},{4,12},{5,13},{6,14},{7,15},{8,0},{9,1},... | collective-permute-start | bytes 196616 | tf_op jit(solution)/shard_map/ppermute | solution.py:375
  75.7 1.0 %collective-permute-start.16 = (f32[32,512]{1,0:T(8,128)S(1)}, f32[32,512]{1,0:T(8,128)S(1)}, u32[]{:S(2)}, u32[]{:S(2)}) collective-permute-start(f32[32,512]{1,0:T(8,128)S(1)} %add.10.refs_0_), channel_id=1, source_target_pairs={{0,16},{1,17},{2,18},{3,19},{4,20},{5,21},{6,22},{7,23},{8,24},{9,... | collective-permute-start | bytes 196616 | tf_op jit(solution)/shard_map/ppermute | solution.py:375
  76.7 1.4 %collective-permute-start.17 = (f32[32,512]{1,0:T(8,128)S(1)}, f32[32,512]{1,0:T(8,128)S(1)}, u32[]{:S(2)}, u32[]{:S(2)}) collective-permute-start(f32[32,512]{1,0:T(8,128)S(1)} %add.10.refs_0_), channel_id=1, source_target_pairs={{0,24},{1,25},{2,26},{3,27},{4,28},{5,29},{6,30},{7,31},{8,16},{9,... | collective-permute-start | bytes 196616 | tf_op jit(solution)/shard_map/ppermute | solution.py:375
  78.1 0.3 collective-permute-done.15.refs_1_
  78.4 1.5 %collective-permute-done.16.refs_2_ = f32[32,512]{1,0:T(8,128)S(1)} collective-permute-done((f32[32,512]{1,0:T(8,128)S(1)}, f32[32,512]{1,0:T(8,128)S(1)}, u32[]{:S(2)}, u32[]{:S(2)}) %collective-permute-start.16) | collective-permute-done | bytes 65568 | tf_op jit(solution)/shard_map/ppermute | solution.py:375
  80.0 1.9 %collective-permute-done.17.refs_3_ = f32[32,512]{1,0:T(8,128)S(1)} collective-permute-done((f32[32,512]{1,0:T(8,128)S(1)}, f32[32,512]{1,0:T(8,128)S(1)}, u32[]{:S(2)}, u32[]{:S(2)}) %collective-permute-start.17) | collective-permute-done | bytes 65568 | tf_op jit(solution)/shard_map/ppermute | solution.py:375
  81.9 0.2 shard_map.100
  82.1 1.8 %collective-permute-start.18 = (f32[16,128]{1,0:T(8,128)S(1)}, f32[16,128]{1,0:T(8,128)S(1)}, u32[]{:S(2)}, u32[]{:S(2)}) collective-permute-start(f32[16,128]{1,0:T(8,128)S(1)} %get-tuple-element.65), channel_id=1, source_target_pairs={{0,2},{1,3},{2,0},{3,1},{4,6},{5,7},{6,4},{7,5},{8,10},{9,11},{10,... | collective-permute-start | bytes 24584 | tf_op jit(solution)/shard_map/ppermute | solution.py:375
  83.9 2.8 %collective-permute-done.18 = f32[16,128]{1,0:T(8,128)S(1)} collective-permute-done((f32[16,128]{1,0:T(8,128)S(1)}, f32[16,128]{1,0:T(8,128)S(1)}, u32[]{:S(2)}, u32[]{:S(2)}) %collective-permute-start.18) | collective-permute-done | bytes 8224 | tf_op jit(solution)/shard_map/ppermute | solution.py:375
  86.7 0.6 subtract_bitcast_fusion
  (3 shorter events, 0.0 us)
Async XLA Ops:
  0.6 2.2 %copy-start = (f32[1,512,512]{2,1,0:T(8,128)S(1)}, f32[1,512,512]{2,1,0:T(8,128)}, u32[]{:S(2)}) copy-start(f32[1,512,512]{2,1,0:T(8,128)} %param.7) | copy-start | bytes 3145732
  2.0 7.1 %copy-start.1 = (bf16[1024,256]{1,0:T(8,128)(2,1)S(1)}, bf16[1024,256]{1,0:T(8,128)(2,1)}, u32[]{:S(2)}) copy-start(bf16[1024,256]{1,0:T(8,128)(2,1)} %participation.1) | copy-start | bytes 1572868
  2.0 7.1 %copy-start.2 = (bf16[1,512,256]{2,1,0:T(8,128)(2,1)S(1)}, bf16[1,512,256]{2,1,0:T(8,128)(2,1)}, u32[]{:S(2)}) copy-start(bf16[1,512,256]{2,1,0:T(8,128)(2,1)} %param.10) | copy-start | bytes 786436
  2.0 7.1 %copy-start.3 = (s32[1024]{0:T(1024)S(1)}, s32[1024]{0:T(1024)}, u32[]{:S(2)}) copy-start(s32[1024]{0:T(1024)} %param.11) | copy-start | bytes 12292
  2.0 7.1 %copy-start.4 = (s32[16]{0:T(128)S(1)}, s32[16]{0:T(128)}, u32[]{:S(2)}) copy-start(s32[16]{0:T(128)} %regime.1) | copy-start | bytes 196
  2.0 12.3 %collective-permute-start = (f32[1344,128]{1,0:T(8,128)S(1)}, f32[1344,128]{1,0:T(8,128)S(1)}, u32[]{:S(2)}, u32[]{:S(2)}) collective-permute-start(f32[1344,128]{1,0:T(8,128)S(1)} %shard_map.86.both), channel_id=1, source_target_pairs={{2,6},{3,7},{4,8},{5,9},{10,14},{11,15},{12,16},{13,17},{18,22},{1... | collective-permute-start | bytes 2064392 | tf_op jit(solution)/shard_map/ppermute | solution.py:375
  2.9 21.9 %collective-permute-start.5 = (f32[512,512]{1,0:T(8,128)S(1)}, f32[512,512]{1,0:T(8,128)S(1)}, u32[]{:S(2)}, u32[]{:S(2)}) collective-permute-start(f32[512,512]{1,0:T(8,128)S(1)} %bitcast.9), channel_id=1, source_target_pairs={{5,9},{11,15},{12,16},{13,17},{18,22},{19,23},{20,24},{26,30}} | collective-permute-start | bytes 3145736 | tf_op jit(solution)/shard_map/ppermute | solution.py:375
  7.7 10.7 %collective-permute-start.1 = (f32[1344,128]{1,0:T(8,128)S(1)}, f32[1344,128]{1,0:T(8,128)S(1)}, u32[]{:S(2)}, u32[]{:S(2)}) collective-permute-start(f32[1344,128]{1,0:T(8,128)S(1)} %shard_map.88), channel_id=1, source_target_pairs={{4,0},{5,1},{10,6},{11,7},{12,8},{13,9},{18,14},{19,15},{20,16},{2... | collective-permute-start | bytes 2064392 | tf_op jit(solution)/shard_map/ppermute | solution.py:375
  10.0 14.7 %collective-permute-start.6 = (f32[520,256]{1,0:T(8,128)S(1)}, f32[520,256]{1,0:T(8,128)S(1)}, u32[]{:S(2)}, u32[]{:S(2)}) collective-permute-start(f32[520,256]{1,0:T(8,128)S(1)} %shard_map.91.local.refs_4_), channel_id=1, source_target_pairs={{0,1},{1,0},{2,3},{3,2},{4,5},{5,4},{6,7},{7,6},{8,9},{9,8},{10,11... | collective-permute-start | bytes 1597448 | tf_op jit(solution)/shard_map/ppermute | solution.py:375
  13.1 14.3 %collective-permute-start.4 = (f32[512,512]{1,0:T(8,128)S(1)}, f32[512,512]{1,0:T(8,128)S(1)}, u32[]{:S(2)}, u32[]{:S(2)}) collective-permute-start(f32[512,512]{1,0:T(8,128)S(1)} %bitcast.11), channel_id=1, source_target_pairs={{4,0},{10,6},{13,9},{19,15},{21,17},{27,23},{28,24}} | collective-permute-start | bytes 3145736 | tf_op jit(solution)/shard_map/ppermute | solution.py:375
  18.8 8.6 %collective-permute-start.3 = (f32[1344,128]{1,0:T(8,128)S(1)}, f32[1344,128]{1,0:T(8,128)S(1)}, u32[]{:S(2)}, u32[]{:S(2)}) collective-permute-start(f32[1344,128]{1,0:T(8,128)S(1)} %get-tuple-element.40), channel_id=1, source_target_pairs={{1,9},{7,15},{9,17},{15,23},{16,24},{22,30}} | collective-permute-start | bytes 2064392 | tf_op jit(solution)/shard_map/ppermute | solution.py:375
  23.4 13.2 %collective-permute-start.2 = (f32[1344,128]{1,0:T(8,128)S(1)}, f32[1344,128]{1,0:T(8,128)S(1)}, u32[]{:S(2)}, u32[]{:S(2)}) collective-permute-start(f32[1344,128]{1,0:T(8,128)S(1)} %get-tuple-element.48), channel_id=1, source_target_pairs={{8,0},{14,6},{25,17},{31,23}} | collective-permute-start | bytes 2064392 | tf_op jit(solution)/shard_map/ppermute | solution.py:375
  25.8 12.9 %collective-permute-start.8 = (f32[512,512]{1,0:T(8,128)S(1)}, f32[512,512]{1,0:T(8,128)S(1)}, u32[]{:S(2)}, u32[]{:S(2)}) collective-permute-start(f32[512,512]{1,0:T(8,128)S(1)} %shard_map.92.lower), channel_id=1, source_target_pairs={{9,17},{15,23},{16,24},{22,30}} | collective-permute-start | bytes 3145736 | tf_op jit(solution)/shard_map/ppermute | solution.py:375
  26.7 9.9 %collective-permute-start.7 = (f32[1344,128]{1,0:T(8,128)S(1)}, f32[1344,128]{1,0:T(8,128)S(1)}, u32[]{:S(2)}, u32[]{:S(2)}) collective-permute-start(f32[1344,128]{1,0:T(8,128)S(1)} %get-tuple-element.48), channel_id=1, source_target_pairs={{17,9},{23,15}} | collective-permute-start | bytes 2064392 | tf_op jit(solution)/shard_map/ppermute | solution.py:375
  38.7 21.1 %collective-permute-start.9 = (f32[1344,128]{1,0:T(8,128)S(1)}, f32[1344,128]{1,0:T(8,128)S(1)}, u32[]{:S(2)}, u32[]{:S(2)}) collective-permute-start(f32[1344,128]{1,0:T(8,128)S(1)} %get-tuple-element.50), channel_id=1, source_target_pairs={{0,17},{6,23},{9,24},{15,30}} | collective-permute-start | bytes 2064392 | tf_op jit(solution)/shard_map/ppermute | solution.py:375
  51.5 13.7 %collective-permute-start.10 = (f32[1344,128]{1,0:T(8,128)S(1)}, f32[1344,128]{1,0:T(8,128)S(1)}, u32[]{:S(2)}, u32[]{:S(2)}) collective-permute-start(f32[1344,128]{1,0:T(8,128)S(1)} %get-tuple-element.60), channel_id=1, source_target_pairs={{17,0},{23,6},{24,9},{30,15}} | collective-permute-start | bytes 2064392 | tf_op jit(solution)/shard_map/ppermute | solution.py:375
  67.1 3.9 %collective-permute-start.11 = (f32[16,512]{1,0:T(8,128)S(1)}, f32[16,512]{1,0:T(8,128)S(1)}, u32[]{:S(2)}, u32[]{:S(2)}) collective-permute-start(f32[16,512]{1,0:T(8,128)S(1)} %shard_map.98.a), channel_id=1, source_target_pairs={{0,3},{6,5},{9,8},{15,14},{17,16},{23,22},{24,27},{30,29}} | collective-permute-start | bytes 98312 | tf_op jit(solution)/shard_map/ppermute | solution.py:375
  68.4 2.9 %collective-permute-start.12 = (f32[16,512]{1,0:T(8,128)S(1)}, f32[16,512]{1,0:T(8,128)S(1)}, u32[]{:S(2)}, u32[]{:S(2)}) collective-permute-start(f32[16,512]{1,0:T(8,128)S(1)} %shard_map.98.a), channel_id=1, source_target_pairs={{0,2},{6,4},{9,11},{15,13},{17,19},{23,21},{24,26},{30,28}} | collective-permute-start | bytes 98312 | tf_op jit(solution)/shard_map/ppermute | solution.py:375
  69.7 2.9 %collective-permute-start.13 = (f32[16,512]{1,0:T(8,128)S(1)}, f32[16,512]{1,0:T(8,128)S(1)}, u32[]{:S(2)}, u32[]{:S(2)}) collective-permute-start(f32[16,512]{1,0:T(8,128)S(1)} %shard_map.98.a), channel_id=1, source_target_pairs={{0,1},{6,7},{9,10},{15,12},{17,18},{23,20},{24,25},{30,31}} | collective-permute-start | bytes 98312 | tf_op jit(solution)/shard_map/ppermute | solution.py:375
  72.8 1.3 %collective-permute-start.14 = (f32[32,512]{1,0:T(8,128)S(1)}, f32[32,512]{1,0:T(8,128)S(1)}, u32[]{:S(2)}, u32[]{:S(2)}) collective-permute-start(f32[32,512]{1,0:T(8,128)S(1)} %get-tuple-element.63), channel_id=1, source_target_pairs={{0,4},{1,5},{2,6},{3,7},{4,0},{5,1},{6,2},{7,3},{8,12},{9,13},{10,... | collective-permute-start | bytes 196616 | tf_op jit(solution)/shard_map/ppermute | solution.py:375
  74.1 4.3 %collective-permute-start.15 = (f32[32,512]{1,0:T(8,128)S(1)}, f32[32,512]{1,0:T(8,128)S(1)}, u32[]{:S(2)}, u32[]{:S(2)}) collective-permute-start(f32[32,512]{1,0:T(8,128)S(1)} %add.10.refs_0_), channel_id=1, source_target_pairs={{0,8},{1,9},{2,10},{3,11},{4,12},{5,13},{6,14},{7,15},{8,0},{9,1},... | collective-permute-start | bytes 196616 | tf_op jit(solution)/shard_map/ppermute | solution.py:375
  75.7 4.3 %collective-permute-start.16 = (f32[32,512]{1,0:T(8,128)S(1)}, f32[32,512]{1,0:T(8,128)S(1)}, u32[]{:S(2)}, u32[]{:S(2)}) collective-permute-start(f32[32,512]{1,0:T(8,128)S(1)} %add.10.refs_0_), channel_id=1, source_target_pairs={{0,16},{1,17},{2,18},{3,19},{4,20},{5,21},{6,22},{7,23},{8,24},{9,... | collective-permute-start | bytes 196616 | tf_op jit(solution)/shard_map/ppermute | solution.py:375
  76.7 5.2 %collective-permute-start.17 = (f32[32,512]{1,0:T(8,128)S(1)}, f32[32,512]{1,0:T(8,128)S(1)}, u32[]{:S(2)}, u32[]{:S(2)}) collective-permute-start(f32[32,512]{1,0:T(8,128)S(1)} %add.10.refs_0_), channel_id=1, source_target_pairs={{0,24},{1,25},{2,26},{3,27},{4,28},{5,29},{6,30},{7,31},{8,16},{9,... | collective-permute-start | bytes 196616 | tf_op jit(solution)/shard_map/ppermute | solution.py:375
  82.1 4.6 %collective-permute-start.18 = (f32[16,128]{1,0:T(8,128)S(1)}, f32[16,128]{1,0:T(8,128)S(1)}, u32[]{:S(2)}, u32[]{:S(2)}) collective-permute-start(f32[16,128]{1,0:T(8,128)S(1)} %get-tuple-element.65), channel_id=1, source_target_pairs={{0,2},{1,3},{2,0},{3,1},{4,6},{5,7},{6,4},{7,5},{8,10},{9,11},{10,... | collective-permute-start | bytes 24584 | tf_op jit(solution)/shard_map/ppermute | solution.py:375
